TPU v7x, 32 devices: a whole 2x2x4 slice. The times are simulated.
32 devices in a mesh: feat: 16 (over z, y, x), tok: 2 (over core).
Axes of the slice: x: 2, y: 2, z: 4, core: 2. Of those that a mesh axis runs over, the one named last changes fastest.
Arguments:
- tokens: bfloat16 [128, 4, 8192], P('feat', None, 'tok'), may hold values from -6 to 6
- gate_weight: bfloat16 [8192, 28672], P('tok', 'feat'), may hold values from -0.0625 to 0.0625
- up_weight: bfloat16 [8192, 28672], P('tok', 'feat'), may hold values from -0.0625 to 0.0625
- down_weight: bfloat16 [28672, 8192], P('feat', 'tok'), may hold values from -0.03125 to 0.03125
- alignment: int32 [3, 128], replicated, may hold values from 0 to 127, each once within a row
Outputs:
- ffn_out: bfloat16 [128, 4, 8192], P('feat', None, 'tok')
- cross: float32 [3, 8192, 8192], P(None, 'feat', 'tok')
Inputs may be any that keep to these rules, and one draw needn't show every extreme that they name: Each row of alignment holds every token index 0 .. 127 exactly once.
All inputs are finite; a program needn't handle non-finite values.
Results may differ from a plain program's by a relative error of at most 0.025.
Values may be sent and summed in bfloat16 or wider, within the bound.
No kernel may reach another device: no remote copies, remote signals or barrier semaphores. Data moves between devices by JAX's collectives and lax.ppermute only.
A program may use at most 192 MiB of HBM per device.

v0:
```python
import math

import jax
import jax.numpy as jnp
from jax import lax
from jax.sharding import PartitionSpec as P


def from_root(value, axis, root):
    mine = lax.axis_index(axis) == root
    return lax.psum(jnp.where(mine, value, jnp.zeros_like(value)), axis)


def on_device(tokens, gate_weight, up_weight, down_weight, alignment):
    languages = tokens.shape[1]
    own_rows = tokens.shape[0]
    gathered = lax.all_gather(tokens, "feat", axis=0, tiled=True)
    tok_width = gathered.shape[2]
    feat_hidden = gate_weight.shape[1]
    all_rows = gathered.shape[0]
    tok_rows = all_rows // lax.axis_size("tok")
    picked = gathered.reshape(tok_rows * lax.axis_size("tok") * languages, tok_width)
    gate_vals = jnp.dot(picked, gate_weight, preferred_element_type=jnp.float32)
    up_vals = jnp.dot(picked, up_weight, preferred_element_type=jnp.float32)
    summed = lax.psum_scatter(
        jnp.stack(
            (
                gate_vals.reshape(tok_rows * lax.axis_size("tok"), languages, feat_hidden),
                up_vals.reshape(tok_rows * lax.axis_size("tok"), languages, feat_hidden),
            ),
            1,
        ).astype(jnp.bfloat16),
        "tok",
        scatter_dimension=0,
        tiled=True,
    ).astype(jnp.float32)
    hidden = (jax.nn.silu(summed[:, 0]) * summed[:, 1]).astype(jnp.bfloat16)
    segment = lax.all_gather(hidden, "tok", axis=0, tiled=True)
    amount = segment.shape[0]
    project_product = jnp.dot(
        segment.reshape(amount * languages, feat_hidden),
        down_weight,
        preferred_element_type=jnp.float32,
    )
    partial_out = project_product.reshape(amount, languages, down_weight.shape[1])
    output_all = lax.psum(partial_out.astype(jnp.bfloat16), "feat")
    ffn_out = lax.dynamic_slice_in_dim(output_all, lax.axis_index("feat") * own_rows, own_rows, 0)
    block_ratio = lax.axis_size("feat") // lax.axis_size("tok")
    feat_index = lax.axis_index("feat")
    feat_width = tok_width // block_ratio
    own_block = lax.dynamic_slice_in_dim(
        output_all[:, 0, :], feat_index % block_ratio * feat_width, feat_width, 1
    )
    english = from_root(own_block, "tok", feat_index // block_ratio)
    scaling = 1.0 / math.sqrt(all_rows)
    blocks = []
    for language in range(1, languages):
        other_rows = jnp.take(output_all[:, language, :], alignment[language - 1], axis=0)
        product = lax.dot_general(
            english, other_rows, (((0,), (0,)), ((), ())), preferred_element_type=jnp.float32
        )
        blocks.append(product * scaling)
    return (ffn_out, jnp.stack(blocks))


def solution(mesh):
    in_specs = (P("feat", None, "tok"), P("tok", "feat"), P("tok", "feat"), P("feat", "tok"), P())
    out_specs = (P("feat", None, "tok"), P(None, "feat", "tok"))
    return jax.shard_map(
        on_device, mesh=mesh, in_specs=in_specs, out_specs=out_specs, check_vma=False
    )
```

profile of v0, /device:TPU:0, one launch (start us, length us, event | category | flops | bytes accessed | tf_op | source)
XLA Modules:
  0.0 367.7 jit_solution(5991590422285122307)
XLA Ops:
  7.2 0.0 all-gather.3.cloned.1.call-start
  7.2 1.8 copy.7
  9.0 0.0 reduce-scatter.2.cloned.1.call-start
  9.1 80.9 %all-gather.3.cloned.1.call-done = bf16[128,4,4096]{2,0,1:T(8,128)(2,1)} async-done(((bf16[8,4,4096]{2,0,1:T(8,128)(2,1)}), bf16[128,4,4096]{2,0,1:T(8,128)(2,1)}) %all-gather.3.cloned.1.call-update) | async-done | bytes 4194320 | tf_op jit(solution)/shard_map/all_gather | solution.py:17
  90.0 15.3 %fusion.15 = bf16[128,1,4,1792]{3,0,2,1:T(8,128)(2,1)S(1)} fusion(bf16[128,4,4096]{2,0,1:T(8,128)(2,1)} %all-gather.3.cloned.1.call-done, bf16[4096,1792]{1,0:T(8,128)(2,1)} %param.9), kind=kOutput, calls=%fused_computation.17 | convolution fusion | flops 7517110272 | bytes 20709376 | tf_op jit(solution)/shard_map/dot_general | solution.py:24
  105.3 12.2 %fusion.18 = bf16[128,1,4,1792]{3,0,2,1:T(8,128)(2,1)S(1)} fusion(bf16[128,4,4096]{2,0,1:T(8,128)(2,1)S(1)} %copy-done.3, bf16[4096,1792]{1,0:T(8,128)(2,1)} %param.8), kind=kOutput, calls=%fused_computation.18 | convolution fusion | flops 7517110272 | bytes 20709376 | tf_op jit(solution)/shard_map/dot_general | solution.py:23
  117.5 2.2 pad_maximum_fusion.1
  119.7 0.0 reduce-scatter.2.cloned.1.call-update
  119.7 0.0 all-gather.5.cloned.1.call-start
  119.7 10.2 %reduce-scatter.2.cloned.1.call-done = bf16[64,2,4,1792]{3,0,2,1:T(8,128)(2,1)} async-done(((bf16[128,2,4,1792]{3,0,2,1:T(8,128)(2,1)}), bf16[64,2,4,1792]{3,0,2,1:T(8,128)(2,1)}) %reduce-scatter.2.cloned.1.call-update) | async-done | bytes 1835024 | tf_op jit(solution)/shard_map/reduce_scatter | solution.py:25
  130.0 1.8 convert_element_type.10
  131.8 1.5 fusion.22
  133.3 0.0 all-gather.5.cloned.1.call-update
  133.3 0.0 all-reduce.3.cloned.1.call-start
  133.3 11.5 %all-gather.5.cloned.1.call-done = bf16[128,4,1792]{2,0,1:T(8,128)(2,1)} async-done(((bf16[64,4,1792]{2,0,1:T(8,128)(2,1)}), bf16[128,4,1792]{2,0,1:T(8,128)(2,1)}) %all-gather.5.cloned.1.call-update) | async-done | bytes 1835024 | tf_op jit(solution)/shard_map/all_gather | solution.py:38
  144.8 12.8 %fusion.6 = bf16[128,4,4096]{2,0,1:T(8,128)(2,1)} fusion(bf16[128,4,1792]{2,0,1:T(8,128)(2,1)} %all-gather.5.cloned.1.call-done, bf16[1792,4096]{1,0:T(8,128)(2,1)} %param.10), kind=kOutput, calls=%fused_computation.13 | convolution fusion | flops 7518289920 | bytes 20709376 | tf_op jit(solution)/shard_map/dot_general | solution.py:40
  157.6 0.0 all-reduce.3.cloned.1.call-update
  157.7 0.2 all-reduce.5.cloned.1.call-start
  157.9 0.4 copy-done.2
  158.4 168.8 %all-reduce.3.cloned.1.call-done = bf16[128,4,4096]{2,0,1:T(8,128)(2,1)} async-done(((bf16[128,4,4096]{2,0,1:T(8,128)(2,1)}), bf16[128,4,4096]{2,0,1:T(8,128)(2,1)}) %all-reduce.3.cloned.1.call-update) | async-done | bytes 4194320 | tf_op jit(solution)/shard_map/psum | solution.py:46
  327.1 2.5 slice_bitcast_fusion.4
  329.7 0.7 select_bitcast_fusion
  330.4 1.0 constant_dynamic-slice_fusion
  331.4 0.9 copy.8
  332.3 2.2 gather_fusion
  334.4 1.2 gather_fusion.2
  335.6 1.2 gather_fusion.1
  336.8 10.6 %all-reduce.5.cloned.1.call-done = bf16[128,512]{1,0:T(8,128)(2,1)} async-done(((bf16[128,512]{1,0:T(8,128)(2,1)}), bf16[128,512]{1,0:T(8,128)(2,1)}) %all-reduce.5.cloned.1.call-update) | async-done | bytes 131088 | tf_op jit(solution)/shard_map/psum | solution.py:11
  347.4 2.3 multiply_bitcast_fusion.1
  349.7 1.3 multiply_bitcast_fusion
  351.1 1.3 multiply_bitcast_fusion.2
  352.4 8.8 %pad_maximum_fusion = f32[3,512,4096]{2,1,0:T(8,128)} fusion(f32[1,512,4096]{2,1,0:T(8,128)S(1)} %multiply_bitcast_fusion, f32[1,512,4096]{2,1,0:T(8,128)S(1)} %multiply_bitcast_fusion.1, f32[1,512,4096]{2,1,0:T(8,128)S(1)} %multiply_bitcast_fusion.2), kind=kLoop, calls=%fused_computation.3 | loop fusion | flops 12582912 | bytes 50331648 | tf_op jit(solution)/shard_map/stack | solution.py:63
  (12 shorter events, 0.1 us)
Async XLA Ops:
  7.2 82.9 %all-gather.3.cloned.1.call-start = ((), (), s32[]{:S(2)}) async-start(), calls=%async_computation.1 | async-start | bytes 4456448 | tf_op jit(solution)/shard_map/all_gather | solution.py:17
  9.0 120.9 %reduce-scatter.2.cloned.1.call-start = ((), (), s32[]{:S(2)}) async-start(), calls=%async_computation.2 | async-start | bytes 5505024 | tf_op jit(solution)/shard_map/reduce_scatter | solution.py:25
  90.0 15.3 %copy-start.3 = (bf16[128,4,4096]{2,0,1:T(8,128)(2,1)S(1)}, bf16[128,4,4096]{2,0,1:T(8,128)(2,1)}, u32[]{:S(2)}) copy-start(bf16[128,4,4096]{2,0,1:T(8,128)(2,1)} %all-gather.3.cloned.1.call-done) | copy-start | bytes 12582916
  119.7 25.1 %all-gather.5.cloned.1.call-start = ((), (), s32[]{:S(2)}) async-start(), calls=%async_computation.3 | async-start | bytes 2752512 | tf_op jit(solution)/shard_map/all_gather | solution.py:38
  133.3 193.8 %all-reduce.3.cloned.1.call-start = ((), (), s32[]{:S(2)}) async-start(), calls=%async_computation.4 | async-start | bytes 8388608 | tf_op jit(solution)/shard_map/psum | solution.py:46
  157.6 0.7 copy-start.2
  157.7 189.8 %all-reduce.5.cloned.1.call-start = ((), (), s32[]{:S(2)}) async-start(), calls=%async_computation.5 | async-start | bytes 262144 | tf_op jit(solution)/shard_map/psum | solution.py:11
  347.4 2.3 copy-start.1
  349.7 1.3 copy-start
Sparse Core Ops, SparseCore 0:
  11.3 78.6 all-gather.2
  119.8 10.1 reduce-scatter.1
  133.4 11.3 all-gather.4
  157.8 169.3 all-reduce.2
  330.5 16.8 all-reduce.4
where the time goes:
time: 368 us
  waiting for transfers between devices  282 us (77%)
  matrix products  45.2 us (12%)
  other arithmetic  14.9 us (4%)
  between operations  13.9 us (4%)
  local copies, waits for them, and re-layouts  11.2 us (3%)
    psum x1, waiting for transfers between devices, on_device(): output_all = lax.psum(partial_out.astype(jnp.bfloat16), 'feat')  169 us
    all_gather x1, waiting for transfers between devices, on_device(): gathered = lax.all_gather(tokens, 'feat', axis=0, tiled=True)  80.9 us
    dot_general x1, matrix products, on_device(): up_vals = jnp.dot(picked, up_weight, preferred_element_type=jnp.float32)  15.3 us
    dot_general x1, matrix products, on_device(): jnp.dot(segment.reshape(amount * languages, feat_hidden), down_weight, pr...  12.8 us
    dot_general x1, matrix products, on_device(): gate_vals = jnp.dot(picked, gate_weight, preferred_element_type=jnp.float32)  12.2 us
    all_gather x1, waiting for transfers between devices, on_device(): segment = lax.all_gather(hidden, 'tok', axis=0, tiled=True)  11.5 us
    psum x1, waiting for transfers between devices, from_root(): return lax.psum(jnp.where(mine, value, jnp.zeros_like(value)), axis)  10.6 us
    reduce_scatter x1, waiting for transfers between devices, on_device(): lax.psum_scatter(jnp.stack((gate_vals.reshape(tok_rows * lax.axis_size('t...  10.2 us
  transfers between devices with their start and end apart: 5, of which 5 were waited for; matrix products, arithmetic and copies ran while one was open for 2% of the time, Pallas kernels for 0%

commit v1 on v0

v1 whole, which is shorter than its diff:
```python
import math

import jax
import jax.numpy as jnp
import numpy as np
from jax import lax
from jax.sharding import PartitionSpec as P

BF16 = jnp.bfloat16
F32 = jnp.float32


def feat_shape(n):
    if n == 16:
        return 4, 2, 2
    if n == 32:
        return 2, 4, 4
    return 1, 1, n


def folded(n):
    return list(range(0, n, 2)) + list(range(1, n, 2))[::-1]


def plane_cycle(ny, nx):
    if ny < 2 or nx < 2:
        return folded(ny * nx)
    cycle = [(0, x) for x in range(nx)]
    for y in range(1, ny):
        xs = range(1, nx) if y % 2 == 0 else range(nx - 1, 0, -1)
        cycle += [(y, x) for x in xs]
    cycle += [(y, 0) for y in range(ny - 1, 0, -1)]
    return [y * nx + x for y, x in cycle]


class Rings:
    def __init__(self, n_feat, n_tok):
        nz, ny, nx = feat_shape(n_feat)
        self.n_feat, self.n_tok = n_feat, n_tok
        self.nz, self.npl = nz, ny * nx
        self.zorder = folded(nz)
        self.porder = plane_cycle(ny, nx)
        self.zpos = {z: i for i, z in enumerate(self.zorder)}
        self.ppos = {p: i for i, p in enumerate(self.porder)}

    def source(self, f, t, j, i):
        sign = 1 if t % 2 == 0 else -1
        z, p = divmod(f, self.npl)
        z2 = self.zorder[(self.zpos[z] - i) % self.nz]
        p2 = self.porder[(self.ppos[p] - sign * j) % self.npl]
        return z2 * self.npl + p2

    def perm(self, which, back):
        pairs = []
        for f in range(self.n_feat):
            for t in range(self.n_tok):
                j, i = (1, 0) if which == "p" else (0, 1)
                s = self.source(f, t, j, i)
                pair = (s * self.n_tok + t, f * self.n_tok + t)
                pairs.append(pair[::-1] if back else pair)
        return sorted(pairs)

    def size(self, which):
        return self.npl if which == "p" else self.nz

    def gather(self, x, which):
        perm = self.perm(which, False)
        out = [x]
        for _ in range(self.size(which) - 1):
            out.append(lax.ppermute(out[-1], ("feat", "tok"), perm))
        return out

    def scatter(self, parts, which):
        perm = self.perm(which, True)
        acc = parts[-1]
        for part in parts[-2::-1]:
            got = lax.ppermute(acc, ("feat", "tok"), perm)
            acc = (got.astype(F32) + part.astype(F32)).astype(BF16)
        return acc


def mirror(n):
    return [(n - j) % n for j in range(n)]


def on_device(tokens, gate_weight, up_weight, down_weight, alignment):
    n_feat, n_tok = lax.axis_size("feat"), lax.axis_size("tok")
    rings = Rings(n_feat, n_tok)
    nz, npl = rings.nz, rings.npl
    own, langs, width = tokens.shape
    rows = own * langs
    hid = gate_weight.shape[1]
    f, t = lax.axis_index("feat"), lax.axis_index("tok")
    cut = max(width * 21 // 32 // 128 * 128, 128)

    x = tokens.transpose(1, 0, 2).reshape(rows, width)

    a = jnp.concatenate(rings.gather(x[:, :cut], "z"), 0)
    a = jnp.concatenate(rings.gather(a, "p"), 0)
    b = jnp.concatenate(rings.gather(x[:, cut:], "p"), 0)
    b = jnp.concatenate(rings.gather(b, "z"), 0)
    b = b.reshape(nz, npl, rows, width - cut).transpose(1, 0, 2, 3).reshape(-1, width - cut)
    full = jnp.concatenate((a, b), 1)

    gate = jnp.dot(full, gate_weight, preferred_element_type=F32).astype(BF16)
    up = jnp.dot(full, up_weight, preferred_element_type=F32).astype(BF16)

    def over_tok(v):
        v = v.reshape(npl, nz * rows, hid)
        flip = [v[j] for j in mirror(npl)]
        if n_tok == 2:
            other = lax.ppermute(v, "tok", [(0, 1), (1, 0)])
            other = jnp.stack([other[j] for j in mirror(npl)])
            return v.astype(F32) + other.astype(F32)
        odd = t % 2 == 1
        v = jnp.where(odd, jnp.stack(flip), v)
        total = lax.psum(v, "tok").astype(F32)
        return jnp.where(odd, jnp.stack([total[j] for j in mirror(npl)]), total)

    hidden = (jax.nn.silu(over_tok(gate)) * over_tok(up)).astype(BF16)
    hidden = hidden.reshape(-1, hid)

    oa = jnp.dot(hidden, down_weight[:, :cut], preferred_element_type=F32).astype(BF16)
    ob = jnp.dot(hidden, down_weight[:, cut:], preferred_element_type=F32).astype(BF16)

    oa = oa.reshape(npl, nz * rows, cut)
    oa = rings.scatter([oa[j] for j in range(npl)], "p").reshape(nz, rows, cut)
    oa = rings.scatter([oa[i] for i in range(nz)], "z")
    ob = ob.reshape(npl, nz, rows, width - cut)
    ob = rings.scatter([ob[:, i].reshape(npl * rows, -1) for i in range(nz)], "z")
    ob = ob.reshape(npl, rows, width - cut)
    ob = rings.scatter([ob[j] for j in range(npl)], "p")

    ffn_out = jnp.concatenate((oa, ob), 1).reshape(langs, own, width).transpose(1, 0, 2)

    a = jnp.stack(rings.gather(oa.reshape(langs, own, cut), "z"), 1)
    a = a.reshape(langs, nz * own, cut)
    a = jnp.stack(rings.gather(a, "p"), 1).reshape(langs, -1, cut)
    b = jnp.stack(rings.gather(ob.reshape(langs, own, width - cut), "p"), 1)
    b = b.reshape(langs, npl * own, width - cut)
    b = jnp.stack(rings.gather(b, "z"), 1)
    b = b.reshape(langs, nz, npl, own, width - cut).transpose(0, 2, 1, 3, 4)
    b = b.reshape(langs, -1, width - cut)
    out_all = jnp.concatenate((a, b), 2)

    ids = np.zeros((n_feat, n_tok, npl, nz, own), np.int32)
    for ff in range(n_feat):
        for tt in range(n_tok):
            for j in range(npl):
                for i in range(nz):
                    ids[ff, tt, j, i] = rings.source(ff, tt, j, i) * own + np.arange(own)
    ids = jnp.asarray(ids.reshape(n_feat * n_tok, -1))
    mine = lax.dynamic_index_in_dim(ids, f * n_tok + t, 0, keepdims=False)

    ratio = n_feat // n_tok
    fw = width // ratio
    own_block = lax.dynamic_slice_in_dim(out_all[0], f % ratio * fw, fw, 1)
    root = f // ratio
    if n_tok == 2:
        other = lax.ppermute(own_block, "tok", [(0, 1), (1, 0)])
        other = other.reshape(npl, nz * own, fw)
        other = jnp.stack([other[j] for j in mirror(npl)]).reshape(-1, fw)
        english = jnp.where(root == t, own_block, other)
    else:
        def flip(v):
            v = v.reshape(npl, nz * own, fw)
            return jnp.stack([v[j] for j in mirror(npl)]).reshape(-1, fw)

        odd = t % 2 == 1
        block = jnp.where(odd, flip(own_block), own_block)
        block = lax.psum(jnp.where(root == t, block, jnp.zeros_like(block)), "tok")
        english = jnp.where(odd, flip(block), block)

    targets = jnp.take(alignment, mine, axis=1)
    onehot = (mine[None, :, None] == targets[:, None, :]).astype(BF16)
    moved = jnp.einsum("lri,ic->lrc", onehot, english, preferred_element_type=F32).astype(BF16)
    scaling = 1.0 / math.sqrt(own * n_feat)
    cross = jnp.einsum("lrc,lrd->lcd", moved, out_all[1:], preferred_element_type=F32) * scaling
    return ffn_out, cross


def solution(mesh):
    in_specs = (P("feat", None, "tok"), P("tok", "feat"), P("tok", "feat"), P("feat", "tok"), P())
    out_specs = (P("feat", None, "tok"), P(None, "feat", "tok"))
    return jax.shard_map(
        on_device, mesh=mesh, in_specs=in_specs, out_specs=out_specs, check_vma=False
    )
```

time: 368 us -> 253 us (0.69)
  waiting for transfers between devices: 282 us -> 133 us
  starting transfers between devices: 0.39 us -> 57.7 us
  between operations: 13.9 us -> 1.1 us
  other arithmetic: 14.9 us -> 7.93 us
  local copies, waits for them, and re-layouts: 11.2 us -> 5.01 us
    psum x2 -> x0, waiting for transfers between devices: 179 us -> none  [the longest x1 169 us: on_device(): output_all = lax.psum(partial_out.astype(jnp.bfloat16), 'feat')]
    ppermute x0 -> x39, waiting for transfers between devices: none -> 133 us  [the longest x12 66.9 us: scatter(): got = lax.ppermute(acc, ('feat', 'tok'), perm)]
    all_gather x2 -> x0, waiting for transfers between devices: 92.4 us -> none  [the longest x1 80.9 us: on_device(): gathered = lax.all_gather(tokens, 'feat', axis=0, tiled=True)]
    ppermute x0 -> x39, starting transfers between devices: none -> 57.7 us  [the longest x24 41.5 us: gather(): out.append(lax.ppermute(out[-1], ('feat', 'tok'), perm))]
    reduce_scatter x1 -> x0, waiting for transfers between devices: 10.2 us -> none  [on_device(): lax.psum_scatter(jnp.stack((gate_vals.reshape(tok_rows * lax.axis_size('t...]
    another operation x2 -> x5, other arithmetic: 10.9 us -> 2.14 us  [the longest x2 1.54 us: on_device(): a = jnp.stack(rings.gather(a, 'p'), 1).reshape(langs, -1, cut)]
    gather x3 -> x1, local copies, waits for them, and re-layouts: 4.54 us -> 0.64 us  [on_device(): targets = jnp.take(alignment, mine, axis=1)]
    dot_general x6 -> x5, matrix products: 45.2 us -> 47.2 us  [the longest x1 12.2 us: on_device(): up = jnp.dot(full, up_weight, preferred_element_type=F32).astype(BF16)]
  transfers between devices with their start and end apart: 5 -> 39, of which waited for: 5 -> 30; matrix products, arithmetic and copies ran while one was open for 2% -> 8% of each run, Pallas kernels for 0% -> 0%
where the time goes in v1:
time: 253 us; the launch traced here: 252 us
  waiting for transfers between devices  133 us (53%)
  starting transfers between devices  57.7 us (23%)
  matrix products  47.2 us (19%)
  other arithmetic  7.93 us (3%)
  local copies, waits for them, and re-layouts  5.01 us (2%)
    ppermute x12, waiting for transfers between devices, scatter(): got = lax.ppermute(acc, ('feat', 'tok'), perm)  66.9 us
    ppermute x24, waiting for transfers between devices, gather(): out.append(lax.ppermute(out[-1], ('feat', 'tok'), perm))  62.8 us
    ppermute x24, starting transfers between devices, gather(): out.append(lax.ppermute(out[-1], ('feat', 'tok'), perm))  41.5 us
    ppermute x12, starting transfers between devices, scatter(): got = lax.ppermute(acc, ('feat', 'tok'), perm)  15.5 us
    dot_general x1, matrix products, on_device(): up = jnp.dot(full, up_weight, preferred_element_type=F32).astype(BF16)  12.2 us
    dot_general x1, matrix products, on_device(): jnp.einsum('lrc,lrd->lcd', moved, out_all[1:], preferred_element_type=F32)  12.2 us
    dot_general x1, matrix products, on_device(): jnp.dot(hidden, down_weight[:, :cut], preferred_element_type=F32)  9.64 us
    dot_general x1, matrix products, on_device(): gate = jnp.dot(full, gate_weight, preferred_element_type=F32).astype(BF16)  7.72 us
  transfers between devices with their start and end apart: 39, of which 30 were waited for; matrix products, arithmetic and copies ran while one was open for 8% of the time, Pallas kernels for 0%

profile of v1, /device:TPU:0, one launch (start us, length us, event | category | flops | bytes accessed | tf_op | source)
XLA Modules:
  0.0 252.4 jit_solution(10761424847366642508)
XLA Ops:
  1.8 3.0 %collective-permute-start.6 = (bf16[32,1408]{1,0:T(8,128)(2,1)S(1)}, bf16[32,1408]{1,0:T(8,128)(2,1)S(1)}, u32[]{:S(2)}, u32[]{:S(2)}) collective-permute-start(bf16[32,1408]{1,0:T(8,128)(2,1)S(1)} %get-tuple-element.20), channel_id=1, source_target_pairs={{0,2},{1,5},{2,6},{3,1},{4,0},{5,7},{6,4},{7,3},{8,10},{9,13},{10,... | collective-permute-start | bytes 270344 | tf_op jit(solution)/shard_map/ppermute | solution.py:70
  10.8 3.4 %collective-permute-start.1 = (bf16[32,2688]{1,0:T(8,128)(2,1)S(1)}, bf16[32,2688]{1,0:T(8,128)(2,1)S(1)}, u32[]{:S(2)}, u32[]{:S(2)}) collective-permute-start(bf16[32,2688]{1,0:T(8,128)(2,1)S(1)} %collective-permute-done), channel_id=1, source_target_pairs={{0,16},{1,17},{2,18},{3,19},{4,20},{5,21},{6,22},{7,23},{8,0},{9,1... | collective-permute-start | bytes 516104 | tf_op jit(solution)/shard_map/ppermute | solution.py:70
  17.1 3.4 %collective-permute-start.2 = (bf16[32,2688]{1,0:T(8,128)(2,1)S(1)}, bf16[32,2688]{1,0:T(8,128)(2,1)S(1)}, u32[]{:S(2)}, u32[]{:S(2)}) collective-permute-start(bf16[32,2688]{1,0:T(8,128)(2,1)S(1)} %collective-permute-done.1), channel_id=1, source_target_pairs={{0,16},{1,17},{2,18},{3,19},{4,20},{5,21},{6,22},{7,23},{8,0},{9,1... | collective-permute-start | bytes 516104 | tf_op jit(solution)/shard_map/ppermute | solution.py:70
  20.5 2.9 %collective-permute-done.2 = bf16[32,2688]{1,0:T(8,128)(2,1)S(1)} collective-permute-done((bf16[32,2688]{1,0:T(8,128)(2,1)S(1)}, bf16[32,2688]{1,0:T(8,128)(2,1)S(1)}, u32[]{:S(2)}, u32[]{:S(2)}) %collective-permute-start.2) | collective-permute-done | bytes 172064 | tf_op jit(solution)/shard_map/ppermute | solution.py:70
  24.8 3.4 %collective-permute-start.9 = (bf16[128,1408]{1,0:T(8,128)(2,1)S(1)}, bf16[128,1408]{1,0:T(8,128)(2,1)S(1)}, u32[]{:S(2)}, u32[]{:S(2)}) collective-permute-start(bf16[128,1408]{1,0:T(8,128)(2,1)S(1)} %pad_maximum_fusion.10), channel_id=1, source_target_pairs={{0,16},{1,17},{2,18},{3,19},{4,20},{5,21},{6,22},{7,23},{8,0},{9,1... | collective-permute-start | bytes 1081352 | tf_op jit(solution)/shard_map/ppermute | solution.py:70
  28.3 6.1 %collective-permute-done.9 = bf16[128,1408]{1,0:T(8,128)(2,1)S(1)} collective-permute-done((bf16[128,1408]{1,0:T(8,128)(2,1)S(1)}, bf16[128,1408]{1,0:T(8,128)(2,1)S(1)}, u32[]{:S(2)}, u32[]{:S(2)}) %collective-permute-start.9) | collective-permute-done | bytes 360480 | tf_op jit(solution)/shard_map/ppermute | solution.py:70
  34.4 3.4 %collective-permute-start.10 = (bf16[128,1408]{1,0:T(8,128)(2,1)S(1)}, bf16[128,1408]{1,0:T(8,128)(2,1)S(1)}, u32[]{:S(2)}, u32[]{:S(2)}) collective-permute-start(bf16[128,1408]{1,0:T(8,128)(2,1)S(1)} %collective-permute-done.9), channel_id=1, source_target_pairs={{0,16},{1,17},{2,18},{3,19},{4,20},{5,21},{6,22},{7,23},{8,0},{9,1... | collective-permute-start | bytes 1081352 | tf_op jit(solution)/shard_map/ppermute | solution.py:70
  38.8 4.2 %collective-permute-done.10 = bf16[128,1408]{1,0:T(8,128)(2,1)S(1)} collective-permute-done((bf16[128,1408]{1,0:T(8,128)(2,1)S(1)}, bf16[128,1408]{1,0:T(8,128)(2,1)S(1)}, u32[]{:S(2)}, u32[]{:S(2)}) %collective-permute-start.10) | collective-permute-done | bytes 360480 | tf_op jit(solution)/shard_map/ppermute | solution.py:70
  43.0 3.4 %collective-permute-start.11 = (bf16[128,1408]{1,0:T(8,128)(2,1)S(1)}, bf16[128,1408]{1,0:T(8,128)(2,1)S(1)}, u32[]{:S(2)}, u32[]{:S(2)}) collective-permute-start(bf16[128,1408]{1,0:T(8,128)(2,1)S(1)} %collective-permute-done.10), channel_id=1, source_target_pairs={{0,16},{1,17},{2,18},{3,19},{4,20},{5,21},{6,22},{7,23},{8,0},{9,1... | collective-permute-start | bytes 1081352 | tf_op jit(solution)/shard_map/ppermute | solution.py:70
  51.8 9.0 %collective-permute-done.5 = bf16[128,2688]{1,0:T(8,128)(2,1)S(1)} collective-permute-done((bf16[128,2688]{1,0:T(8,128)(2,1)S(1)}, bf16[128,2688]{1,0:T(8,128)(2,1)S(1)}, u32[]{:S(2)}, u32[]{:S(2)}) %collective-permute-start.5) | collective-permute-done | bytes 688160 | tf_op jit(solution)/shard_map/ppermute | solution.py:70
  61.0 12.2 %convolution_convert_fusion = bf16[512,1792]{1,0:T(8,128)(2,1)S(1)} fusion(bf16[4096,1792]{1,0:T(8,128)(2,1)} %param.8, bf16[512,1408]{1,0:T(8,128)(2,1)S(1)} %bitcast.121, bf16[512,2688]{1,0:T(8,128)(2,1)S(1)} %constant_dynamic-update-slice_fusion), kind=kOutput, calls=%fused_computation.14 | convolution fusion | flops 7525498880 | bytes 20709376 | tf_op jit(solution)/shard_map/dot_general | solution.py:106
  73.4 7.7 %convolution_convert_fusion.1 = bf16[512,1792]{1,0:T(8,128)(2,1)S(1)} fusion(bf16[4096,1792]{1,0:T(8,128)(2,1)S(1)} %bitcast.139, bf16[512,1408]{1,0:T(8,128)(2,1)S(1)} %bitcast.122, bf16[512,2688]{1,0:T(8,128)(2,1)S(1)} %constant_dynamic-update-slice_fusion), kind=kOutput, calls=%fused_computation.15 | convolution fusion | flops 7525498880 | bytes 20709376 | tf_op jit(solution)/shard_map/dot_general | solution.py:105
  81.7 3.3 %collective-permute-done.12 = bf16[4,128,1792]{2,1,0:T(8,128)(2,1)S(1)} collective-permute-done((bf16[4,128,1792]{2,1,0:T(8,128)(2,1)S(1)}, bf16[4,128,1792]{2,1,0:T(8,128)(2,1)S(1)}, u32[]{:S(2)}, u32[]{:S(2)}) %collective-permute-start.12) | collective-permute-done | bytes 1835040 | tf_op jit(solution)/shard_map/ppermute | solution.py:112
  87.4 9.6 %fusion.4 = bf16[512,2688]{1,0:T(8,128)(2,1)S(1)} fusion(bf16[512,1792]{1,0:T(8,128)(2,1)S(1)} %fusion.8, bf16[1792,4096]{1,0:T(8,128)(2,1)} %param.9), kind=kOutput, calls=%fused_computation.6 | convolution fusion | flops 4933877760 | bytes 14221312 | tf_op jit(solution)/shard_map/dot_general | solution.py:123
  99.7 8.5 %collective-permute-done.14 = bf16[128,2688]{1,0:T(8,128)(2,1)S(1)} collective-permute-done((bf16[128,2688]{1,0:T(8,128)(2,1)S(1)}, bf16[128,2688]{1,0:T(8,128)(2,1)S(1)}, u32[]{:S(2)}, u32[]{:S(2)}) %collective-permute-start.14) | collective-permute-done | bytes 688160 | tf_op jit(solution)/shard_map/ppermute | solution.py:77
  110.8 8.9 %collective-permute-done.15 = bf16[128,2688]{1,0:T(8,128)(2,1)S(1)} collective-permute-done((bf16[128,2688]{1,0:T(8,128)(2,1)S(1)}, bf16[128,2688]{1,0:T(8,128)(2,1)S(1)}, u32[]{:S(2)}, u32[]{:S(2)}) %collective-permute-start.15) | collective-permute-done | bytes 688160 | tf_op jit(solution)/shard_map/ppermute | solution.py:77
  122.0 5.4 %fusion.10 = bf16[512,1408]{1,0:T(8,128)(2,1)S(1)} fusion(bf16[512,1792]{1,0:T(8,128)(2,1)S(1)} %fusion.8, bf16[1792,4096]{1,0:T(8,128)(2,1)} %param.9), kind=kOutput, calls=%fused_computation.16 | convolution fusion | flops 2584412160 | bytes 8323072 | tf_op jit(solution)/shard_map/dot_general | solution.py:124
  127.4 3.5 %collective-permute-done.16 = bf16[128,2688]{1,0:T(8,128)(2,1)S(1)} collective-permute-done((bf16[128,2688]{1,0:T(8,128)(2,1)S(1)}, bf16[128,2688]{1,0:T(8,128)(2,1)S(1)}, u32[]{:S(2)}, u32[]{:S(2)}) %collective-permute-start.16) | collective-permute-done | bytes 688160 | tf_op jit(solution)/shard_map/ppermute | solution.py:77
  133.3 6.1 %collective-permute-done.17 = bf16[32,2688]{1,0:T(8,128)(2,1)S(1)} collective-permute-done((bf16[32,2688]{1,0:T(8,128)(2,1)S(1)}, bf16[32,2688]{1,0:T(8,128)(2,1)S(1)}, u32[]{:S(2)}, u32[]{:S(2)}) %collective-permute-start.17) | collective-permute-done | bytes 172064 | tf_op jit(solution)/shard_map/ppermute | solution.py:77
  139.5 7.5 %collective-permute-done.20 = bf16[128,1408]{1,0:T(8,128)(2,1)S(1)} collective-permute-done((bf16[128,1408]{1,0:T(8,128)(2,1)S(1)}, bf16[128,1408]{1,0:T(8,128)(2,1)S(1)}, u32[]{:S(2)}, u32[]{:S(2)}) %collective-permute-start.20) | collective-permute-done | bytes 360480 | tf_op jit(solution)/shard_map/ppermute | solution.py:77
  147.1 3.5 %collective-permute-done.18 = bf16[32,2688]{1,0:T(8,128)(2,1)S(1)} collective-permute-done((bf16[32,2688]{1,0:T(8,128)(2,1)S(1)}, bf16[32,2688]{1,0:T(8,128)(2,1)S(1)}, u32[]{:S(2)}, u32[]{:S(2)}) %collective-permute-start.18) | collective-permute-done | bytes 172064 | tf_op jit(solution)/shard_map/ppermute | solution.py:77
  150.7 8.5 %collective-permute-done.21 = bf16[128,1408]{1,0:T(8,128)(2,1)S(1)} collective-permute-done((bf16[128,1408]{1,0:T(8,128)(2,1)S(1)}, bf16[128,1408]{1,0:T(8,128)(2,1)S(1)}, u32[]{:S(2)}, u32[]{:S(2)}) %collective-permute-start.21) | collective-permute-done | bytes 360480 | tf_op jit(solution)/shard_map/ppermute | solution.py:77
  159.4 3.6 %collective-permute-done.19 = bf16[32,2688]{1,0:T(8,128)(2,1)S(1)} collective-permute-done((bf16[32,2688]{1,0:T(8,128)(2,1)S(1)}, bf16[32,2688]{1,0:T(8,128)(2,1)S(1)}, u32[]{:S(2)}, u32[]{:S(2)}) %collective-permute-start.19) | collective-permute-done | bytes 172064 | tf_op jit(solution)/shard_map/ppermute | solution.py:77
  163.1 9.7 %collective-permute-done.22 = bf16[128,1408]{1,0:T(8,128)(2,1)S(1)} collective-permute-done((bf16[128,1408]{1,0:T(8,128)(2,1)S(1)}, bf16[128,1408]{1,0:T(8,128)(2,1)S(1)}, u32[]{:S(2)}, u32[]{:S(2)}) %collective-permute-start.22) | collective-permute-done | bytes 360480 | tf_op jit(solution)/shard_map/ppermute | solution.py:77
  186.1 2.8 %collective-permute-done.25 = bf16[32,1408]{1,0:T(8,128)(2,1)S(1)} collective-permute-done((bf16[32,1408]{1,0:T(8,128)(2,1)S(1)}, bf16[32,1408]{1,0:T(8,128)(2,1)S(1)}, u32[]{:S(2)}, u32[]{:S(2)}) %collective-permute-start.25) | collective-permute-done | bytes 90144 | tf_op jit(solution)/shard_map/ppermute | solution.py:77
  190.6 7.3 %collective-permute-done.32 = bf16[4,8,1408]{2,1,0:T(8,128)(2,1)S(1)} collective-permute-done((bf16[4,8,1408]{2,1,0:T(8,128)(2,1)S(1)}, bf16[4,8,1408]{2,1,0:T(8,128)(2,1)S(1)}, u32[]{:S(2)}, u32[]{:S(2)}) %collective-permute-start.32) | collective-permute-done | bytes 90144 | tf_op jit(solution)/shard_map/ppermute | solution.py:70
  198.0 4.5 %collective-permute-done.33 = bf16[4,8,1408]{2,1,0:T(8,128)(2,1)S(1)} collective-permute-done((bf16[4,8,1408]{2,1,0:T(8,128)(2,1)S(1)}, bf16[4,8,1408]{2,1,0:T(8,128)(2,1)S(1)}, u32[]{:S(2)}, u32[]{:S(2)}) %collective-permute-start.33) | collective-permute-done | bytes 90144 | tf_op jit(solution)/shard_map/ppermute | solution.py:70
  202.5 4.5 %collective-permute-done.34 = bf16[4,8,1408]{2,1,0:T(8,128)(2,1)S(1)} collective-permute-done((bf16[4,8,1408]{2,1,0:T(8,128)(2,1)S(1)}, bf16[4,8,1408]{2,1,0:T(8,128)(2,1)S(1)}, u32[]{:S(2)}, u32[]{:S(2)}) %collective-permute-start.34) | collective-permute-done | bytes 90144 | tf_op jit(solution)/shard_map/ppermute | solution.py:70
  208.9 6.0 %collective-permute-done.35 = bf16[4,32,1408]{2,1,0:T(8,128)(2,1)S(1)} collective-permute-done((bf16[4,32,1408]{2,1,0:T(8,128)(2,1)S(1)}, bf16[4,32,1408]{2,1,0:T(8,128)(2,1)S(1)}, u32[]{:S(2)}, u32[]{:S(2)}) %collective-permute-start.35) | collective-permute-done | bytes 360480 | tf_op jit(solution)/shard_map/ppermute | solution.py:70
  218.1 6.1 %collective-permute-done.36 = bf16[4,32,1408]{2,1,0:T(8,128)(2,1)} collective-permute-done((bf16[4,32,1408]{2,1,0:T(8,128)(2,1)S(1)}, bf16[4,32,1408]{2,1,0:T(8,128)(2,1)}, u32[]{:S(2)}, u32[]{:S(2)}) %collective-permute-start.36) | collective-permute-done | bytes 360480 | tf_op jit(solution)/shard_map/ppermute | solution.py:70
  234.0 2.9 %collective-permute-done.31 = bf16[4,32,2688]{2,1,0:T(8,128)(2,1)} collective-permute-done((bf16[4,32,2688]{2,1,0:T(8,128)(2,1)S(1)}, bf16[4,32,2688]{2,1,0:T(8,128)(2,1)}, u32[]{:S(2)}, u32[]{:S(2)}) %collective-permute-start.31) | collective-permute-done | bytes 688160 | tf_op jit(solution)/shard_map/ppermute | solution.py:70
  240.2 12.2 %broadcast_multiply_fusion = f32[3,512,4096]{2,1,0:T(8,128)} fusion(bf16[4,128,1408]{2,1,0:T(8,128)(2,1)} %bitcast.114, bf16[4,128,2688]{2,1,0:T(8,128)(2,1)S(1)} %bitcast.112, bf16[128,512]{1,0:T(8,128)(2,1)S(1)} %bitcast_select_fusion, s32[3,128]{1,0:T(4,128)S(1)} %copy.27, s32[128]{0:T(128)S(1)} %fusion.31), kind=kOutput, calls=%fused_computation.1 | convolution fusion | flops 1673773056 | bytes 29493248 | tf_op jit(solution)/shard_map/lrc,lrd->lcd/dot_general | solution.py:178
  (122 shorter events, 64.8 us)
Async XLA Ops:
  1.8 5.7 %collective-permute-start.6 = (bf16[32,1408]{1,0:T(8,128)(2,1)S(1)}, bf16[32,1408]{1,0:T(8,128)(2,1)S(1)}, u32[]{:S(2)}, u32[]{:S(2)}) collective-permute-start(bf16[32,1408]{1,0:T(8,128)(2,1)S(1)} %get-tuple-element.20), channel_id=1, source_target_pairs={{0,2},{1,5},{2,6},{3,1},{4,0},{5,7},{6,4},{7,3},{8,10},{9,13},{10,... | collective-permute-start | bytes 270344 | tf_op jit(solution)/shard_map/ppermute | solution.py:70
  4.8 6.0 %collective-permute-start = (bf16[32,2688]{1,0:T(8,128)(2,1)S(1)}, bf16[32,2688]{1,0:T(8,128)(2,1)S(1)}, u32[]{:S(2)}, u32[]{:S(2)}) collective-permute-start(bf16[32,2688]{1,0:T(8,128)(2,1)S(1)} %get-tuple-element.18), channel_id=1, source_target_pairs={{0,16},{1,17},{2,18},{3,19},{4,20},{5,21},{6,22},{7,23},{8,0},{9,1... | collective-permute-start | bytes 516104 | tf_op jit(solution)/shard_map/ppermute | solution.py:70
  7.4 6.8 %collective-permute-start.7 = (bf16[32,1408]{1,0:T(8,128)(2,1)S(1)}, bf16[32,1408]{1,0:T(8,128)(2,1)S(1)}, u32[]{:S(2)}, u32[]{:S(2)}) collective-permute-start(bf16[32,1408]{1,0:T(8,128)(2,1)S(1)} %collective-permute-done.6), channel_id=1, source_target_pairs={{0,2},{1,5},{2,6},{3,1},{4,0},{5,7},{6,4},{7,3},{8,10},{9,13},{10,... | collective-permute-start | bytes 270344 | tf_op jit(solution)/shard_map/ppermute | solution.py:70
  10.8 6.3 %collective-permute-start.1 = (bf16[32,2688]{1,0:T(8,128)(2,1)S(1)}, bf16[32,2688]{1,0:T(8,128)(2,1)S(1)}, u32[]{:S(2)}, u32[]{:S(2)}) collective-permute-start(bf16[32,2688]{1,0:T(8,128)(2,1)S(1)} %collective-permute-done), channel_id=1, source_target_pairs={{0,16},{1,17},{2,18},{3,19},{4,20},{5,21},{6,22},{7,23},{8,0},{9,1... | collective-permute-start | bytes 516104 | tf_op jit(solution)/shard_map/ppermute | solution.py:70
  14.2 10.5 %collective-permute-start.8 = (bf16[32,1408]{1,0:T(8,128)(2,1)S(1)}, bf16[32,1408]{1,0:T(8,128)(2,1)S(1)}, u32[]{:S(2)}, u32[]{:S(2)}) collective-permute-start(bf16[32,1408]{1,0:T(8,128)(2,1)S(1)} %collective-permute-done.7), channel_id=1, source_target_pairs={{0,2},{1,5},{2,6},{3,1},{4,0},{5,7},{6,4},{7,3},{8,10},{9,13},{10,... | collective-permute-start | bytes 270344 | tf_op jit(solution)/shard_map/ppermute | solution.py:70
  17.1 6.3 %collective-permute-start.2 = (bf16[32,2688]{1,0:T(8,128)(2,1)S(1)}, bf16[32,2688]{1,0:T(8,128)(2,1)S(1)}, u32[]{:S(2)}, u32[]{:S(2)}) collective-permute-start(bf16[32,2688]{1,0:T(8,128)(2,1)S(1)} %collective-permute-done.1), channel_id=1, source_target_pairs={{0,16},{1,17},{2,18},{3,19},{4,20},{5,21},{6,22},{7,23},{8,0},{9,1... | collective-permute-start | bytes 516104 | tf_op jit(solution)/shard_map/ppermute | solution.py:70
  23.5 14.3 %collective-permute-start.3 = (bf16[128,2688]{1,0:T(8,128)(2,1)S(1)}, bf16[128,2688]{1,0:T(8,128)(2,1)S(1)}, u32[]{:S(2)}, u32[]{:S(2)}) collective-permute-start(bf16[128,2688]{1,0:T(8,128)(2,1)S(1)} %pad_maximum_fusion.8), channel_id=1, source_target_pairs={{0,2},{1,5},{2,6},{3,1},{4,0},{5,7},{6,4},{7,3},{8,10},{9,13},{10,... | collective-permute-start | bytes 2064392 | tf_op jit(solution)/shard_map/ppermute | solution.py:70
  24.8 9.6 %collective-permute-start.9 = (bf16[128,1408]{1,0:T(8,128)(2,1)S(1)}, bf16[128,1408]{1,0:T(8,128)(2,1)S(1)}, u32[]{:S(2)}, u32[]{:S(2)}) collective-permute-start(bf16[128,1408]{1,0:T(8,128)(2,1)S(1)} %pad_maximum_fusion.10), channel_id=1, source_target_pairs={{0,16},{1,17},{2,18},{3,19},{4,20},{5,21},{6,22},{7,23},{8,0},{9,1... | collective-permute-start | bytes 1081352 | tf_op jit(solution)/shard_map/ppermute | solution.py:70
  34.4 8.6 %collective-permute-start.10 = (bf16[128,1408]{1,0:T(8,128)(2,1)S(1)}, bf16[128,1408]{1,0:T(8,128)(2,1)S(1)}, u32[]{:S(2)}, u32[]{:S(2)}) collective-permute-start(bf16[128,1408]{1,0:T(8,128)(2,1)S(1)} %collective-permute-done.9), channel_id=1, source_target_pairs={{0,16},{1,17},{2,18},{3,19},{4,20},{5,21},{6,22},{7,23},{8,0},{9,1... | collective-permute-start | bytes 1081352 | tf_op jit(solution)/shard_map/ppermute | solution.py:70
  37.8 10.9 %collective-permute-start.4 = (bf16[128,2688]{1,0:T(8,128)(2,1)S(1)}, bf16[128,2688]{1,0:T(8,128)(2,1)S(1)}, u32[]{:S(2)}, u32[]{:S(2)}) collective-permute-start(bf16[128,2688]{1,0:T(8,128)(2,1)S(1)} %collective-permute-done.3), channel_id=1, source_target_pairs={{0,2},{1,5},{2,6},{3,1},{4,0},{5,7},{6,4},{7,3},{8,10},{9,13},{10,... | collective-permute-start | bytes 2064392 | tf_op jit(solution)/shard_map/ppermute | solution.py:70
  43.0 8.5 %collective-permute-start.11 = (bf16[128,1408]{1,0:T(8,128)(2,1)S(1)}, bf16[128,1408]{1,0:T(8,128)(2,1)S(1)}, u32[]{:S(2)}, u32[]{:S(2)}) collective-permute-start(bf16[128,1408]{1,0:T(8,128)(2,1)S(1)} %collective-permute-done.10), channel_id=1, source_target_pairs={{0,16},{1,17},{2,18},{3,19},{4,20},{5,21},{6,22},{7,23},{8,0},{9,1... | collective-permute-start | bytes 1081352 | tf_op jit(solution)/shard_map/ppermute | solution.py:70
  48.7 12.1 %collective-permute-start.5 = (bf16[128,2688]{1,0:T(8,128)(2,1)S(1)}, bf16[128,2688]{1,0:T(8,128)(2,1)S(1)}, u32[]{:S(2)}, u32[]{:S(2)}) collective-permute-start(bf16[128,2688]{1,0:T(8,128)(2,1)S(1)} %collective-permute-done.4), channel_id=1, source_target_pairs={{0,2},{1,5},{2,6},{3,1},{4,0},{5,7},{6,4},{7,3},{8,10},{9,13},{10,... | collective-permute-start | bytes 2064392 | tf_op jit(solution)/shard_map/ppermute | solution.py:70
  73.2 8.4 %collective-permute-start.13 = (bf16[4,128,1792]{2,1,0:T(8,128)(2,1)S(1)}, bf16[4,128,1792]{2,1,0:T(8,128)(2,1)S(1)}, u32[]{:S(2)}, u32[]{:S(2)}) collective-permute-start(bf16[4,128,1792]{2,1,0:T(8,128)(2,1)S(1)} %bitcast.115), channel_id=1, source_target_pairs={{0,1},{1,0},{2,3},{3,2},{4,5},{5,4},{6,7},{7,6},{8,9},{9,8},{10,11... | collective-permute-start | bytes 5505032 | tf_op jit(solution)/shard_map/ppermute | solution.py:112
  97.1 11.0 %collective-permute-start.14 = (bf16[128,2688]{1,0:T(8,128)(2,1)S(1)}, bf16[128,2688]{1,0:T(8,128)(2,1)S(1)}, u32[]{:S(2)}, u32[]{:S(2)}) collective-permute-start(bf16[128,2688]{1,0:T(8,128)(2,1)S(1)} %slice.176), channel_id=1, source_target_pairs={{0,4},{1,3},{2,0},{3,7},{4,6},{5,1},{6,2},{7,5},{8,12},{9,11},{10,... | collective-permute-start | bytes 2064392 | tf_op jit(solution)/shard_map/ppermute | solution.py:77
  108.3 11.4 %collective-permute-start.15 = (bf16[128,2688]{1,0:T(8,128)(2,1)S(1)}, bf16[128,2688]{1,0:T(8,128)(2,1)S(1)}, u32[]{:S(2)}, u32[]{:S(2)}) collective-permute-start(bf16[128,2688]{1,0:T(8,128)(2,1)S(1)} %add_convert_fusion.2), channel_id=1, source_target_pairs={{0,4},{1,3},{2,0},{3,7},{4,6},{5,1},{6,2},{7,5},{8,12},{9,11},{10,... | collective-permute-start | bytes 2064392 | tf_op jit(solution)/shard_map/ppermute | solution.py:77
  119.9 11.0 %collective-permute-start.16 = (bf16[128,2688]{1,0:T(8,128)(2,1)S(1)}, bf16[128,2688]{1,0:T(8,128)(2,1)S(1)}, u32[]{:S(2)}, u32[]{:S(2)}) collective-permute-start(bf16[128,2688]{1,0:T(8,128)(2,1)S(1)} %add_convert_fusion.1), channel_id=1, source_target_pairs={{0,4},{1,3},{2,0},{3,7},{4,6},{5,1},{6,2},{7,5},{8,12},{9,11},{10,... | collective-permute-start | bytes 2064392 | tf_op jit(solution)/shard_map/ppermute | solution.py:77
  131.1 8.3 %collective-permute-start.17 = (bf16[32,2688]{1,0:T(8,128)(2,1)S(1)}, bf16[32,2688]{1,0:T(8,128)(2,1)S(1)}, u32[]{:S(2)}, u32[]{:S(2)}) collective-permute-start(bf16[32,2688]{1,0:T(8,128)(2,1)S(1)} %slice.180), channel_id=1, source_target_pairs={{0,8},{1,9},{2,10},{3,11},{4,12},{5,13},{6,14},{7,15},{8,24},{9,25... | collective-permute-start | bytes 516104 | tf_op jit(solution)/shard_map/ppermute | solution.py:77
  131.3 15.6 %collective-permute-start.20 = (bf16[128,1408]{1,0:T(8,128)(2,1)S(1)}, bf16[128,1408]{1,0:T(8,128)(2,1)S(1)}, u32[]{:S(2)}, u32[]{:S(2)}) collective-permute-start(bf16[128,1408]{1,0:T(8,128)(2,1)S(1)} %bitcast.130), channel_id=1, source_target_pairs={{0,8},{1,9},{2,10},{3,11},{4,12},{5,13},{6,14},{7,15},{8,24},{9,25... | collective-permute-start | bytes 1081352 | tf_op jit(solution)/shard_map/ppermute | solution.py:77
  139.4 11.2 %collective-permute-start.18 = (bf16[32,2688]{1,0:T(8,128)(2,1)S(1)}, bf16[32,2688]{1,0:T(8,128)(2,1)S(1)}, u32[]{:S(2)}, u32[]{:S(2)}) collective-permute-start(bf16[32,2688]{1,0:T(8,128)(2,1)S(1)} %add_convert_fusion.5), channel_id=1, source_target_pairs={{0,8},{1,9},{2,10},{3,11},{4,12},{5,13},{6,14},{7,15},{8,24},{9,25... | collective-permute-start | bytes 516104 | tf_op jit(solution)/shard_map/ppermute | solution.py:77
  147.0 12.2 %collective-permute-start.21 = (bf16[128,1408]{1,0:T(8,128)(2,1)S(1)}, bf16[128,1408]{1,0:T(8,128)(2,1)S(1)}, u32[]{:S(2)}, u32[]{:S(2)}) collective-permute-start(bf16[128,1408]{1,0:T(8,128)(2,1)S(1)} %fusion.15), channel_id=1, source_target_pairs={{0,8},{1,9},{2,10},{3,11},{4,12},{5,13},{6,14},{7,15},{8,24},{9,25... | collective-permute-start | bytes 1081352 | tf_op jit(solution)/shard_map/ppermute | solution.py:77
  150.7 12.3 %collective-permute-start.19 = (bf16[32,2688]{1,0:T(8,128)(2,1)S(1)}, bf16[32,2688]{1,0:T(8,128)(2,1)S(1)}, u32[]{:S(2)}, u32[]{:S(2)}) collective-permute-start(bf16[32,2688]{1,0:T(8,128)(2,1)S(1)} %add_convert_fusion.4), channel_id=1, source_target_pairs={{0,8},{1,9},{2,10},{3,11},{4,12},{5,13},{6,14},{7,15},{8,24},{9,25... | collective-permute-start | bytes 516104 | tf_op jit(solution)/shard_map/ppermute | solution.py:77
  159.4 13.5 %collective-permute-start.22 = (bf16[128,1408]{1,0:T(8,128)(2,1)S(1)}, bf16[128,1408]{1,0:T(8,128)(2,1)S(1)}, u32[]{:S(2)}, u32[]{:S(2)}) collective-permute-start(bf16[128,1408]{1,0:T(8,128)(2,1)S(1)} %fusion.14), channel_id=1, source_target_pairs={{0,8},{1,9},{2,10},{3,11},{4,12},{5,13},{6,14},{7,15},{8,24},{9,25... | collective-permute-start | bytes 1081352 | tf_op jit(solution)/shard_map/ppermute | solution.py:77
  163.0 12.0 %collective-permute-start.26 = (bf16[4,8,2688]{2,1,0:T(8,128)(2,1)S(1)}, bf16[4,8,2688]{2,1,0:T(8,128)(2,1)S(1)}, u32[]{:S(2)}, u32[]{:S(2)}) collective-permute-start(bf16[4,8,2688]{2,1,0:T(8,128)(2,1)S(1)} %bitcast.118), channel_id=1, source_target_pairs={{0,16},{1,17},{2,18},{3,19},{4,20},{5,21},{6,22},{7,23},{8,0},{9,1... | collective-permute-start | bytes 516104 | tf_op jit(solution)/shard_map/ppermute | solution.py:70
  177.6 5.6 %collective-permute-start.24 = (bf16[32,1408]{1,0:T(8,128)(2,1)S(1)}, bf16[32,1408]{1,0:T(8,128)(2,1)S(1)}, u32[]{:S(2)}, u32[]{:S(2)}) collective-permute-start(bf16[32,1408]{1,0:T(8,128)(2,1)S(1)} %add_convert_fusion.8), channel_id=1, source_target_pairs={{0,4},{1,3},{2,0},{3,7},{4,6},{5,1},{6,2},{7,5},{8,12},{9,11},{10,... | collective-permute-start | bytes 270344 | tf_op jit(solution)/shard_map/ppermute | solution.py:77
  183.2 5.6 %collective-permute-start.25 = (bf16[32,1408]{1,0:T(8,128)(2,1)S(1)}, bf16[32,1408]{1,0:T(8,128)(2,1)S(1)}, u32[]{:S(2)}, u32[]{:S(2)}) collective-permute-start(bf16[32,1408]{1,0:T(8,128)(2,1)S(1)} %add_convert_fusion.7), channel_id=1, source_target_pairs={{0,4},{1,3},{2,0},{3,7},{4,6},{5,1},{6,2},{7,5},{8,12},{9,11},{10,... | collective-permute-start | bytes 270344 | tf_op jit(solution)/shard_map/ppermute | solution.py:77
  186.0 22.9 %collective-permute-start.29 = (bf16[4,32,2688]{2,1,0:T(8,128)(2,1)S(1)}, bf16[4,32,2688]{2,1,0:T(8,128)(2,1)S(1)}, u32[]{:S(2)}, u32[]{:S(2)}) collective-permute-start(bf16[4,32,2688]{2,1,0:T(8,128)(2,1)S(1)} %get-tuple-element.15), channel_id=1, source_target_pairs={{0,2},{1,5},{2,6},{3,1},{4,0},{5,7},{6,4},{7,3},{8,10},{9,13},{10,... | collective-permute-start | bytes 2064392 | tf_op jit(solution)/shard_map/ppermute | solution.py:70
  188.9 9.0 %collective-permute-start.32 = (bf16[4,8,1408]{2,1,0:T(8,128)(2,1)S(1)}, bf16[4,8,1408]{2,1,0:T(8,128)(2,1)S(1)}, u32[]{:S(2)}, u32[]{:S(2)}) collective-permute-start(bf16[4,8,1408]{2,1,0:T(8,128)(2,1)S(1)} %bitcast.125), channel_id=1, source_target_pairs={{0,2},{1,5},{2,6},{3,1},{4,0},{5,7},{6,4},{7,3},{8,10},{9,13},{10,... | collective-permute-start | bytes 270344 | tf_op jit(solution)/shard_map/ppermute | solution.py:70
  207.0 7.9 %collective-permute-start.35 = (bf16[4,32,1408]{2,1,0:T(8,128)(2,1)S(1)}, bf16[4,32,1408]{2,1,0:T(8,128)(2,1)S(1)}, u32[]{:S(2)}, u32[]{:S(2)}) collective-permute-start(bf16[4,32,1408]{2,1,0:T(8,128)(2,1)S(1)} %get-tuple-element.17), channel_id=1, source_target_pairs={{0,16},{1,17},{2,18},{3,19},{4,20},{5,21},{6,22},{7,23},{8,0},{9,1... | collective-permute-start | bytes 1081352 | tf_op jit(solution)/shard_map/ppermute | solution.py:70
  208.9 16.9 %collective-permute-start.30 = (bf16[4,32,2688]{2,1,0:T(8,128)(2,1)S(1)}, bf16[4,32,2688]{2,1,0:T(8,128)(2,1)S(1)}, u32[]{:S(2)}, u32[]{:S(2)}) collective-permute-start(bf16[4,32,2688]{2,1,0:T(8,128)(2,1)S(1)} %collective-permute-done.29), channel_id=1, source_target_pairs={{0,2},{1,5},{2,6},{3,1},{4,0},{5,7},{6,4},{7,3},{8,10},{9,13},{10,... | collective-permute-start | bytes 2064392 | tf_op jit(solution)/shard_map/ppermute | solution.py:70
  214.9 9.3 %collective-permute-start.36 = (bf16[4,32,1408]{2,1,0:T(8,128)(2,1)S(1)}, bf16[4,32,1408]{2,1,0:T(8,128)(2,1)}, u32[]{:S(2)}, u32[]{:S(2)}) collective-permute-start(bf16[4,32,1408]{2,1,0:T(8,128)(2,1)S(1)} %collective-permute-done.35), channel_id=1, source_target_pairs={{0,16},{1,17},{2,18},{3,19},{4,20},{5,21},{6,22},{7,23},{8,0},{9,1... | collective-permute-start | bytes 1081352 | tf_op jit(solution)/shard_map/ppermute | solution.py:70
  224.2 8.4 %collective-permute-start.37 = (bf16[4,32,1408]{2,1,0:T(8,128)(2,1)}, bf16[4,32,1408]{2,1,0:T(8,128)(2,1)}, u32[]{:S(2)}, u32[]{:S(2)}) collective-permute-start(bf16[4,32,1408]{2,1,0:T(8,128)(2,1)} %collective-permute-done.36), channel_id=1, source_target_pairs={{0,16},{1,17},{2,18},{3,19},{4,20},{5,21},{6,22},{7,23},{8,0},{9,1... | collective-permute-start | bytes 1081352 | tf_op jit(solution)/shard_map/ppermute | solution.py:70
  225.8 11.1 %collective-permute-start.31 = (bf16[4,32,2688]{2,1,0:T(8,128)(2,1)S(1)}, bf16[4,32,2688]{2,1,0:T(8,128)(2,1)}, u32[]{:S(2)}, u32[]{:S(2)}) collective-permute-start(bf16[4,32,2688]{2,1,0:T(8,128)(2,1)S(1)} %collective-permute-done.30), channel_id=1, source_target_pairs={{0,2},{1,5},{2,6},{3,1},{4,0},{5,7},{6,4},{7,3},{8,10},{9,13},{10,... | collective-permute-start | bytes 2064392 | tf_op jit(solution)/shard_map/ppermute | solution.py:70
  (13 other events, 149.5 us)

commit v2 on v1

--- a/solution.py
+++ b/solution.py
@@ -4,6 +4,8 @@
 import jax.numpy as jnp
 import numpy as np
 from jax import lax
+from jax.experimental import pallas as pl
+from jax.experimental.pallas import tpu as pltpu
 from jax.sharding import PartitionSpec as P
 
 BF16 = jnp.bfloat16
@@ -63,27 +65,40 @@
     def size(self, which):
         return self.npl if which == "p" else self.nz
 
-    def gather(self, x, which):
-        perm = self.perm(which, False)
-        out = [x]
-        for _ in range(self.size(which) - 1):
-            out.append(lax.ppermute(out[-1], ("feat", "tok"), perm))
-        return out
-
-    def scatter(self, parts, which):
-        perm = self.perm(which, True)
-        acc = parts[-1]
-        for part in parts[-2::-1]:
-            got = lax.ppermute(acc, ("feat", "tok"), perm)
-            acc = (got.astype(F32) + part.astype(F32)).astype(BF16)
-        return acc
+    def step(self, x, which, back=False):
+        return lax.ppermute(x, ("feat", "tok"), self.perm(which, back))
+
+    def gather(self, a, b, wa, wb):
+        a, b = [a], [b]
+        for k in range(1, max(self.size(wa), self.size(wb))):
+            if k < self.size(wa):
+                a.append(self.step(a[-1], wa))
+            if k < self.size(wb):
+                b.append(self.step(b[-1], wb))
+            a[-1], b[-1] = lax.optimization_barrier((a[-1], b[-1]))
+        return a, b
+
+    def scatter(self, parts_a, parts_b, wa, wb, source):
+        ja, jb = self.size(wa) - 1, self.size(wb) - 1
+        a, b = parts_a(source, ja), parts_b(source, jb)
+        while ja or jb:
+            a, b, source = lax.optimization_barrier((a, b, source))
+            got = [self.step(a, wa, True) if ja else a, self.step(b, wb, True) if jb else b]
+            more = [parts_a(source, ja - 1) if ja else None, parts_b(source, jb - 1) if jb else None]
+            got, more = lax.optimization_barrier((got, more))
+            a, b = (
+                g if m is None else (g.astype(F32) + m.astype(F32)).astype(BF16)
+                for g, m in zip(got, more)
+            )
+            ja, jb = max(ja - 1, 0), max(jb - 1, 0)
+        return a, b
 
 
 def mirror(n):
     return [(n - j) % n for j in range(n)]
 
 
-def on_device(tokens, gate_weight, up_weight, down_weight, alignment):
+def on_any(tokens, gate_weight, up_weight, down_weight, alignment):
     n_feat, n_tok = lax.axis_size("feat"), lax.axis_size("tok")
     rings = Rings(n_feat, n_tok)
     nz, npl = rings.nz, rings.npl
@@ -95,10 +110,9 @@
 
     x = tokens.transpose(1, 0, 2).reshape(rows, width)
 
-    a = jnp.concatenate(rings.gather(x[:, :cut], "z"), 0)
-    a = jnp.concatenate(rings.gather(a, "p"), 0)
-    b = jnp.concatenate(rings.gather(x[:, cut:], "p"), 0)
-    b = jnp.concatenate(rings.gather(b, "z"), 0)
+    a, b = rings.gather(x[:, :cut], x[:, cut:], "z", "p")
+    a, b = rings.gather(jnp.concatenate(a, 0), jnp.concatenate(b, 0), "p", "z")
+    a, b = jnp.concatenate(a, 0), jnp.concatenate(b, 0)
     b = b.reshape(nz, npl, rows, width - cut).transpose(1, 0, 2, 3).reshape(-1, width - cut)
     full = jnp.concatenate((a, b), 1)
 
@@ -120,25 +134,27 @@
     hidden = (jax.nn.silu(over_tok(gate)) * over_tok(up)).astype(BF16)
     hidden = hidden.reshape(-1, hid)
 
-    oa = jnp.dot(hidden, down_weight[:, :cut], preferred_element_type=F32).astype(BF16)
-    ob = jnp.dot(hidden, down_weight[:, cut:], preferred_element_type=F32).astype(BF16)
-
-    oa = oa.reshape(npl, nz * rows, cut)
-    oa = rings.scatter([oa[j] for j in range(npl)], "p").reshape(nz, rows, cut)
-    oa = rings.scatter([oa[i] for i in range(nz)], "z")
-    ob = ob.reshape(npl, nz, rows, width - cut)
-    ob = rings.scatter([ob[:, i].reshape(npl * rows, -1) for i in range(nz)], "z")
-    ob = ob.reshape(npl, rows, width - cut)
-    ob = rings.scatter([ob[j] for j in range(npl)], "p")
+    def down_a(h, j):
+        h = h.reshape(npl, -1, hid)[j]
+        return jnp.dot(h, down_weight[:, :cut], preferred_element_type=F32).astype(BF16)
+
+    def down_b(h, i):
+        h = h.reshape(npl, nz, rows, hid)[:, i].reshape(-1, hid)
+        return jnp.dot(h, down_weight[:, cut:], preferred_element_type=F32).astype(BF16)
+
+    oa, ob = rings.scatter(down_a, down_b, "p", "z", hidden)
+    oa, ob = oa.reshape(nz, rows, cut), ob.reshape(npl, rows, width - cut)
+    oa, ob = rings.scatter(lambda s, j: s[0][j], lambda s, j: s[1][j], "z", "p", (oa, ob))
 
     ffn_out = jnp.concatenate((oa, ob), 1).reshape(langs, own, width).transpose(1, 0, 2)
 
-    a = jnp.stack(rings.gather(oa.reshape(langs, own, cut), "z"), 1)
-    a = a.reshape(langs, nz * own, cut)
-    a = jnp.stack(rings.gather(a, "p"), 1).reshape(langs, -1, cut)
-    b = jnp.stack(rings.gather(ob.reshape(langs, own, width - cut), "p"), 1)
-    b = b.reshape(langs, npl * own, width - cut)
-    b = jnp.stack(rings.gather(b, "z"), 1)
+    a, b = oa.reshape(langs, own, cut), ob.reshape(langs, own, width - cut)
+    a, b = rings.gather(a, b, "z", "p")
+    a = jnp.stack(a, 1).reshape(langs, nz * own, cut)
+    b = jnp.stack(b, 1).reshape(langs, npl * own, width - cut)
+    a, b = rings.gather(a, b, "p", "z")
+    a = jnp.stack(a, 1).reshape(langs, -1, cut)
+    b = jnp.stack(b, 1)
     b = b.reshape(langs, nz, npl, own, width - cut).transpose(0, 2, 1, 3, 4)
     b = b.reshape(langs, -1, width - cut)
     out_all = jnp.concatenate((a, b), 2)
@@ -179,9 +195,192 @@
     return ffn_out, cross
 
 
+class Small:
+    def __init__(self):
+        self.rings = Rings(16, 2)
+
+    def mask(self, slot, t):
+        one, two = slot & 1, slot >> 1
+        return one + 2 * two if t == 0 else 2 * one + two
+
+    def plane(self, x, slot):
+        pairs = [(2 * f + t, 2 * (f ^ self.mask(slot, t)) + t) for f in range(16) for t in range(2)]
+        return lax.ppermute(x, ("feat", "tok"), pairs)
+
+    def z(self, x, slot=1, back=False):
+        pairs = []
+        for f in range(16):
+            for t in range(2):
+                pair = (2 * self.rings.source(f, t, 0, slot) + t, 2 * f + t)
+                pairs.append(pair[::-1] if back else pair)
+        return lax.ppermute(x, ("feat", "tok"), sorted(pairs))
+
+    def tokens(self, own):
+        ids = np.zeros((16, 2, 4, 4, own), np.int32)
+        for f in range(16):
+            for t in range(2):
+                for p in range(4):
+                    for i in range(4):
+                        source = self.rings.source(f ^ self.mask(p, t), t, 0, i)
+                        ids[f, t, p, i] = source * own + np.arange(own)
+        return ids.reshape(32, -1)
+
+
+def total(*parts):
+    return sum(p.astype(F32) for p in parts).astype(BF16)
+
+
+def cross_kernel(scaling, hot_a, hot_b, english, *refs):
+    out, moved_a, moved_b = refs[8:]
+    lang, step = pl.program_id(0), pl.program_id(1)
+    tile = out.shape[1]
+
+    @pl.when(step == 0)
+    def _():
+        for hot, moved in ((hot_a, moved_a), (hot_b, moved_b)):
+            rows = jnp.dot(hot[lang], english[...], preferred_element_type=F32)
+            moved[...] = rows.astype(BF16).T
+
+    at = pl.ds(pl.multiple_of(step * tile, tile), tile)
+    start = 0
+    for moved, blocks in ((moved_a, refs[:4]), (moved_b, refs[4:8])):
+        width = blocks[0].shape[2]
+        rows = jnp.concatenate([b[lang + 1] for b in blocks], 0)
+        out[0, :, start:start + width] = jnp.dot(
+            moved[at, :], rows, preferred_element_type=F32
+        ) * scaling
+        start += width
+
+
+def cross_products(hot_a, hot_b, english, a, b, scaling):
+    langs, tokens, _ = hot_a.shape
+    height = english.shape[1]
+    width = a[0].shape[2] + b[0].shape[2]
+    tile = 256
+    return pl.pallas_call(
+        lambda *refs: cross_kernel(scaling, *refs),
+        grid=(langs, height // tile),
+        in_specs=[pl.BlockSpec(memory_space=pltpu.VMEM)] * 11,
+        out_specs=pl.BlockSpec((1, tile, width), lambda l, r: (l, r, 0)),
+        out_shape=jax.ShapeDtypeStruct((langs, height, width), F32),
+        scratch_shapes=[pltpu.VMEM((height, tokens), BF16)] * 2,
+        compiler_params=pltpu.CompilerParams(
+            dimension_semantics=("arbitrary", "arbitrary"), vmem_limit_bytes=16 << 20
+        ),
+    )(hot_a, hot_b, english, *a, *b)
+
+
+def on_small(tokens, gate_weight, up_weight, down_weight, alignment):
+    net = Small()
+    own, langs, width = tokens.shape
+    rows = own * langs
+    hid = gate_weight.shape[1]
+    f, t = lax.axis_index("feat"), lax.axis_index("tok")
+    cut = width * 5 // 8
+    lock = lax.optimization_barrier
+
+    x = tokens.transpose(1, 0, 2).reshape(rows, width)
+
+    a, b = x[:, :cut], x[:, cut:]
+    b1, a1, b2, a2, b3, a3 = (
+        net.plane(b, 1), net.z(a, 1), net.plane(b, 2), net.z(a, 3), net.plane(b, 3), None
+    )
+    a3 = net.z(a1, 1)
+    a0 = jnp.concatenate((a, a1, a3, a2), 0)
+    b0 = jnp.concatenate((b, b1, b2, b3), 0)
+    a0, b0 = lock((a0, b0))
+    a0, a1, b1 = lock((a0, net.plane(a0, 1), net.z(b0)))
+    a0, a1, a2, b2 = lock((a0, a1, net.plane(a0, 2), net.z(b1)))
+    a3, b3 = lock((net.plane(a1, 2), net.z(b2)))
+    a = jnp.concatenate((a0, a1, a2, a3), 0)
+    b = jnp.stack((b0, b1, b2, b3)).reshape(4, 4, rows, width - cut)
+    b = b.transpose(1, 0, 2, 3).reshape(-1, width - cut)
+    full = jnp.concatenate((a, b), 1)
+
+    def core(v):
+        return lax.ppermute(v, "tok", [(0, 1), (1, 0)])
+
+    def mirror(v):
+        v = v.reshape(4, -1, v.shape[-1])
+        return jnp.stack((v[0], v[2], v[1], v[3])).reshape(-1, v.shape[-1])
+
+    gate = jnp.dot(full, gate_weight, preferred_element_type=F32).astype(BF16)
+    up = jnp.dot(full, up_weight, preferred_element_type=F32).astype(BF16)
+    gate = gate.astype(F32) + mirror(core(gate)).astype(F32)
+    up = up.astype(F32) + mirror(core(up)).astype(F32)
+    hidden = (jax.nn.silu(gate) * up).astype(BF16)
+
+    def down_a(h, j):
+        h = h[j * 4 * rows:(j + 1) * 4 * rows]
+        return jnp.dot(h, down_weight[:, :cut], preferred_element_type=F32).astype(BF16)
+
+    def down_b(h, i):
+        h = h.reshape(4, 4, rows, hid)[:, i].reshape(-1, hid)
+        return jnp.dot(h, down_weight[:, cut:], preferred_element_type=F32).astype(BF16)
+
+    p, q = down_a(hidden, 3), down_b(hidden, 3)
+    p, q, hidden = lock((p, q, hidden))
+    s3, r3 = net.plane(p, 2), net.z(q, back=True)
+    p, q = down_a(hidden, 2), down_b(hidden, 2)
+    s3, r3, p, q, hidden = lock((s3, r3, p, q, hidden))
+    p, q, hidden = lock((p, total(q, r3), hidden))
+    s2, r2 = net.plane(p, 2), net.z(q, back=True)
+    p, q = down_a(hidden, 1), down_b(hidden, 1)
+    s2, r2, p, q, hidden = lock((s2, r2, p, q, hidden))
+    p, q, hidden = lock((total(p, s3), total(q, r2), hidden))
+    s1, r1 = net.plane(p, 1), net.z(q, back=True)
+    p, q = down_a(hidden, 0), down_b(hidden, 0)
+    s1, r1, p, q = lock((s1, r1, p, q))
+    p = total(p, s1, s2).reshape(4, rows, cut)
+    q = total(q, r1).reshape(4, rows, width - cut)
+    p, q = lock((p, q))
+    got = lock((
+        net.plane(q[1], 1), net.z(p[1], 1, True), net.plane(q[2], 2),
+        net.z(p[3], 3, True), net.plane(q[3], 3), net.z(p[2], 2, True),
+    ))
+    p, q = lock((total(p[0], *got[1::2]), total(q[0], *got[::2])))
+
+    ffn_out = jnp.concatenate((p, q), 1).reshape(langs, own, width).transpose(1, 0, 2)
+
+    got = lock((
+        net.plane(q, 1), net.z(p, 1), net.plane(q, 2), net.z(p, 3), net.plane(q, 3), net.z(p, 2)
+    ))
+
+    def join(*v):
+        v = [x.reshape(langs, own, -1) for x in v]
+        return jnp.stack(v, 1).reshape(langs, 4 * own, -1)
+
+    p0 = join(p, got[1], got[5], got[3])
+    q0 = join(q, got[0], got[2], got[4])
+    p0, q0 = lock((p0, q0))
+    p0, p1, q1 = lock((p0, net.plane(p0, 1), net.z(q0)))
+    p0, p1, p2, q2 = lock((p0, p1, net.plane(p0, 2), net.z(q1)))
+    p3, q3 = lock((net.plane(p1, 2), net.z(q2)))
+
+    ea = jnp.concatenate((p0[0], p1[0], p2[0], p3[0]), 0)
+    eb = jnp.stack((q0[0], q1[0], q2[0], q3[0])).reshape(4, 4, own, width - cut)
+    eb = eb.transpose(1, 0, 2, 3).reshape(-1, width - cut)
+    fw = width // 8
+    block = lax.dynamic_slice_in_dim(jnp.concatenate((ea, eb), 1), f % 8 * fw, fw, 1)
+    english = jnp.where(f // 8 == t, block, mirror(core(block)))
+
+    ids = jnp.asarray(net.tokens(own))
+    ids = lax.dynamic_index_in_dim(ids, f * 2 + t, 0, keepdims=False)
+    targets = jnp.take(alignment, ids, axis=1)
+    hot_a = (ids[None, :, None] == targets[:, None, :]).astype(BF16)
+    hot_b = hot_a.reshape(-1, 4, 4, own, 16 * own).transpose(0, 2, 1, 3, 4).reshape(hot_a.shape)
+    scaling = 1.0 / math.sqrt(own * 16)
+    cross = cross_products(
+        hot_a, hot_b, english, (p0, p1, p2, p3), (q0, q1, q2, q3), scaling
+    )
+    return ffn_out, cross
+
+
 def solution(mesh):
     in_specs = (P("feat", None, "tok"), P("tok", "feat"), P("tok", "feat"), P("feat", "tok"), P())
     out_specs = (P("feat", None, "tok"), P(None, "feat", "tok"))
+    small = mesh.shape["feat"] == 16 and mesh.shape["tok"] == 2
+    body = on_small if small else on_any
     return jax.shard_map(
-        on_device, mesh=mesh, in_specs=in_specs, out_specs=out_specs, check_vma=False
+        body, mesh=mesh, in_specs=in_specs, out_specs=out_specs, check_vma=False
     )

time: 253 us -> 206 us (0.81)
  waiting for transfers between devices: 133 us -> 100 us
  matrix products: 47.2 us -> 35.3 us
  Pallas kernels: 0 us -> 10.3 us
  starting transfers between devices: 57.7 us -> 48.5 us
    ppermute x39, waiting for transfers between devices: 133 us -> 100 us  [the longest x18 82 us: z(): return lax.ppermute(x, ('feat', 'tok'), sorted(pairs))]
    dot_general x5 -> x10, matrix products: 47.2 us -> 35.3 us  [the longest x1 13 us: on_small(): up = jnp.dot(full, up_weight, preferred_element_type=F32).astype(BF16)]
    pallas_call x0 -> x1, Pallas kernels: none -> 10.3 us  [cross_products(): pl.pallas_call(lambda *refs: cross_kernel(scaling, *refs), grid=(langs, h...]
    ppermute x39, starting transfers between devices: 57.7 us -> 48.5 us  [the longest x18 26.9 us: z(): return lax.ppermute(x, ('feat', 'tok'), sorted(pairs))]
  transfers between devices with their start and end apart: 39 -> 39, of which waited for: 30 -> 25; matrix products, arithmetic and copies ran while one was open for 8% -> 12% of each run, Pallas kernels for 0% -> 0%
where the time goes in v2:
time: 206 us
  waiting for transfers between devices  100 us (49%)
  starting transfers between devices  48.5 us (24%)
  matrix products  35.3 us (17%)
  Pallas kernels  10.3 us (5%)
  other arithmetic  5.75 us (3%)
  local copies, waits for them, and re-layouts  4.45 us (2%)
    ppermute x18, waiting for transfers between devices, z(): return lax.ppermute(x, ('feat', 'tok'), sorted(pairs))  82 us
    ppermute x18, starting transfers between devices, z(): return lax.ppermute(x, ('feat', 'tok'), sorted(pairs))  26.9 us
    ppermute x18, starting transfers between devices, plane(): return lax.ppermute(x, ('feat', 'tok'), pairs)  20.9 us
    ppermute x18, waiting for transfers between devices, plane(): return lax.ppermute(x, ('feat', 'tok'), pairs)  14.5 us
    dot_general x1, matrix products, on_small(): up = jnp.dot(full, up_weight, preferred_element_type=F32).astype(BF16)  13 us
    dot_general x1, matrix products, on_small(): gate = jnp.dot(full, gate_weight, preferred_element_type=F32).astype(BF16)  12.9 us
    pallas_call x1, Pallas kernels, cross_products(): pl.pallas_call(lambda *refs: cross_kernel(scaling, *refs), grid=(langs, h...  10.3 us
    dot_general x4, matrix products, down_a(): jnp.dot(h, down_weight[:, :cut], preferred_element_type=F32).astype(BF16)  5.72 us
  transfers between devices with their start and end apart: 39, of which 25 were waited for; matrix products, arithmetic and copies ran while one was open for 12% of the time, Pallas kernels for 0%

profile of v2, /device:TPU:0, one launch (start us, length us, event | category | flops | bytes accessed | tf_op | source)
XLA Modules:
  0.0 205.7 jit_solution(9064999909858456128)
XLA Ops:
  1.8 4.1 %collective-permute-start = (bf16[32,2560]{1,0:T(8,128)(2,1)S(1)}, bf16[32,2560]{1,0:T(8,128)(2,1)S(1)}, u32[]{:S(2)}, u32[]{:S(2)}) collective-permute-start(bf16[32,2560]{1,0:T(8,128)(2,1)S(1)} %slice.216), channel_id=1, source_target_pairs={{0,16},{1,17},{2,18},{3,19},{4,20},{5,21},{6,22},{7,23},{8,0},{9,1... | collective-permute-start | bytes 491528 | tf_op jit(solution)/shard_map/ppermute | solution.py:216
  5.8 2.5 %collective-permute-start.5 = (bf16[32,1536]{1,0:T(8,128)(2,1)S(1)}, bf16[32,1536]{1,0:T(8,128)(2,1)S(1)}, u32[]{:S(2)}, u32[]{:S(2)}) collective-permute-start(bf16[32,1536]{1,0:T(8,128)(2,1)S(1)} %slice.217), channel_id=1, source_target_pairs={{0,6},{1,7},{2,4},{3,5},{4,2},{5,3},{6,0},{7,1},{8,14},{9,15},{10,... | collective-permute-start | bytes 294920 | tf_op jit(solution)/shard_map/ppermute | solution.py:208
  10.0 3.4 %collective-permute-start.1 = (bf16[32,2560]{1,0:T(8,128)(2,1)S(1)}, bf16[32,2560]{1,0:T(8,128)(2,1)S(1)}, u32[]{:S(2)}, u32[]{:S(2)}) collective-permute-start(bf16[32,2560]{1,0:T(8,128)(2,1)S(1)} %collective-permute-done), channel_id=1, source_target_pairs={{0,16},{1,17},{2,18},{3,19},{4,20},{5,21},{6,22},{7,23},{8,0},{9,1... | collective-permute-start | bytes 491528 | tf_op jit(solution)/shard_map/ppermute | solution.py:216
  13.6 3.5 %collective-permute-done.2 = bf16[32,2560]{1,0:T(8,128)(2,1)S(1)} collective-permute-done((bf16[32,2560]{1,0:T(8,128)(2,1)S(1)}, bf16[32,2560]{1,0:T(8,128)(2,1)S(1)}, u32[]{:S(2)}, u32[]{:S(2)}) %collective-permute-start.2) | collective-permute-done | bytes 163872 | tf_op jit(solution)/shard_map/ppermute | solution.py:216
  21.4 9.3 %collective-permute-done.7 = bf16[128,1536]{1,0:T(8,128)(2,1)S(1)} collective-permute-done((bf16[128,1536]{1,0:T(8,128)(2,1)S(1)}, bf16[128,1536]{1,0:T(8,128)(2,1)S(1)}, u32[]{:S(2)}, u32[]{:S(2)}) %collective-permute-start.7) | collective-permute-done | bytes 393248 | tf_op jit(solution)/shard_map/ppermute | solution.py:216
  32.4 10.0 %collective-permute-done.9 = bf16[128,1536]{1,0:T(8,128)(2,1)S(1)} collective-permute-done((bf16[128,1536]{1,0:T(8,128)(2,1)S(1)}, bf16[128,1536]{1,0:T(8,128)(2,1)S(1)}, u32[]{:S(2)}, u32[]{:S(2)}) %collective-permute-start.9) | collective-permute-done | bytes 393248 | tf_op jit(solution)/shard_map/ppermute | solution.py:216
  44.0 9.0 %collective-permute-done.11 = bf16[128,1536]{1,0:T(8,128)(2,1)S(1)} collective-permute-done((bf16[128,1536]{1,0:T(8,128)(2,1)S(1)}, bf16[128,1536]{1,0:T(8,128)(2,1)S(1)}, u32[]{:S(2)}, u32[]{:S(2)}) %collective-permute-start.11) | collective-permute-done | bytes 393248 | tf_op jit(solution)/shard_map/ppermute | solution.py:216
  53.4 12.9 %convolution_convert_fusion.1 = bf16[512,1792]{1,0:T(8,128)(2,1)S(1)} fusion(bf16[4096,1792]{1,0:T(8,128)(2,1)} %param.7, bf16[512,1536]{1,0:T(8,128)(2,1)S(1)} %bitcast.140, bf16[128,2560]{1,0:T(8,128)(2,1)S(1)} %collective-permute-done.10, bf16[128,2560]{1,0:T(8,128)(2,1)S(1)} %collective-permute-done.8, ...), kind=kOutput, calls=%fused_computation.27 | convolution fusion | flops 7538081792 | bytes 20709376 | tf_op jit(solution)/shard_map/dot_general | solution.py:307
  66.4 13.0 %convolution_convert_fusion = bf16[512,1792]{1,0:T(8,128)(2,1)S(1)} fusion(bf16[4096,1792]{1,0:T(8,128)(2,1)} %param.8, bf16[512,1536]{1,0:T(8,128)(2,1)S(1)} %bitcast.141, bf16[128,2560]{1,0:T(8,128)(2,1)S(1)} %collective-permute-done.10, bf16[128,2560]{1,0:T(8,128)(2,1)S(1)} %collective-permute-done.8, bf16[128,2560]{1,0:T(8,128)(2,1)S(1)} %collective-permute-done.6, ...), kind=kOutput, calls=%fused_computation.26 | convolution fusion | flops 7538081792 | bytes 20709376 | tf_op jit(solution)/shard_map/dot_general | solution.py:308
  80.1 3.3 %collective-permute-done.13 = bf16[512,1792]{1,0:T(8,128)(2,1)S(1)} collective-permute-done((bf16[512,1792]{1,0:T(8,128)(2,1)S(1)}, bf16[512,1792]{1,0:T(8,128)(2,1)S(1)}, u32[]{:S(2)}, u32[]{:S(2)}) %collective-permute-start.13) | collective-permute-done | bytes 1835040 | tf_op jit(solution)/shard_map/ppermute | solution.py:301
  84.3 1.8 fusion.9
  92.4 8.4 %collective-permute-done.15 = bf16[128,1536]{1,0:T(8,128)(2,1)S(1)} collective-permute-done((bf16[128,1536]{1,0:T(8,128)(2,1)S(1)}, bf16[128,1536]{1,0:T(8,128)(2,1)S(1)}, u32[]{:S(2)}, u32[]{:S(2)}) %collective-permute-start.15) | collective-permute-done | bytes 393248 | tf_op jit(solution)/shard_map/ppermute | solution.py:216
  104.9 7.6 %collective-permute-done.17 = bf16[128,1536]{1,0:T(8,128)(2,1)S(1)} collective-permute-done((bf16[128,1536]{1,0:T(8,128)(2,1)S(1)}, bf16[128,1536]{1,0:T(8,128)(2,1)S(1)}, u32[]{:S(2)}, u32[]{:S(2)}) %collective-permute-start.17) | collective-permute-done | bytes 393248 | tf_op jit(solution)/shard_map/ppermute | solution.py:216
  113.4 2.0 collective-permute-start.19
  115.3 1.7 collective-permute-start.18
  119.5 4.2 %collective-permute-done.19 = bf16[128,1536]{1,0:T(8,128)(2,1)S(1)} collective-permute-done((bf16[128,1536]{1,0:T(8,128)(2,1)S(1)}, bf16[128,1536]{1,0:T(8,128)(2,1)S(1)}, u32[]{:S(2)}, u32[]{:S(2)}) %collective-permute-start.19) | collective-permute-done | bytes 393248 | tf_op jit(solution)/shard_map/ppermute | solution.py:216
  123.7 2.3 %collective-permute-done.18 = bf16[128,2560]{1,0:T(8,128)(2,1)S(1)} collective-permute-done((bf16[128,2560]{1,0:T(8,128)(2,1)S(1)}, bf16[128,2560]{1,0:T(8,128)(2,1)S(1)}, u32[]{:S(2)}, u32[]{:S(2)}) %collective-permute-start.18) | collective-permute-done | bytes 655392 | tf_op jit(solution)/shard_map/ppermute | solution.py:208
  129.2 1.6 collective-permute-start.21
  130.9 2.0 collective-permute-start.22
  133.8 1.7 collective-permute-done.22
  135.5 2.0 collective-permute-done.20
  137.5 4.6 %collective-permute-done.21 = bf16[32,2560]{1,0:T(8,128)(2,1)S(1)} collective-permute-done((bf16[32,2560]{1,0:T(8,128)(2,1)S(1)}, bf16[32,2560]{1,0:T(8,128)(2,1)S(1)}, u32[]{:S(2)}, u32[]{:S(2)}) %collective-permute-start.21) | collective-permute-done | bytes 163872 | tf_op jit(solution)/shard_map/ppermute | solution.py:216
  145.1 2.9 %collective-permute-start.27 = (bf16[32,2560]{1,0:T(8,128)(2,1)S(1)}, bf16[32,2560]{1,0:T(8,128)(2,1)S(1)}, u32[]{:S(2)}, u32[]{:S(2)}) collective-permute-start(bf16[32,2560]{1,0:T(8,128)(2,1)S(1)} %fusion.48), channel_id=1, source_target_pairs={{0,16},{1,17},{2,18},{3,19},{4,20},{5,21},{6,22},{7,23},{8,0},{9,1... | collective-permute-start | bytes 491528 | tf_op jit(solution)/shard_map/ppermute | solution.py:216
  150.0 2.6 %collective-permute-done.28 = bf16[32,1536]{1,0:T(8,128)(2,1)S(1)} collective-permute-done((bf16[32,1536]{1,0:T(8,128)(2,1)S(1)}, bf16[32,1536]{1,0:T(8,128)(2,1)S(1)}, u32[]{:S(2)}, u32[]{:S(2)}) %collective-permute-start.28) | collective-permute-done | bytes 98336 | tf_op jit(solution)/shard_map/ppermute | solution.py:208
  153.2 4.4 %collective-permute-done.29 = bf16[32,2560]{1,0:T(8,128)(2,1)S(1)} collective-permute-done((bf16[32,2560]{1,0:T(8,128)(2,1)S(1)}, bf16[32,2560]{1,0:T(8,128)(2,1)S(1)}, u32[]{:S(2)}, u32[]{:S(2)}) %collective-permute-start.29) | collective-permute-done | bytes 163872 | tf_op jit(solution)/shard_map/ppermute | solution.py:216
  157.8 1.8 collective-permute-start.32
  161.5 7.0 %collective-permute-done.33.refs_8_ = bf16[4,32,1536]{2,1,0:T(8,128)(2,1)S(1)} collective-permute-done((bf16[4,32,1536]{2,1,0:T(8,128)(2,1)S(1)}, bf16[4,32,1536]{2,1,0:T(8,128)(2,1)S(1)}, u32[]{:S(2)}, u32[]{:S(2)}) %collective-permute-start.33) | collective-permute-done | bytes 393248 | tf_op jit(solution)/shard_map/ppermute | solution.py:216
  172.6 7.9 %collective-permute-done.35.refs_9_ = bf16[4,32,1536]{2,1,0:T(8,128)(2,1)S(1)} collective-permute-done((bf16[4,32,1536]{2,1,0:T(8,128)(2,1)S(1)}, bf16[4,32,1536]{2,1,0:T(8,128)(2,1)S(1)}, u32[]{:S(2)}, u32[]{:S(2)}) %collective-permute-start.35) | collective-permute-done | bytes 393248 | tf_op jit(solution)/shard_map/ppermute | solution.py:216
  182.1 2.8 %collective-permute-start.36 = (bf16[4,32,2560]{2,1,0:T(8,128)(2,1)S(1)}, bf16[4,32,2560]{2,1,0:T(8,128)(2,1)S(1)}, u32[]{:S(2)}, u32[]{:S(2)}) collective-permute-start(bf16[4,32,2560]{2,1,0:T(8,128)(2,1)S(1)} %collective-permute-done.32.refs_4_), channel_id=1, source_target_pairs={{0,4},{1,3},{2,6},{3,1},{4,0},{5,7},{6,2},{7,5},{8,12},{9,11},{10,... | collective-permute-start | bytes 1966088 | tf_op jit(solution)/shard_map/ppermute | solution.py:208
  185.0 4.1 %collective-permute-done.37.refs_10_ = bf16[4,32,1536]{2,1,0:T(8,128)(2,1)S(1)} collective-permute-done((bf16[4,32,1536]{2,1,0:T(8,128)(2,1)S(1)}, bf16[4,32,1536]{2,1,0:T(8,128)(2,1)S(1)}, u32[]{:S(2)}, u32[]{:S(2)}) %collective-permute-start.37) | collective-permute-done | bytes 393248 | tf_op jit(solution)/shard_map/ppermute | solution.py:216
  189.1 4.5 %collective-permute-done.36.refs_6_ = bf16[4,32,2560]{2,1,0:T(8,128)(2,1)S(1)} collective-permute-done((bf16[4,32,2560]{2,1,0:T(8,128)(2,1)S(1)}, bf16[4,32,2560]{2,1,0:T(8,128)(2,1)S(1)}, u32[]{:S(2)}, u32[]{:S(2)}) %collective-permute-start.36) | collective-permute-done | bytes 655392 | tf_op jit(solution)/shard_map/ppermute | solution.py:208
  195.4 10.3 %shard_map.77 = f32[3,512,4096]{2,1,0:T(8,128)} custom-call(bf16[3,128,128]{2,1,0:T(8,128)(2,1)S(1)} %get-tuple-element.147.refs_0_, bf16[3,128,128]{2,1,0:T(8,128)(2,1)S(1)} %get-tuple-element.146.refs_1_, bf16[128,512]{1,0:T(8,128)(2,1)S(1)} %bitcast_select_fusion.refs_2_, bf16[4,32,2560]{2,1,0:T(8,128)(2,1)S(1)} %maximum_bitcast_fusion.1.refs_3_, ...), custom_call_target="tpu_custom_call" | custom-call | tf_op jit(solution)/shard_map/pallas_call | solution.py:260
  (122 shorter events, 45.4 us)
Async XLA Ops:
  1.8 8.3 %collective-permute-start = (bf16[32,2560]{1,0:T(8,128)(2,1)S(1)}, bf16[32,2560]{1,0:T(8,128)(2,1)S(1)}, u32[]{:S(2)}, u32[]{:S(2)}) collective-permute-start(bf16[32,2560]{1,0:T(8,128)(2,1)S(1)} %slice.216), channel_id=1, source_target_pairs={{0,16},{1,17},{2,18},{3,19},{4,20},{5,21},{6,22},{7,23},{8,0},{9,1... | collective-permute-start | bytes 491528 | tf_op jit(solution)/shard_map/ppermute | solution.py:216
  5.8 7.6 %collective-permute-start.5 = (bf16[32,1536]{1,0:T(8,128)(2,1)S(1)}, bf16[32,1536]{1,0:T(8,128)(2,1)S(1)}, u32[]{:S(2)}, u32[]{:S(2)}) collective-permute-start(bf16[32,1536]{1,0:T(8,128)(2,1)S(1)} %slice.217), channel_id=1, source_target_pairs={{0,6},{1,7},{2,4},{3,5},{4,2},{5,3},{6,0},{7,1},{8,14},{9,15},{10,... | collective-permute-start | bytes 294920 | tf_op jit(solution)/shard_map/ppermute | solution.py:208
  8.4 5.2 %collective-permute-start.4 = (bf16[32,1536]{1,0:T(8,128)(2,1)S(1)}, bf16[32,1536]{1,0:T(8,128)(2,1)S(1)}, u32[]{:S(2)}, u32[]{:S(2)}) collective-permute-start(bf16[32,1536]{1,0:T(8,128)(2,1)S(1)} %slice.217), channel_id=1, source_target_pairs={{0,4},{1,3},{2,6},{3,1},{4,0},{5,7},{6,2},{7,5},{8,12},{9,11},{10,... | collective-permute-start | bytes 294920 | tf_op jit(solution)/shard_map/ppermute | solution.py:208
  9.4 7.7 %collective-permute-start.2 = (bf16[32,2560]{1,0:T(8,128)(2,1)S(1)}, bf16[32,2560]{1,0:T(8,128)(2,1)S(1)}, u32[]{:S(2)}, u32[]{:S(2)}) collective-permute-start(bf16[32,2560]{1,0:T(8,128)(2,1)S(1)} %slice.216), channel_id=1, source_target_pairs={{0,8},{1,9},{2,10},{3,11},{4,12},{5,13},{6,14},{7,15},{8,24},{9,25... | collective-permute-start | bytes 491528 | tf_op jit(solution)/shard_map/ppermute | solution.py:216
  10.0 8.5 %collective-permute-start.1 = (bf16[32,2560]{1,0:T(8,128)(2,1)S(1)}, bf16[32,2560]{1,0:T(8,128)(2,1)S(1)}, u32[]{:S(2)}, u32[]{:S(2)}) collective-permute-start(bf16[32,2560]{1,0:T(8,128)(2,1)S(1)} %collective-permute-done), channel_id=1, source_target_pairs={{0,16},{1,17},{2,18},{3,19},{4,20},{5,21},{6,22},{7,23},{8,0},{9,1... | collective-permute-start | bytes 491528 | tf_op jit(solution)/shard_map/ppermute | solution.py:216
  18.6 12.1 %collective-permute-start.6 = (bf16[128,2560]{1,0:T(8,128)(2,1)S(1)}, bf16[128,2560]{1,0:T(8,128)(2,1)S(1)}, u32[]{:S(2)}, u32[]{:S(2)}) collective-permute-start(bf16[128,2560]{1,0:T(8,128)(2,1)S(1)} %pad_maximum_fusion.3), channel_id=1, source_target_pairs={{0,2},{1,5},{2,0},{3,7},{4,6},{5,1},{6,4},{7,3},{8,10},{9,13},{10,... | collective-permute-start | bytes 1966088 | tf_op jit(solution)/shard_map/ppermute | solution.py:208
  20.1 10.5 %collective-permute-start.7 = (bf16[128,1536]{1,0:T(8,128)(2,1)S(1)}, bf16[128,1536]{1,0:T(8,128)(2,1)S(1)}, u32[]{:S(2)}, u32[]{:S(2)}) collective-permute-start(bf16[128,1536]{1,0:T(8,128)(2,1)S(1)} %pad_maximum_fusion.4), channel_id=1, source_target_pairs={{0,16},{1,17},{2,18},{3,19},{4,20},{5,21},{6,22},{7,23},{8,0},{9,1... | collective-permute-start | bytes 1179656 | tf_op jit(solution)/shard_map/ppermute | solution.py:216
  30.6 11.8 %collective-permute-start.8 = (bf16[128,2560]{1,0:T(8,128)(2,1)S(1)}, bf16[128,2560]{1,0:T(8,128)(2,1)S(1)}, u32[]{:S(2)}, u32[]{:S(2)}) collective-permute-start(bf16[128,2560]{1,0:T(8,128)(2,1)S(1)} %pad_maximum_fusion.3), channel_id=1, source_target_pairs={{0,4},{1,3},{2,6},{3,1},{4,0},{5,7},{6,2},{7,5},{8,12},{9,11},{10,... | collective-permute-start | bytes 1966088 | tf_op jit(solution)/shard_map/ppermute | solution.py:208
  31.2 11.3 %collective-permute-start.9 = (bf16[128,1536]{1,0:T(8,128)(2,1)S(1)}, bf16[128,1536]{1,0:T(8,128)(2,1)S(1)}, u32[]{:S(2)}, u32[]{:S(2)}) collective-permute-start(bf16[128,1536]{1,0:T(8,128)(2,1)S(1)} %collective-permute-done.7), channel_id=1, source_target_pairs={{0,16},{1,17},{2,18},{3,19},{4,20},{5,21},{6,22},{7,23},{8,0},{9,1... | collective-permute-start | bytes 1179656 | tf_op jit(solution)/shard_map/ppermute | solution.py:216
  42.5 10.6 %collective-permute-start.10 = (bf16[128,2560]{1,0:T(8,128)(2,1)S(1)}, bf16[128,2560]{1,0:T(8,128)(2,1)S(1)}, u32[]{:S(2)}, u32[]{:S(2)}) collective-permute-start(bf16[128,2560]{1,0:T(8,128)(2,1)S(1)} %collective-permute-done.6), channel_id=1, source_target_pairs={{0,4},{1,3},{2,6},{3,1},{4,0},{5,7},{6,2},{7,5},{8,12},{9,11},{10,... | collective-permute-start | bytes 1966088 | tf_op jit(solution)/shard_map/ppermute | solution.py:208
  42.5 10.5 %collective-permute-start.11 = (bf16[128,1536]{1,0:T(8,128)(2,1)S(1)}, bf16[128,1536]{1,0:T(8,128)(2,1)S(1)}, u32[]{:S(2)}, u32[]{:S(2)}) collective-permute-start(bf16[128,1536]{1,0:T(8,128)(2,1)S(1)} %collective-permute-done.9), channel_id=1, source_target_pairs={{0,16},{1,17},{2,18},{3,19},{4,20},{5,21},{6,22},{7,23},{8,0},{9,1... | collective-permute-start | bytes 1179656 | tf_op jit(solution)/shard_map/ppermute | solution.py:216
  66.3 13.7 %collective-permute-start.12 = (bf16[512,1792]{1,0:T(8,128)(2,1)S(1)}, bf16[512,1792]{1,0:T(8,128)(2,1)S(1)}, u32[]{:S(2)}, u32[]{:S(2)}) collective-permute-start(bf16[512,1792]{1,0:T(8,128)(2,1)S(1)} %convolution_convert_fusion.1), channel_id=1, source_target_pairs={{0,1},{1,0},{2,3},{3,2},{4,5},{5,4},{6,7},{7,6},{8,9},{9,8},{10,11... | collective-permute-start | bytes 5505032 | tf_op jit(solution)/shard_map/ppermute | solution.py:301
  88.5 12.3 %collective-permute-start.15 = (bf16[128,1536]{1,0:T(8,128)(2,1)S(1)}, bf16[128,1536]{1,0:T(8,128)(2,1)S(1)}, u32[]{:S(2)}, u32[]{:S(2)}) collective-permute-start(bf16[128,1536]{1,0:T(8,128)(2,1)S(1)} %fusion.30), channel_id=1, source_target_pairs={{0,8},{1,9},{2,10},{3,11},{4,12},{5,13},{6,14},{7,15},{8,24},{9,25... | collective-permute-start | bytes 1179656 | tf_op jit(solution)/shard_map/ppermute | solution.py:216
  90.0 10.8 %collective-permute-start.14 = (bf16[128,2560]{1,0:T(8,128)(2,1)S(1)}, bf16[128,2560]{1,0:T(8,128)(2,1)S(1)}, u32[]{:S(2)}, u32[]{:S(2)}) collective-permute-start(bf16[128,2560]{1,0:T(8,128)(2,1)S(1)} %fusion.10), channel_id=1, source_target_pairs={{0,4},{1,3},{2,6},{3,1},{4,0},{5,7},{6,2},{7,5},{8,12},{9,11},{10,... | collective-permute-start | bytes 1966088 | tf_op jit(solution)/shard_map/ppermute | solution.py:208
  101.0 11.5 %collective-permute-start.17 = (bf16[128,1536]{1,0:T(8,128)(2,1)S(1)}, bf16[128,1536]{1,0:T(8,128)(2,1)S(1)}, u32[]{:S(2)}, u32[]{:S(2)}) collective-permute-start(bf16[128,1536]{1,0:T(8,128)(2,1)S(1)} %add_convert_fusion.4), channel_id=1, source_target_pairs={{0,8},{1,9},{2,10},{3,11},{4,12},{5,13},{6,14},{7,15},{8,24},{9,25... | collective-permute-start | bytes 1179656 | tf_op jit(solution)/shard_map/ppermute | solution.py:216
  102.5 10.6 %collective-permute-start.16 = (bf16[128,2560]{1,0:T(8,128)(2,1)S(1)}, bf16[128,2560]{1,0:T(8,128)(2,1)S(1)}, u32[]{:S(2)}, u32[]{:S(2)}) collective-permute-start(bf16[128,2560]{1,0:T(8,128)(2,1)S(1)} %fusion.13), channel_id=1, source_target_pairs={{0,4},{1,3},{2,6},{3,1},{4,0},{5,7},{6,2},{7,5},{8,12},{9,11},{10,... | collective-permute-start | bytes 1966088 | tf_op jit(solution)/shard_map/ppermute | solution.py:208
  113.4 10.3 %collective-permute-start.19 = (bf16[128,1536]{1,0:T(8,128)(2,1)S(1)}, bf16[128,1536]{1,0:T(8,128)(2,1)S(1)}, u32[]{:S(2)}, u32[]{:S(2)}) collective-permute-start(bf16[128,1536]{1,0:T(8,128)(2,1)S(1)} %add_convert_fusion.3), channel_id=1, source_target_pairs={{0,8},{1,9},{2,10},{3,11},{4,12},{5,13},{6,14},{7,15},{8,24},{9,25... | collective-permute-start | bytes 1179656 | tf_op jit(solution)/shard_map/ppermute | solution.py:216
  115.3 10.6 %collective-permute-start.18 = (bf16[128,2560]{1,0:T(8,128)(2,1)S(1)}, bf16[128,2560]{1,0:T(8,128)(2,1)S(1)}, u32[]{:S(2)}, u32[]{:S(2)}) collective-permute-start(bf16[128,2560]{1,0:T(8,128)(2,1)S(1)} %add_convert_fusion.1), channel_id=1, source_target_pairs={{0,2},{1,5},{2,0},{3,7},{4,6},{5,1},{6,4},{7,3},{8,10},{9,13},{10,... | collective-permute-start | bytes 1966088 | tf_op jit(solution)/shard_map/ppermute | solution.py:208
  126.3 6.5 %collective-permute-start.24 = (bf16[32,1536]{1,0:T(8,128)(2,1)S(1)}, bf16[32,1536]{1,0:T(8,128)(2,1)S(1)}, u32[]{:S(2)}, u32[]{:S(2)}) collective-permute-start(bf16[32,1536]{1,0:T(8,128)(2,1)S(1)} %get-tuple-element.137), channel_id=1, source_target_pairs={{0,6},{1,7},{2,4},{3,5},{4,2},{5,3},{6,0},{7,1},{8,14},{9,15},{10,... | collective-permute-start | bytes 294920 | tf_op jit(solution)/shard_map/ppermute | solution.py:208
  127.6 9.9 %collective-permute-start.25 = (bf16[32,2560]{1,0:T(8,128)(2,1)S(1)}, bf16[32,2560]{1,0:T(8,128)(2,1)S(1)}, u32[]{:S(2)}, u32[]{:S(2)}) collective-permute-start(bf16[32,2560]{1,0:T(8,128)(2,1)S(1)} %get-tuple-element.134), channel_id=1, source_target_pairs={{0,24},{1,25},{2,26},{3,27},{4,28},{5,29},{6,30},{7,31},{8,16},{9,... | collective-permute-start | bytes 491528 | tf_op jit(solution)/shard_map/ppermute | solution.py:216
  128.8 8.7 %collective-permute-start.23 = (bf16[32,2560]{1,0:T(8,128)(2,1)S(1)}, bf16[32,2560]{1,0:T(8,128)(2,1)S(1)}, u32[]{:S(2)}, u32[]{:S(2)}) collective-permute-start(bf16[32,2560]{1,0:T(8,128)(2,1)S(1)} %get-tuple-element.135), channel_id=1, source_target_pairs={{0,16},{1,17},{2,18},{3,19},{4,20},{5,21},{6,22},{7,23},{8,0},{9,1... | collective-permute-start | bytes 491528 | tf_op jit(solution)/shard_map/ppermute | solution.py:216
  129.2 12.9 %collective-permute-start.21 = (bf16[32,2560]{1,0:T(8,128)(2,1)S(1)}, bf16[32,2560]{1,0:T(8,128)(2,1)S(1)}, u32[]{:S(2)}, u32[]{:S(2)}) collective-permute-start(bf16[32,2560]{1,0:T(8,128)(2,1)S(1)} %get-tuple-element.136), channel_id=1, source_target_pairs={{0,8},{1,9},{2,10},{3,11},{4,12},{5,13},{6,14},{7,15},{8,24},{9,25... | collective-permute-start | bytes 491528 | tf_op jit(solution)/shard_map/ppermute | solution.py:216
  142.3 6.3 %collective-permute-start.30 = (bf16[32,1536]{1,0:T(8,128)(2,1)S(1)}, bf16[32,1536]{1,0:T(8,128)(2,1)S(1)}, u32[]{:S(2)}, u32[]{:S(2)}) collective-permute-start(bf16[32,1536]{1,0:T(8,128)(2,1)S(1)} %fusion.51), channel_id=1, source_target_pairs={{0,6},{1,7},{2,4},{3,5},{4,2},{5,3},{6,0},{7,1},{8,14},{9,15},{10,... | collective-permute-start | bytes 294920 | tf_op jit(solution)/shard_map/ppermute | solution.py:208
  143.8 9.4 %collective-permute-start.31 = (bf16[32,2560]{1,0:T(8,128)(2,1)S(1)}, bf16[32,2560]{1,0:T(8,128)(2,1)S(1)}, u32[]{:S(2)}, u32[]{:S(2)}) collective-permute-start(bf16[32,2560]{1,0:T(8,128)(2,1)S(1)} %fusion.48), channel_id=1, source_target_pairs={{0,24},{1,25},{2,26},{3,27},{4,28},{5,29},{6,30},{7,31},{8,16},{9,... | collective-permute-start | bytes 491528 | tf_op jit(solution)/shard_map/ppermute | solution.py:216
  145.1 12.5 %collective-permute-start.29 = (bf16[32,2560]{1,0:T(8,128)(2,1)S(1)}, bf16[32,2560]{1,0:T(8,128)(2,1)S(1)}, u32[]{:S(2)}, u32[]{:S(2)}) collective-permute-start(bf16[32,2560]{1,0:T(8,128)(2,1)S(1)} %fusion.48), channel_id=1, source_target_pairs={{0,8},{1,9},{2,10},{3,11},{4,12},{5,13},{6,14},{7,15},{8,24},{9,25... | collective-permute-start | bytes 491528 | tf_op jit(solution)/shard_map/ppermute | solution.py:216
  145.1 12.5 %collective-permute-start.27 = (bf16[32,2560]{1,0:T(8,128)(2,1)S(1)}, bf16[32,2560]{1,0:T(8,128)(2,1)S(1)}, u32[]{:S(2)}, u32[]{:S(2)}) collective-permute-start(bf16[32,2560]{1,0:T(8,128)(2,1)S(1)} %fusion.48), channel_id=1, source_target_pairs={{0,16},{1,17},{2,18},{3,19},{4,20},{5,21},{6,22},{7,23},{8,0},{9,1... | collective-permute-start | bytes 491528 | tf_op jit(solution)/shard_map/ppermute | solution.py:216
  157.8 10.8 %collective-permute-start.32 = (bf16[4,32,2560]{2,1,0:T(8,128)(2,1)S(1)}, bf16[4,32,2560]{2,1,0:T(8,128)(2,1)S(1)}, u32[]{:S(2)}, u32[]{:S(2)}) collective-permute-start(bf16[4,32,2560]{2,1,0:T(8,128)(2,1)S(1)} %maximum_bitcast_fusion.1.refs_3_), channel_id=1, source_target_pairs={{0,2},{1,5},{2,0},{3,7},{4,6},{5,1},{6,4},{7,3},{8,10},{9,13},{10,... | collective-permute-start | bytes 1966088 | tf_op jit(solution)/shard_map/ppermute | solution.py:208
  159.5 9.0 %collective-permute-start.33 = (bf16[4,32,1536]{2,1,0:T(8,128)(2,1)S(1)}, bf16[4,32,1536]{2,1,0:T(8,128)(2,1)S(1)}, u32[]{:S(2)}, u32[]{:S(2)}) collective-permute-start(bf16[4,32,1536]{2,1,0:T(8,128)(2,1)S(1)} %maximum_bitcast_fusion.2.refs_7_), channel_id=1, source_target_pairs={{0,16},{1,17},{2,18},{3,19},{4,20},{5,21},{6,22},{7,23},{8,0},{9,1... | collective-permute-start | bytes 1179656 | tf_op jit(solution)/shard_map/ppermute | solution.py:216
  168.5 12.0 %collective-permute-start.34 = (bf16[4,32,2560]{2,1,0:T(8,128)(2,1)S(1)}, bf16[4,32,2560]{2,1,0:T(8,128)(2,1)S(1)}, u32[]{:S(2)}, u32[]{:S(2)}) collective-permute-start(bf16[4,32,2560]{2,1,0:T(8,128)(2,1)S(1)} %maximum_bitcast_fusion.1.refs_3_), channel_id=1, source_target_pairs={{0,4},{1,3},{2,6},{3,1},{4,0},{5,7},{6,2},{7,5},{8,12},{9,11},{10,... | collective-permute-start | bytes 1966088 | tf_op jit(solution)/shard_map/ppermute | solution.py:208
  171.1 9.4 %collective-permute-start.35 = (bf16[4,32,1536]{2,1,0:T(8,128)(2,1)S(1)}, bf16[4,32,1536]{2,1,0:T(8,128)(2,1)S(1)}, u32[]{:S(2)}, u32[]{:S(2)}) collective-permute-start(bf16[4,32,1536]{2,1,0:T(8,128)(2,1)S(1)} %collective-permute-done.33.refs_8_), channel_id=1, source_target_pairs={{0,16},{1,17},{2,18},{3,19},{4,20},{5,21},{6,22},{7,23},{8,0},{9,1... | collective-permute-start | bytes 1179656 | tf_op jit(solution)/shard_map/ppermute | solution.py:216
  180.5 8.5 %collective-permute-start.37 = (bf16[4,32,1536]{2,1,0:T(8,128)(2,1)S(1)}, bf16[4,32,1536]{2,1,0:T(8,128)(2,1)S(1)}, u32[]{:S(2)}, u32[]{:S(2)}) collective-permute-start(bf16[4,32,1536]{2,1,0:T(8,128)(2,1)S(1)} %collective-permute-done.35.refs_9_), channel_id=1, source_target_pairs={{0,16},{1,17},{2,18},{3,19},{4,20},{5,21},{6,22},{7,23},{8,0},{9,1... | collective-permute-start | bytes 1179656 | tf_op jit(solution)/shard_map/ppermute | solution.py:216
  182.1 11.4 %collective-permute-start.36 = (bf16[4,32,2560]{2,1,0:T(8,128)(2,1)S(1)}, bf16[4,32,2560]{2,1,0:T(8,128)(2,1)S(1)}, u32[]{:S(2)}, u32[]{:S(2)}) collective-permute-start(bf16[4,32,2560]{2,1,0:T(8,128)(2,1)S(1)} %collective-permute-done.32.refs_4_), channel_id=1, source_target_pairs={{0,4},{1,3},{2,6},{3,1},{4,0},{5,7},{6,2},{7,5},{8,12},{9,11},{10,... | collective-permute-start | bytes 1966088 | tf_op jit(solution)/shard_map/ppermute | solution.py:208
  (12 other events, 128.8 us)

commit v3 on v2

--- a/solution.py
+++ b/solution.py
@@ -230,6 +230,72 @@
     return sum(p.astype(F32) for p in parts).astype(BF16)
 
 
+def early_kernel(gate_weight, up_weight, x, gate, up):
+    gate[...] = jnp.dot(x[...], gate_weight[...], preferred_element_type=F32)
+    up[...] = jnp.dot(x[...], up_weight[...], preferred_element_type=F32)
+
+
+def late_kernel(gate_weight, up_weight, *refs):
+    mids, a3, b, (gate, up, x) = refs[:6], refs[6], refs[7:11], refs[11:]
+    block, cut = a3.shape
+    rows = block // 4
+
+    @pl.when(pl.program_id(0) == 0)
+    def _():
+        for p in range(4):
+            for i in range(4):
+                start = p * block + i * rows
+                x[start:start + rows, :] = b[i][p * rows:(p + 1) * rows, :]
+
+    for weight, mid, out in ((gate_weight, mids[::2], gate), (up_weight, mids[1::2], up)):
+        more = jnp.dot(x[...], weight[cut:, :], preferred_element_type=F32)
+        last = jnp.dot(a3[...], weight[:cut, :], preferred_element_type=F32)
+        start = 0
+        for part in [*mid, last]:
+            end = start + part.shape[0]
+            out[start:end, :] = (more[start:end] + part[...]).astype(BF16)
+            start = end
+
+
+TILE = 256
+
+
+def early_products(x, gate_weight, up_weight):
+    rows, cut = x.shape
+    hid = gate_weight.shape[1]
+    weight = pl.BlockSpec((cut, TILE), lambda n: (0, n))
+    out = pl.BlockSpec((rows, TILE), lambda n: (0, n))
+    return pl.pallas_call(
+        early_kernel,
+        grid=(hid // TILE,),
+        in_specs=[weight] * 2 + [pl.BlockSpec(memory_space=pltpu.VMEM)],
+        out_specs=[out] * 2,
+        out_shape=[jax.ShapeDtypeStruct((rows, hid), F32)] * 2,
+        compiler_params=pltpu.CompilerParams(
+            dimension_semantics=("arbitrary",), vmem_limit_bytes=7 << 20
+        ),
+    )(gate_weight, up_weight, x)
+
+
+def late_products(mids, a3, b, gate_weight, up_weight, first, count):
+    width = gate_weight.shape[0]
+    block = a3.shape[0]
+    weight = pl.BlockSpec((width, TILE), lambda n: (0, n + first))
+    mid = [pl.BlockSpec((m.shape[0], TILE), lambda n: (0, n + first)) for m in mids]
+    out = pl.BlockSpec((4 * block, TILE), lambda n: (0, n))
+    return pl.pallas_call(
+        late_kernel,
+        grid=(count,),
+        in_specs=[weight] * 2 + mid + [pl.BlockSpec(memory_space=pltpu.VMEM)] * 5,
+        out_specs=[out] * 2,
+        out_shape=[jax.ShapeDtypeStruct((4 * block, count * TILE), BF16)] * 2,
+        scratch_shapes=[pltpu.VMEM((4 * block, b[0].shape[1]), BF16)],
+        compiler_params=pltpu.CompilerParams(
+            dimension_semantics=("arbitrary",), vmem_limit_bytes=12 << 20
+        ),
+    )(gate_weight, up_weight, *mids, a3, *b)
+
+
 def cross_kernel(scaling, hot_a, hot_b, english, *refs):
     out, moved_a, moved_b = refs[8:]
     lang, step = pl.program_id(0), pl.program_id(1)
@@ -265,7 +331,7 @@
         out_shape=jax.ShapeDtypeStruct((langs, height, width), F32),
         scratch_shapes=[pltpu.VMEM((height, tokens), BF16)] * 2,
         compiler_params=pltpu.CompilerParams(
-            dimension_semantics=("arbitrary", "arbitrary"), vmem_limit_bytes=16 << 20
+            dimension_semantics=("arbitrary", "arbitrary"), vmem_limit_bytes=12 << 20
         ),
     )(hot_a, hot_b, english, *a, *b)
 
@@ -286,16 +352,19 @@
         net.plane(b, 1), net.z(a, 1), net.plane(b, 2), net.z(a, 3), net.plane(b, 3), None
     )
     a3 = net.z(a1, 1)
+    weights = [pltpu.with_memory_space_constraint(w, pltpu.HBM) for w in (gate_weight, up_weight)]
+    b0 = jnp.concatenate((b, b1, b2, b3), 0)
     a0 = jnp.concatenate((a, a1, a3, a2), 0)
-    b0 = jnp.concatenate((b, b1, b2, b3), 0)
     a0, b0 = lock((a0, b0))
-    a0, a1, b1 = lock((a0, net.plane(a0, 1), net.z(b0)))
-    a0, a1, a2, b2 = lock((a0, a1, net.plane(a0, 2), net.z(b1)))
-    a3, b3 = lock((net.plane(a1, 2), net.z(b2)))
-    a = jnp.concatenate((a0, a1, a2, a3), 0)
-    b = jnp.stack((b0, b1, b2, b3)).reshape(4, 4, rows, width - cut)
-    b = b.transpose(1, 0, 2, 3).reshape(-1, width - cut)
-    full = jnp.concatenate((a, b), 1)
+    a1, b1 = net.plane(a0, 1), net.z(b0)
+    mids = early_products(a0, *weights)
+    a0, a1, b1, mids = lock((a0, a1, b1, mids))
+    a2, b2 = net.plane(a0, 2), net.z(b1)
+    mids += early_products(a1, *weights)
+    a0, a1, a2, b2, mids = lock((a0, a1, a2, b2, mids))
+    a3, b3 = net.plane(a1, 2), net.z(b2)
+    mids += early_products(a2, *weights)
+    a3, b3, mids = lock((a3, b3, mids))
 
     def core(v):
         return lax.ppermute(v, "tok", [(0, 1), (1, 0)])
@@ -304,11 +373,17 @@
         v = v.reshape(4, -1, v.shape[-1])
         return jnp.stack((v[0], v[2], v[1], v[3])).reshape(-1, v.shape[-1])
 
-    gate = jnp.dot(full, gate_weight, preferred_element_type=F32).astype(BF16)
-    up = jnp.dot(full, up_weight, preferred_element_type=F32).astype(BF16)
-    gate = gate.astype(F32) + mirror(core(gate)).astype(F32)
-    up = up.astype(F32) + mirror(core(up)).astype(F32)
-    hidden = (jax.nn.silu(gate) * up).astype(BF16)
+    tiles = hid // TILE
+    early = tiles // 2 + 1
+    hidden = []
+    for first, count in ((0, early), (early, tiles - early)):
+        gate, up = late_products(
+            mids, a3, (b0, b1, b2, b3), *weights, first, count
+        )
+        gate = gate.astype(F32) + mirror(core(gate)).astype(F32)
+        up = up.astype(F32) + mirror(core(up)).astype(F32)
+        hidden.append((jax.nn.silu(gate) * up).astype(BF16))
+    hidden = jnp.concatenate(hidden, 1)
 
     def down_a(h, j):
         h = h[j * 4 * rows:(j + 1) * 4 * rows]
@@ -334,24 +409,23 @@
     p = total(p, s1, s2).reshape(4, rows, cut)
     q = total(q, r1).reshape(4, rows, width - cut)
     p, q = lock((p, q))
-    got = lock((
-        net.plane(q[1], 1), net.z(p[1], 1, True), net.plane(q[2], 2),
-        net.z(p[3], 3, True), net.plane(q[3], 3), net.z(p[2], 2, True),
+    r1, r2, r3, g1, g3, g2 = lock((
+        net.plane(q[1], 1), net.plane(q[2], 2), net.plane(q[3], 3),
+        net.z(p[1], 1, True), net.z(p[3], 3, True), net.z(p[2], 2, True),
     ))
-    p, q = lock((total(p[0], *got[1::2]), total(q[0], *got[::2])))
+    p, q = lock((total(p[0], g1, g2, g3), total(q[0], r1, r2, r3)))
 
     ffn_out = jnp.concatenate((p, q), 1).reshape(langs, own, width).transpose(1, 0, 2)
 
-    got = lock((
-        net.plane(q, 1), net.z(p, 1), net.plane(q, 2), net.z(p, 3), net.plane(q, 3), net.z(p, 2)
-    ))
+    r1, g1, r2, g3, r3 = net.plane(q, 1), net.z(p, 1), net.plane(q, 2), net.z(p, 3), net.plane(q, 3)
+    g2 = net.z(g1, 1)
 
     def join(*v):
         v = [x.reshape(langs, own, -1) for x in v]
         return jnp.stack(v, 1).reshape(langs, 4 * own, -1)
 
-    p0 = join(p, got[1], got[5], got[3])
-    q0 = join(q, got[0], got[2], got[4])
+    p0 = join(p, g1, g2, g3)
+    q0 = join(q, r1, r2, r3)
     p0, q0 = lock((p0, q0))
     p0, p1, q1 = lock((p0, net.plane(p0, 1), net.z(q0)))
     p0, p1, p2, q2 = lock((p0, p1, net.plane(p0, 2), net.z(q1)))

time: 206 us -> 196 us (0.951)
  Pallas kernels: 10.3 us -> 55.8 us
  waiting for transfers between devices: 100 us -> 69.7 us
  matrix products: 35.3 us -> 9.21 us
    pallas_call x0 -> x5, Pallas kernels: none -> 45.5 us  [the longest x3 28.1 us: early_products(): pl.pallas_call(early_kernel, grid=(hid // TILE,), in_specs=[weight] * 2 +...]
    ppermute x18, waiting for transfers between devices: 82 us -> 52.4 us  [z(): return lax.ppermute(x, ('feat', 'tok'), sorted(pairs))]
    dot_general x2 -> x0, matrix products: 25.9 us -> none  [the longest x1 13 us: on_small(): up = jnp.dot(full, up_weight, preferred_element_type=F32).astype(BF16)]
  transfers between devices with their start and end apart: 39 -> 41, of which waited for: 25 -> 23; matrix products, arithmetic and copies ran while one was open for 12% -> 6% of each run, Pallas kernels for 0% -> 19%
where the time goes in v3:
time: 196 us
  waiting for transfers between devices  69.7 us (36%)
  Pallas kernels  55.8 us (28%)
  starting transfers between devices  49.9 us (25%)
  matrix products  9.21 us (5%)
  other arithmetic  5.62 us (3%)
  local copies, waits for them, and re-layouts  4.32 us (2%)
    ppermute x18, waiting for transfers between devices, z(): return lax.ppermute(x, ('feat', 'tok'), sorted(pairs))  52.4 us
    pallas_call x3, Pallas kernels, early_products(): pl.pallas_call(early_kernel, grid=(hid // TILE,), in_specs=[weight] * 2 +...  28.1 us
    ppermute x18, starting transfers between devices, z(): return lax.ppermute(x, ('feat', 'tok'), sorted(pairs))  26.3 us
    ppermute x18, starting transfers between devices, plane(): return lax.ppermute(x, ('feat', 'tok'), pairs)  22.4 us
    pallas_call x2, Pallas kernels, late_products(): pl.pallas_call(late_kernel, grid=(count,), in_specs=[weight] * 2 + mid +...  17.4 us
    ppermute x18, waiting for transfers between devices, plane(): return lax.ppermute(x, ('feat', 'tok'), pairs)  14.4 us
    pallas_call x1, Pallas kernels, cross_products(): pl.pallas_call(lambda *refs: cross_kernel(scaling, *refs), grid=(langs, h...  10.3 us
    dot_general x4, matrix products, down_a(): jnp.dot(h, down_weight[:, :cut], preferred_element_type=F32).astype(BF16)  5.45 us
  transfers between devices with their start and end apart: 41, of which 23 were waited for; matrix products, arithmetic and copies ran while one was open for 6% of the time, Pallas kernels for 19%

profile of v3, /device:TPU:0, one launch (start us, length us, event | category | flops | bytes accessed | tf_op | source)
XLA Modules:
  0.0 195.7 jit_solution(2214153402905640454)
XLA Ops:
  1.8 4.1 %collective-permute-start = (bf16[32,2560]{1,0:T(8,128)(2,1)S(1)}, bf16[32,2560]{1,0:T(8,128)(2,1)S(1)}, u32[]{:S(2)}, u32[]{:S(2)}) collective-permute-start(bf16[32,2560]{1,0:T(8,128)(2,1)S(1)} %slice.280), channel_id=1, source_target_pairs={{0,16},{1,17},{2,18},{3,19},{4,20},{5,21},{6,22},{7,23},{8,0},{9,1... | collective-permute-start | bytes 491528 | tf_op jit(solution)/shard_map/ppermute | solution.py:216
  5.8 2.5 %collective-permute-start.5 = (bf16[32,1536]{1,0:T(8,128)(2,1)S(1)}, bf16[32,1536]{1,0:T(8,128)(2,1)S(1)}, u32[]{:S(2)}, u32[]{:S(2)}) collective-permute-start(bf16[32,1536]{1,0:T(8,128)(2,1)S(1)} %slice.281), channel_id=1, source_target_pairs={{0,6},{1,7},{2,4},{3,5},{4,2},{5,3},{6,0},{7,1},{8,14},{9,15},{10,... | collective-permute-start | bytes 294920 | tf_op jit(solution)/shard_map/ppermute | solution.py:208
  10.0 3.4 %collective-permute-start.1 = (bf16[32,2560]{1,0:T(8,128)(2,1)S(1)}, bf16[32,2560]{1,0:T(8,128)(2,1)S(1)}, u32[]{:S(2)}, u32[]{:S(2)}) collective-permute-start(bf16[32,2560]{1,0:T(8,128)(2,1)S(1)} %collective-permute-done), channel_id=1, source_target_pairs={{0,16},{1,17},{2,18},{3,19},{4,20},{5,21},{6,22},{7,23},{8,0},{9,1... | collective-permute-start | bytes 491528 | tf_op jit(solution)/shard_map/ppermute | solution.py:216
  13.6 3.5 %collective-permute-done.2 = bf16[32,2560]{1,0:T(8,128)(2,1)S(1)} collective-permute-done((bf16[32,2560]{1,0:T(8,128)(2,1)S(1)}, bf16[32,2560]{1,0:T(8,128)(2,1)S(1)}, u32[]{:S(2)}, u32[]{:S(2)}) %collective-permute-start.2) | collective-permute-done | bytes 163872 | tf_op jit(solution)/shard_map/ppermute | solution.py:216
  18.6 1.6 collective-permute-start.6
  21.4 9.4 %shard_map.77 = (f32[128,1792]{1,0:T(8,128)S(1)}, f32[128,1792]{1,0:T(8,128)S(1)}) custom-call(bf16[4096,1792]{1,0:T(8,128)(2,1)} %gate_weight.9, bf16[4096,1792]{1,0:T(8,128)(2,1)} %up_weight.9, bf16[128,2560]{1,0:T(8,128)(2,1)S(1)} %pad_maximum_fusion.5.x), custom_call_target="tpu_custom_call" | custom-call | tf_op jit(solution)/shard_map/pallas_call | solution.py:268
  30.8 1.6 collective-permute-start.8
  33.8 9.4 %shard_map.78 = (f32[128,1792]{1,0:T(8,128)S(1)}, f32[128,1792]{1,0:T(8,128)S(1)}) custom-call(bf16[4096,1792]{1,0:T(8,128)(2,1)} %gate_weight.9, bf16[4096,1792]{1,0:T(8,128)(2,1)} %up_weight.9, bf16[128,2560]{1,0:T(8,128)(2,1)S(1)} %collective-permute-done.6.x), custom_call_target="tpu_custom_call" | custom-call | tf_op jit(solution)/shard_map/pallas_call | solution.py:268
  43.8 1.5 collective-permute-start.11
  45.3 9.4 %shard_map.79 = (f32[128,1792]{1,0:T(8,128)S(1)}, f32[128,1792]{1,0:T(8,128)S(1)}) custom-call(bf16[4096,1792]{1,0:T(8,128)(2,1)} %gate_weight.9, bf16[4096,1792]{1,0:T(8,128)(2,1)} %up_weight.9, bf16[128,2560]{1,0:T(8,128)(2,1)S(1)} %collective-permute-done.8.x), custom_call_target="tpu_custom_call" | custom-call | tf_op jit(solution)/shard_map/pallas_call | solution.py:268
  54.7 7.4 %shard_map.81 = (bf16[512,768]{1,0:T(8,128)(2,1)S(1)}, bf16[512,768]{1,0:T(8,128)(2,1)S(1)}) custom-call(bf16[4096,1792]{1,0:T(8,128)(2,1)} %gate_weight.9, bf16[4096,1792]{1,0:T(8,128)(2,1)} %up_weight.9, f32[128,1792]{1,0:T(8,128)S(1)} %get-tuple-element.98.refs_0_, f32[128,1792]{1,0:T(8,128)S(1)} %get-tuple-element.99.refs_1_, ...), custom_call_target="tpu_custom_call" | custom-call | tf_op jit(solution)/shard_map/pallas_call | solution.py:286
  62.7 10.0 %shard_map.80 = (bf16[512,1024]{1,0:T(8,128)(2,1)S(1)}, bf16[512,1024]{1,0:T(8,128)(2,1)S(1)}) custom-call(bf16[4096,1792]{1,0:T(8,128)(2,1)} %gate_weight.9, bf16[4096,1792]{1,0:T(8,128)(2,1)} %up_weight.9, f32[128,1792]{1,0:T(8,128)S(1)} %get-tuple-element.98.refs_0_, f32[128,1792]{1,0:T(8,128)S(1)} %get-tuple-element.99.refs_1_, ...), custom_call_target="tpu_custom_call" | custom-call | tf_op jit(solution)/shard_map/pallas_call | solution.py:286
  85.5 7.7 %collective-permute-done.17 = bf16[128,1536]{1,0:T(8,128)(2,1)S(1)} collective-permute-done((bf16[128,1536]{1,0:T(8,128)(2,1)S(1)}, bf16[128,1536]{1,0:T(8,128)(2,1)S(1)}, u32[]{:S(2)}, u32[]{:S(2)}) %collective-permute-start.17) | collective-permute-done | bytes 393248 | tf_op jit(solution)/shard_map/ppermute | solution.py:216
  94.0 1.6 collective-permute-start.18
  97.9 6.8 %collective-permute-done.19 = bf16[128,1536]{1,0:T(8,128)(2,1)S(1)} collective-permute-done((bf16[128,1536]{1,0:T(8,128)(2,1)S(1)}, bf16[128,1536]{1,0:T(8,128)(2,1)S(1)}, u32[]{:S(2)}, u32[]{:S(2)}) %collective-permute-start.19) | collective-permute-done | bytes 393248 | tf_op jit(solution)/shard_map/ppermute | solution.py:216
  110.0 5.4 %collective-permute-done.21 = bf16[128,1536]{1,0:T(8,128)(2,1)S(1)} collective-permute-done((bf16[128,1536]{1,0:T(8,128)(2,1)S(1)}, bf16[128,1536]{1,0:T(8,128)(2,1)S(1)}, u32[]{:S(2)}, u32[]{:S(2)}) %collective-permute-start.21) | collective-permute-done | bytes 393248 | tf_op jit(solution)/shard_map/ppermute | solution.py:216
  115.3 1.6 collective-permute-done.20
  117.4 1.6 collective-permute-start.24
  119.1 2.4 %collective-permute-start.27 = (bf16[32,2560]{1,0:T(8,128)(2,1)S(1)}, bf16[32,2560]{1,0:T(8,128)(2,1)S(1)}, u32[]{:S(2)}, u32[]{:S(2)}) collective-permute-start(bf16[32,2560]{1,0:T(8,128)(2,1)S(1)} %get-tuple-element.172), channel_id=1, source_target_pairs={{0,24},{1,25},{2,26},{3,27},{4,28},{5,29},{6,30},{7,31},{8,16},{9,... | collective-permute-start | bytes 491528 | tf_op jit(solution)/shard_map/ppermute | solution.py:216
  125.5 2.6 %collective-permute-done.23 = bf16[32,1536]{1,0:T(8,128)(2,1)S(1)} collective-permute-done((bf16[32,1536]{1,0:T(8,128)(2,1)S(1)}, bf16[32,1536]{1,0:T(8,128)(2,1)S(1)}, u32[]{:S(2)}, u32[]{:S(2)}) %collective-permute-start.23) | collective-permute-done | bytes 98336 | tf_op jit(solution)/shard_map/ppermute | solution.py:208
  129.2 3.8 %collective-permute-done.25 = bf16[32,2560]{1,0:T(8,128)(2,1)S(1)} collective-permute-done((bf16[32,2560]{1,0:T(8,128)(2,1)S(1)}, bf16[32,2560]{1,0:T(8,128)(2,1)S(1)}, u32[]{:S(2)}, u32[]{:S(2)}) %collective-permute-start.25) | collective-permute-done | bytes 163872 | tf_op jit(solution)/shard_map/ppermute | solution.py:216
  136.8 1.9 collective-permute-start.30
  141.0 3.2 %collective-permute-done.30 = bf16[32,2560]{1,0:T(8,128)(2,1)S(1)} collective-permute-done((bf16[32,2560]{1,0:T(8,128)(2,1)S(1)}, bf16[32,2560]{1,0:T(8,128)(2,1)S(1)}, u32[]{:S(2)}, u32[]{:S(2)}) %collective-permute-start.30) | collective-permute-done | bytes 163872 | tf_op jit(solution)/shard_map/ppermute | solution.py:216
  144.1 1.6 collective-permute-done.29
  145.9 1.9 collective-permute-start.34
  150.2 5.3 %collective-permute-done.35.refs_8_ = bf16[4,32,1536]{2,1,0:T(8,128)(2,1)S(1)} collective-permute-done((bf16[4,32,1536]{2,1,0:T(8,128)(2,1)S(1)}, bf16[4,32,1536]{2,1,0:T(8,128)(2,1)S(1)}, u32[]{:S(2)}, u32[]{:S(2)}) %collective-permute-start.35) | collective-permute-done | bytes 393248 | tf_op jit(solution)/shard_map/ppermute | solution.py:216
  155.5 2.6 %collective-permute-done.34.refs_4_ = bf16[4,32,2560]{2,1,0:T(8,128)(2,1)S(1)} collective-permute-done((bf16[4,32,2560]{2,1,0:T(8,128)(2,1)S(1)}, bf16[4,32,2560]{2,1,0:T(8,128)(2,1)S(1)}, u32[]{:S(2)}, u32[]{:S(2)}) %collective-permute-start.34) | collective-permute-done | bytes 655392 | tf_op jit(solution)/shard_map/ppermute | solution.py:208
  162.2 8.2 %collective-permute-done.37.refs_9_ = bf16[4,32,1536]{2,1,0:T(8,128)(2,1)S(1)} collective-permute-done((bf16[4,32,1536]{2,1,0:T(8,128)(2,1)S(1)}, bf16[4,32,1536]{2,1,0:T(8,128)(2,1)S(1)}, u32[]{:S(2)}, u32[]{:S(2)}) %collective-permute-start.37) | collective-permute-done | bytes 393248 | tf_op jit(solution)/shard_map/ppermute | solution.py:216
  170.4 2.5 %collective-permute-start.39 = (bf16[4,32,1536]{2,1,0:T(8,128)(2,1)S(1)}, bf16[4,32,1536]{2,1,0:T(8,128)(2,1)S(1)}, u32[]{:S(2)}, u32[]{:S(2)}) collective-permute-start(bf16[4,32,1536]{2,1,0:T(8,128)(2,1)S(1)} %collective-permute-done.37.refs_9_), channel_id=1, source_target_pairs={{0,16},{1,17},{2,18},{3,19},{4,20},{5,21},{6,22},{7,23},{8,0},{9,1... | collective-permute-start | bytes 1179656 | tf_op jit(solution)/shard_map/ppermute | solution.py:216
  173.5 4.9 %collective-permute-done.39.refs_10_ = bf16[4,32,1536]{2,1,0:T(8,128)(2,1)S(1)} collective-permute-done((bf16[4,32,1536]{2,1,0:T(8,128)(2,1)S(1)}, bf16[4,32,1536]{2,1,0:T(8,128)(2,1)S(1)}, u32[]{:S(2)}, u32[]{:S(2)}) %collective-permute-start.39) | collective-permute-done | bytes 393248 | tf_op jit(solution)/shard_map/ppermute | solution.py:216
  178.4 5.1 %collective-permute-done.38.refs_6_ = bf16[4,32,2560]{2,1,0:T(8,128)(2,1)S(1)} collective-permute-done((bf16[4,32,2560]{2,1,0:T(8,128)(2,1)S(1)}, bf16[4,32,2560]{2,1,0:T(8,128)(2,1)S(1)}, u32[]{:S(2)}, u32[]{:S(2)}) %collective-permute-start.38) | collective-permute-done | bytes 655392 | tf_op jit(solution)/shard_map/ppermute | solution.py:208
  185.4 10.3 %shard_map.82 = f32[3,512,4096]{2,1,0:T(8,128)} custom-call(bf16[3,128,128]{2,1,0:T(8,128)(2,1)S(1)} %get-tuple-element.185.refs_0_, bf16[3,128,128]{2,1,0:T(8,128)(2,1)S(1)} %get-tuple-element.184.refs_1_, bf16[128,512]{1,0:T(8,128)(2,1)S(1)} %bitcast_select_fusion.refs_2_, bf16[4,32,2560]{2,1,0:T(8,128)(2,1)S(1)} %maximum_bitcast_fusion.refs_3_, ...), custom_call_target="tpu_custom_call" | custom-call | tf_op jit(solution)/shard_map/pallas_call | solution.py:326
  (132 shorter events, 49.9 us)
Async XLA Ops:
  1.8 8.3 %collective-permute-start = (bf16[32,2560]{1,0:T(8,128)(2,1)S(1)}, bf16[32,2560]{1,0:T(8,128)(2,1)S(1)}, u32[]{:S(2)}, u32[]{:S(2)}) collective-permute-start(bf16[32,2560]{1,0:T(8,128)(2,1)S(1)} %slice.280), channel_id=1, source_target_pairs={{0,16},{1,17},{2,18},{3,19},{4,20},{5,21},{6,22},{7,23},{8,0},{9,1... | collective-permute-start | bytes 491528 | tf_op jit(solution)/shard_map/ppermute | solution.py:216
  5.8 7.6 %collective-permute-start.5 = (bf16[32,1536]{1,0:T(8,128)(2,1)S(1)}, bf16[32,1536]{1,0:T(8,128)(2,1)S(1)}, u32[]{:S(2)}, u32[]{:S(2)}) collective-permute-start(bf16[32,1536]{1,0:T(8,128)(2,1)S(1)} %slice.281), channel_id=1, source_target_pairs={{0,6},{1,7},{2,4},{3,5},{4,2},{5,3},{6,0},{7,1},{8,14},{9,15},{10,... | collective-permute-start | bytes 294920 | tf_op jit(solution)/shard_map/ppermute | solution.py:208
  9.4 7.7 %collective-permute-start.2 = (bf16[32,2560]{1,0:T(8,128)(2,1)S(1)}, bf16[32,2560]{1,0:T(8,128)(2,1)S(1)}, u32[]{:S(2)}, u32[]{:S(2)}) collective-permute-start(bf16[32,2560]{1,0:T(8,128)(2,1)S(1)} %slice.280), channel_id=1, source_target_pairs={{0,8},{1,9},{2,10},{3,11},{4,12},{5,13},{6,14},{7,15},{8,24},{9,25... | collective-permute-start | bytes 491528 | tf_op jit(solution)/shard_map/ppermute | solution.py:216
  10.0 8.5 %collective-permute-start.1 = (bf16[32,2560]{1,0:T(8,128)(2,1)S(1)}, bf16[32,2560]{1,0:T(8,128)(2,1)S(1)}, u32[]{:S(2)}, u32[]{:S(2)}) collective-permute-start(bf16[32,2560]{1,0:T(8,128)(2,1)S(1)} %collective-permute-done), channel_id=1, source_target_pairs={{0,16},{1,17},{2,18},{3,19},{4,20},{5,21},{6,22},{7,23},{8,0},{9,1... | collective-permute-start | bytes 491528 | tf_op jit(solution)/shard_map/ppermute | solution.py:216
  18.6 12.2 %collective-permute-start.6 = (bf16[128,2560]{1,0:T(8,128)(2,1)S(1)}, bf16[128,2560]{1,0:T(8,128)(2,1)S(1)}, u32[]{:S(2)}, u32[]{:S(2)}) collective-permute-start(bf16[128,2560]{1,0:T(8,128)(2,1)S(1)} %pad_maximum_fusion.5.x), channel_id=1, source_target_pairs={{0,2},{1,5},{2,0},{3,7},{4,6},{5,1},{6,4},{7,3},{8,10},{9,13},{10,... | collective-permute-start | bytes 1966088 | tf_op jit(solution)/shard_map/ppermute | solution.py:208
  20.1 10.7 %collective-permute-start.7 = (bf16[128,1536]{1,0:T(8,128)(2,1)S(1)}, bf16[128,1536]{1,0:T(8,128)(2,1)S(1)}, u32[]{:S(2)}, u32[]{:S(2)}) collective-permute-start(bf16[128,1536]{1,0:T(8,128)(2,1)S(1)} %pad_maximum_fusion.6.refs_7_), channel_id=1, source_target_pairs={{0,16},{1,17},{2,18},{3,19},{4,20},{5,21},{6,22},{7,23},{8,0},{9,1... | collective-permute-start | bytes 1179656 | tf_op jit(solution)/shard_map/ppermute | solution.py:216
  30.8 12.4 %collective-permute-start.8 = (bf16[128,2560]{1,0:T(8,128)(2,1)S(1)}, bf16[128,2560]{1,0:T(8,128)(2,1)S(1)}, u32[]{:S(2)}, u32[]{:S(2)}) collective-permute-start(bf16[128,2560]{1,0:T(8,128)(2,1)S(1)} %pad_maximum_fusion.5.x), channel_id=1, source_target_pairs={{0,4},{1,3},{2,6},{3,1},{4,0},{5,7},{6,2},{7,5},{8,12},{9,11},{10,... | collective-permute-start | bytes 1966088 | tf_op jit(solution)/shard_map/ppermute | solution.py:208
  32.4 10.8 %collective-permute-start.9 = (bf16[128,1536]{1,0:T(8,128)(2,1)S(1)}, bf16[128,1536]{1,0:T(8,128)(2,1)S(1)}, u32[]{:S(2)}, u32[]{:S(2)}) collective-permute-start(bf16[128,1536]{1,0:T(8,128)(2,1)S(1)} %collective-permute-done.7.refs_8_), channel_id=1, source_target_pairs={{0,16},{1,17},{2,18},{3,19},{4,20},{5,21},{6,22},{7,23},{8,0},{9,1... | collective-permute-start | bytes 1179656 | tf_op jit(solution)/shard_map/ppermute | solution.py:216
  43.2 11.5 %collective-permute-start.10 = (bf16[128,2560]{1,0:T(8,128)(2,1)S(1)}, bf16[128,2560]{1,0:T(8,128)(2,1)S(1)}, u32[]{:S(2)}, u32[]{:S(2)}) collective-permute-start(bf16[128,2560]{1,0:T(8,128)(2,1)S(1)} %collective-permute-done.6.x), channel_id=1, source_target_pairs={{0,4},{1,3},{2,6},{3,1},{4,0},{5,7},{6,2},{7,5},{8,12},{9,11},{10,... | collective-permute-start | bytes 1966088 | tf_op jit(solution)/shard_map/ppermute | solution.py:208
  43.8 10.9 %collective-permute-start.11 = (bf16[128,1536]{1,0:T(8,128)(2,1)S(1)}, bf16[128,1536]{1,0:T(8,128)(2,1)S(1)}, u32[]{:S(2)}, u32[]{:S(2)}) collective-permute-start(bf16[128,1536]{1,0:T(8,128)(2,1)S(1)} %collective-permute-done.9.refs_9_), channel_id=1, source_target_pairs={{0,16},{1,17},{2,18},{3,19},{4,20},{5,21},{6,22},{7,23},{8,0},{9,1... | collective-permute-start | bytes 1179656 | tf_op jit(solution)/shard_map/ppermute | solution.py:216
  62.1 11.1 %collective-permute-start.14 = (bf16[512,768]{1,0:T(8,128)(2,1)S(1)}, bf16[512,768]{1,0:T(8,128)(2,1)S(1)}, u32[]{:S(2)}, u32[]{:S(2)}) collective-permute-start(bf16[512,768]{1,0:T(8,128)(2,1)S(1)} %get-tuple-element.108), channel_id=1, source_target_pairs={{0,1},{1,0},{2,3},{3,2},{4,5},{5,4},{6,7},{7,6},{8,9},{9,8},{10,11... | collective-permute-start | bytes 2359304 | tf_op jit(solution)/shard_map/ppermute | solution.py:370
  62.2 11.1 %collective-permute-start.15 = (bf16[512,768]{1,0:T(8,128)(2,1)S(1)}, bf16[512,768]{1,0:T(8,128)(2,1)S(1)}, u32[]{:S(2)}, u32[]{:S(2)}) collective-permute-start(bf16[512,768]{1,0:T(8,128)(2,1)S(1)} %get-tuple-element.109), channel_id=1, source_target_pairs={{0,1},{1,0},{2,3},{3,2},{4,5},{5,4},{6,7},{7,6},{8,9},{9,8},{10,11... | collective-permute-start | bytes 2359304 | tf_op jit(solution)/shard_map/ppermute | solution.py:370
  81.0 12.3 %collective-permute-start.17 = (bf16[128,1536]{1,0:T(8,128)(2,1)S(1)}, bf16[128,1536]{1,0:T(8,128)(2,1)S(1)}, u32[]{:S(2)}, u32[]{:S(2)}) collective-permute-start(bf16[128,1536]{1,0:T(8,128)(2,1)S(1)} %fusion.28), channel_id=1, source_target_pairs={{0,8},{1,9},{2,10},{3,11},{4,12},{5,13},{6,14},{7,15},{8,24},{9,25... | collective-permute-start | bytes 1179656 | tf_op jit(solution)/shard_map/ppermute | solution.py:216
  81.7 11.6 %collective-permute-start.16 = (bf16[128,2560]{1,0:T(8,128)(2,1)S(1)}, bf16[128,2560]{1,0:T(8,128)(2,1)S(1)}, u32[]{:S(2)}, u32[]{:S(2)}) collective-permute-start(bf16[128,2560]{1,0:T(8,128)(2,1)S(1)} %fusion.8), channel_id=1, source_target_pairs={{0,4},{1,3},{2,6},{3,1},{4,0},{5,7},{6,2},{7,5},{8,12},{9,11},{10,... | collective-permute-start | bytes 1966088 | tf_op jit(solution)/shard_map/ppermute | solution.py:208
  93.4 11.3 %collective-permute-start.19 = (bf16[128,1536]{1,0:T(8,128)(2,1)S(1)}, bf16[128,1536]{1,0:T(8,128)(2,1)S(1)}, u32[]{:S(2)}, u32[]{:S(2)}) collective-permute-start(bf16[128,1536]{1,0:T(8,128)(2,1)S(1)} %add_convert_fusion.4), channel_id=1, source_target_pairs={{0,8},{1,9},{2,10},{3,11},{4,12},{5,13},{6,14},{7,15},{8,24},{9,25... | collective-permute-start | bytes 1179656 | tf_op jit(solution)/shard_map/ppermute | solution.py:216
  94.0 10.7 %collective-permute-start.18 = (bf16[128,2560]{1,0:T(8,128)(2,1)S(1)}, bf16[128,2560]{1,0:T(8,128)(2,1)S(1)}, u32[]{:S(2)}, u32[]{:S(2)}) collective-permute-start(bf16[128,2560]{1,0:T(8,128)(2,1)S(1)} %fusion.11), channel_id=1, source_target_pairs={{0,4},{1,3},{2,6},{3,1},{4,0},{5,7},{6,2},{7,5},{8,12},{9,11},{10,... | collective-permute-start | bytes 1966088 | tf_op jit(solution)/shard_map/ppermute | solution.py:208
  105.0 10.4 %collective-permute-start.21 = (bf16[128,1536]{1,0:T(8,128)(2,1)S(1)}, bf16[128,1536]{1,0:T(8,128)(2,1)S(1)}, u32[]{:S(2)}, u32[]{:S(2)}) collective-permute-start(bf16[128,1536]{1,0:T(8,128)(2,1)S(1)} %add_convert_fusion.3), channel_id=1, source_target_pairs={{0,8},{1,9},{2,10},{3,11},{4,12},{5,13},{6,14},{7,15},{8,24},{9,25... | collective-permute-start | bytes 1179656 | tf_op jit(solution)/shard_map/ppermute | solution.py:216
  106.4 10.6 %collective-permute-start.20 = (bf16[128,2560]{1,0:T(8,128)(2,1)S(1)}, bf16[128,2560]{1,0:T(8,128)(2,1)S(1)}, u32[]{:S(2)}, u32[]{:S(2)}) collective-permute-start(bf16[128,2560]{1,0:T(8,128)(2,1)S(1)} %add_convert_fusion.1), channel_id=1, source_target_pairs={{0,2},{1,5},{2,0},{3,7},{4,6},{5,1},{6,4},{7,3},{8,10},{9,13},{10,... | collective-permute-start | bytes 1966088 | tf_op jit(solution)/shard_map/ppermute | solution.py:208
  117.4 7.2 %collective-permute-start.24 = (bf16[32,1536]{1,0:T(8,128)(2,1)S(1)}, bf16[32,1536]{1,0:T(8,128)(2,1)S(1)}, u32[]{:S(2)}, u32[]{:S(2)}) collective-permute-start(bf16[32,1536]{1,0:T(8,128)(2,1)S(1)} %get-tuple-element.175), channel_id=1, source_target_pairs={{0,6},{1,7},{2,4},{3,5},{4,2},{5,3},{6,0},{7,1},{8,14},{9,15},{10,... | collective-permute-start | bytes 294920 | tf_op jit(solution)/shard_map/ppermute | solution.py:208
  119.1 10.2 %collective-permute-start.27 = (bf16[32,2560]{1,0:T(8,128)(2,1)S(1)}, bf16[32,2560]{1,0:T(8,128)(2,1)S(1)}, u32[]{:S(2)}, u32[]{:S(2)}) collective-permute-start(bf16[32,2560]{1,0:T(8,128)(2,1)S(1)} %get-tuple-element.172), channel_id=1, source_target_pairs={{0,24},{1,25},{2,26},{3,27},{4,28},{5,29},{6,30},{7,31},{8,16},{9,... | collective-permute-start | bytes 491528 | tf_op jit(solution)/shard_map/ppermute | solution.py:216
  121.4 7.8 %collective-permute-start.26 = (bf16[32,2560]{1,0:T(8,128)(2,1)S(1)}, bf16[32,2560]{1,0:T(8,128)(2,1)S(1)}, u32[]{:S(2)}, u32[]{:S(2)}) collective-permute-start(bf16[32,2560]{1,0:T(8,128)(2,1)S(1)} %get-tuple-element.173), channel_id=1, source_target_pairs={{0,16},{1,17},{2,18},{3,19},{4,20},{5,21},{6,22},{7,23},{8,0},{9,1... | collective-permute-start | bytes 491528 | tf_op jit(solution)/shard_map/ppermute | solution.py:216
  122.0 11.1 %collective-permute-start.25 = (bf16[32,2560]{1,0:T(8,128)(2,1)S(1)}, bf16[32,2560]{1,0:T(8,128)(2,1)S(1)}, u32[]{:S(2)}, u32[]{:S(2)}) collective-permute-start(bf16[32,2560]{1,0:T(8,128)(2,1)S(1)} %get-tuple-element.174), channel_id=1, source_target_pairs={{0,8},{1,9},{2,10},{3,11},{4,12},{5,13},{6,14},{7,15},{8,24},{9,25... | collective-permute-start | bytes 491528 | tf_op jit(solution)/shard_map/ppermute | solution.py:216
  133.2 5.6 %collective-permute-start.28 = (bf16[32,2560]{1,0:T(8,128)(2,1)S(1)}, bf16[32,2560]{1,0:T(8,128)(2,1)S(1)}, u32[]{:S(2)}, u32[]{:S(2)}) collective-permute-start(bf16[32,2560]{1,0:T(8,128)(2,1)S(1)} %fusion.51), channel_id=1, source_target_pairs={{0,16},{1,17},{2,18},{3,19},{4,20},{5,21},{6,22},{7,23},{8,0},{9,1... | collective-permute-start | bytes 491528 | tf_op jit(solution)/shard_map/ppermute | solution.py:216
  133.3 6.5 %collective-permute-start.33 = (bf16[32,1536]{1,0:T(8,128)(2,1)S(1)}, bf16[32,1536]{1,0:T(8,128)(2,1)S(1)}, u32[]{:S(2)}, u32[]{:S(2)}) collective-permute-start(bf16[32,1536]{1,0:T(8,128)(2,1)S(1)} %fusion.54), channel_id=1, source_target_pairs={{0,6},{1,7},{2,4},{3,5},{4,2},{5,3},{6,0},{7,1},{8,14},{9,15},{10,... | collective-permute-start | bytes 294920 | tf_op jit(solution)/shard_map/ppermute | solution.py:208
  136.8 7.3 %collective-permute-start.30 = (bf16[32,2560]{1,0:T(8,128)(2,1)S(1)}, bf16[32,2560]{1,0:T(8,128)(2,1)S(1)}, u32[]{:S(2)}, u32[]{:S(2)}) collective-permute-start(bf16[32,2560]{1,0:T(8,128)(2,1)S(1)} %fusion.51), channel_id=1, source_target_pairs={{0,8},{1,9},{2,10},{3,11},{4,12},{5,13},{6,14},{7,15},{8,24},{9,25... | collective-permute-start | bytes 491528 | tf_op jit(solution)/shard_map/ppermute | solution.py:216
  138.8 7.0 %collective-permute-start.29 = (bf16[32,2560]{1,0:T(8,128)(2,1)S(1)}, bf16[32,2560]{1,0:T(8,128)(2,1)S(1)}, u32[]{:S(2)}, u32[]{:S(2)}) collective-permute-start(bf16[32,2560]{1,0:T(8,128)(2,1)S(1)} %collective-permute-done.28), channel_id=1, source_target_pairs={{0,16},{1,17},{2,18},{3,19},{4,20},{5,21},{6,22},{7,23},{8,0},{9,1... | collective-permute-start | bytes 491528 | tf_op jit(solution)/shard_map/ppermute | solution.py:216
  145.9 12.2 %collective-permute-start.34 = (bf16[4,32,2560]{2,1,0:T(8,128)(2,1)S(1)}, bf16[4,32,2560]{2,1,0:T(8,128)(2,1)S(1)}, u32[]{:S(2)}, u32[]{:S(2)}) collective-permute-start(bf16[4,32,2560]{2,1,0:T(8,128)(2,1)S(1)} %maximum_bitcast_fusion.refs_3_), channel_id=1, source_target_pairs={{0,2},{1,5},{2,0},{3,7},{4,6},{5,1},{6,4},{7,3},{8,10},{9,13},{10,... | collective-permute-start | bytes 1966088 | tf_op jit(solution)/shard_map/ppermute | solution.py:208
  147.8 7.8 %collective-permute-start.35 = (bf16[4,32,1536]{2,1,0:T(8,128)(2,1)S(1)}, bf16[4,32,1536]{2,1,0:T(8,128)(2,1)S(1)}, u32[]{:S(2)}, u32[]{:S(2)}) collective-permute-start(bf16[4,32,1536]{2,1,0:T(8,128)(2,1)S(1)} %maximum_bitcast_fusion.1.refs_7_), channel_id=1, source_target_pairs={{0,16},{1,17},{2,18},{3,19},{4,20},{5,21},{6,22},{7,23},{8,0},{9,1... | collective-permute-start | bytes 1179656 | tf_op jit(solution)/shard_map/ppermute | solution.py:216
  158.1 12.3 %collective-permute-start.36 = (bf16[4,32,2560]{2,1,0:T(8,128)(2,1)S(1)}, bf16[4,32,2560]{2,1,0:T(8,128)(2,1)S(1)}, u32[]{:S(2)}, u32[]{:S(2)}) collective-permute-start(bf16[4,32,2560]{2,1,0:T(8,128)(2,1)S(1)} %maximum_bitcast_fusion.refs_3_), channel_id=1, source_target_pairs={{0,4},{1,3},{2,6},{3,1},{4,0},{5,7},{6,2},{7,5},{8,12},{9,11},{10,... | collective-permute-start | bytes 1966088 | tf_op jit(solution)/shard_map/ppermute | solution.py:208
  160.6 9.8 %collective-permute-start.37 = (bf16[4,32,1536]{2,1,0:T(8,128)(2,1)S(1)}, bf16[4,32,1536]{2,1,0:T(8,128)(2,1)S(1)}, u32[]{:S(2)}, u32[]{:S(2)}) collective-permute-start(bf16[4,32,1536]{2,1,0:T(8,128)(2,1)S(1)} %collective-permute-done.35.refs_8_), channel_id=1, source_target_pairs={{0,16},{1,17},{2,18},{3,19},{4,20},{5,21},{6,22},{7,23},{8,0},{9,1... | collective-permute-start | bytes 1179656 | tf_op jit(solution)/shard_map/ppermute | solution.py:216
  170.4 8.0 %collective-permute-start.39 = (bf16[4,32,1536]{2,1,0:T(8,128)(2,1)S(1)}, bf16[4,32,1536]{2,1,0:T(8,128)(2,1)S(1)}, u32[]{:S(2)}, u32[]{:S(2)}) collective-permute-start(bf16[4,32,1536]{2,1,0:T(8,128)(2,1)S(1)} %collective-permute-done.37.refs_9_), channel_id=1, source_target_pairs={{0,16},{1,17},{2,18},{3,19},{4,20},{5,21},{6,22},{7,23},{8,0},{9,1... | collective-permute-start | bytes 1179656 | tf_op jit(solution)/shard_map/ppermute | solution.py:216
  172.9 10.7 %collective-permute-start.38 = (bf16[4,32,2560]{2,1,0:T(8,128)(2,1)S(1)}, bf16[4,32,2560]{2,1,0:T(8,128)(2,1)S(1)}, u32[]{:S(2)}, u32[]{:S(2)}) collective-permute-start(bf16[4,32,2560]{2,1,0:T(8,128)(2,1)S(1)} %collective-permute-done.34.refs_4_), channel_id=1, source_target_pairs={{0,4},{1,3},{2,6},{3,1},{4,0},{5,7},{6,2},{7,5},{8,12},{9,11},{10,... | collective-permute-start | bytes 1966088 | tf_op jit(solution)/shard_map/ppermute | solution.py:208
  (14 other events, 121.0 us)

commit v4 on v3

--- a/solution.py
+++ b/solution.py
@@ -374,7 +374,7 @@
         return jnp.stack((v[0], v[2], v[1], v[3])).reshape(-1, v.shape[-1])
 
     tiles = hid // TILE
-    early = tiles // 2 + 1
+    early = tiles // 2 + 2
     hidden = []
     for first, count in ((0, early), (early, tiles - early)):
         gate, up = late_products(

time: 196 us -> 199 us (1.015)
  starting transfers between devices: 49.9 us -> 51.9 us
    ppermute x18, starting transfers between devices: 26.3 us -> 28.3 us  [z(): return lax.ppermute(x, ('feat', 'tok'), sorted(pairs))]
  transfers between devices with their start and end apart: 41 -> 41, of which waited for: 23 -> 22; matrix products, arithmetic and copies ran while one was open for 6% -> 6% of each run, Pallas kernels for 19% -> 20%
where the time goes in v4:
time: 199 us; the launch traced here: 198 us
  waiting for transfers between devices  70.3 us (35%)
  Pallas kernels  55.9 us (28%)
  starting transfers between devices  51.9 us (26%)
  matrix products  9.2 us (5%)
  other arithmetic  5.44 us (3%)
  local copies, waits for them, and re-layouts  4.32 us (2%)
    ppermute x18, waiting for transfers between devices, z(): return lax.ppermute(x, ('feat', 'tok'), sorted(pairs))  52.9 us
    ppermute x18, starting transfers between devices, z(): return lax.ppermute(x, ('feat', 'tok'), sorted(pairs))  28.3 us
    pallas_call x3, Pallas kernels, early_products(): pl.pallas_call(early_kernel, grid=(hid // TILE,), in_specs=[weight] * 2 +...  28.1 us
    ppermute x18, starting transfers between devices, plane(): return lax.ppermute(x, ('feat', 'tok'), pairs)  22.3 us
    pallas_call x2, Pallas kernels, late_products(): pl.pallas_call(late_kernel, grid=(count,), in_specs=[weight] * 2 + mid +...  17.5 us
    ppermute x18, waiting for transfers between devices, plane(): return lax.ppermute(x, ('feat', 'tok'), pairs)  13.1 us
    pallas_call x1, Pallas kernels, cross_products(): pl.pallas_call(lambda *refs: cross_kernel(scaling, *refs), grid=(langs, h...  10.3 us
    dot_general x4, matrix products, down_a(): jnp.dot(h, down_weight[:, :cut], preferred_element_type=F32).astype(BF16)  5.44 us
  transfers between devices with their start and end apart: 41, of which 22 were waited for; matrix products, arithmetic and copies ran while one was open for 6% of the time, Pallas kernels for 20%

profile of v4, /device:TPU:0, one launch (start us, length us, event | category | flops | bytes accessed | tf_op | source)
XLA Modules:
  0.0 198.3 jit_solution(7609739347214583200)
XLA Ops:
  1.8 4.1 %collective-permute-start = (bf16[32,2560]{1,0:T(8,128)(2,1)S(1)}, bf16[32,2560]{1,0:T(8,128)(2,1)S(1)}, u32[]{:S(2)}, u32[]{:S(2)}) collective-permute-start(bf16[32,2560]{1,0:T(8,128)(2,1)S(1)} %slice.280), channel_id=1, source_target_pairs={{0,16},{1,17},{2,18},{3,19},{4,20},{5,21},{6,22},{7,23},{8,0},{9,1... | collective-permute-start | bytes 491528 | tf_op jit(solution)/shard_map/ppermute | solution.py:216
  5.8 2.5 %collective-permute-start.5 = (bf16[32,1536]{1,0:T(8,128)(2,1)S(1)}, bf16[32,1536]{1,0:T(8,128)(2,1)S(1)}, u32[]{:S(2)}, u32[]{:S(2)}) collective-permute-start(bf16[32,1536]{1,0:T(8,128)(2,1)S(1)} %slice.281), channel_id=1, source_target_pairs={{0,6},{1,7},{2,4},{3,5},{4,2},{5,3},{6,0},{7,1},{8,14},{9,15},{10,... | collective-permute-start | bytes 294920 | tf_op jit(solution)/shard_map/ppermute | solution.py:208
  10.0 3.4 %collective-permute-start.1 = (bf16[32,2560]{1,0:T(8,128)(2,1)S(1)}, bf16[32,2560]{1,0:T(8,128)(2,1)S(1)}, u32[]{:S(2)}, u32[]{:S(2)}) collective-permute-start(bf16[32,2560]{1,0:T(8,128)(2,1)S(1)} %collective-permute-done), channel_id=1, source_target_pairs={{0,16},{1,17},{2,18},{3,19},{4,20},{5,21},{6,22},{7,23},{8,0},{9,1... | collective-permute-start | bytes 491528 | tf_op jit(solution)/shard_map/ppermute | solution.py:216
  13.6 3.5 %collective-permute-done.2 = bf16[32,2560]{1,0:T(8,128)(2,1)S(1)} collective-permute-done((bf16[32,2560]{1,0:T(8,128)(2,1)S(1)}, bf16[32,2560]{1,0:T(8,128)(2,1)S(1)}, u32[]{:S(2)}, u32[]{:S(2)}) %collective-permute-start.2) | collective-permute-done | bytes 163872 | tf_op jit(solution)/shard_map/ppermute | solution.py:216
  18.6 1.6 collective-permute-start.6
  21.4 9.4 %shard_map.77 = (f32[128,1792]{1,0:T(8,128)S(1)}, f32[128,1792]{1,0:T(8,128)S(1)}) custom-call(bf16[4096,1792]{1,0:T(8,128)(2,1)} %gate_weight.9, bf16[4096,1792]{1,0:T(8,128)(2,1)} %up_weight.9, bf16[128,2560]{1,0:T(8,128)(2,1)S(1)} %pad_maximum_fusion.3.x), custom_call_target="tpu_custom_call" | custom-call | tf_op jit(solution)/shard_map/pallas_call | solution.py:268
  30.8 1.6 collective-permute-start.8
  33.8 9.4 %shard_map.78 = (f32[128,1792]{1,0:T(8,128)S(1)}, f32[128,1792]{1,0:T(8,128)S(1)}) custom-call(bf16[4096,1792]{1,0:T(8,128)(2,1)} %gate_weight.9, bf16[4096,1792]{1,0:T(8,128)(2,1)} %up_weight.9, bf16[128,2560]{1,0:T(8,128)(2,1)S(1)} %collective-permute-done.6.x), custom_call_target="tpu_custom_call" | custom-call | tf_op jit(solution)/shard_map/pallas_call | solution.py:268
  45.3 9.4 %shard_map.79 = (f32[128,1792]{1,0:T(8,128)S(1)}, f32[128,1792]{1,0:T(8,128)S(1)}) custom-call(bf16[4096,1792]{1,0:T(8,128)(2,1)} %gate_weight.9, bf16[4096,1792]{1,0:T(8,128)(2,1)} %up_weight.9, bf16[128,2560]{1,0:T(8,128)(2,1)S(1)} %collective-permute-done.8.x), custom_call_target="tpu_custom_call" | custom-call | tf_op jit(solution)/shard_map/pallas_call | solution.py:268
  54.7 5.2 %shard_map.81 = (bf16[512,512]{1,0:T(8,128)(2,1)S(1)}, bf16[512,512]{1,0:T(8,128)(2,1)S(1)}) custom-call(bf16[4096,1792]{1,0:T(8,128)(2,1)} %gate_weight.9, bf16[4096,1792]{1,0:T(8,128)(2,1)} %up_weight.9, f32[128,1792]{1,0:T(8,128)S(1)} %get-tuple-element.98.refs_0_, f32[128,1792]{1,0:T(8,128)S(1)} %get-tuple-element.99.refs_1_, ...), custom_call_target="tpu_custom_call" | custom-call | tf_op jit(solution)/shard_map/pallas_call | solution.py:286
  60.0 12.4 %shard_map.80 = (bf16[512,1280]{1,0:T(8,128)(2,1)S(1)}, bf16[512,1280]{1,0:T(8,128)(2,1)S(1)}) custom-call(bf16[4096,1792]{1,0:T(8,128)(2,1)} %gate_weight.9, bf16[4096,1792]{1,0:T(8,128)(2,1)} %up_weight.9, f32[128,1792]{1,0:T(8,128)S(1)} %get-tuple-element.98.refs_0_, f32[128,1792]{1,0:T(8,128)S(1)} %get-tuple-element.99.refs_1_, ...), custom_call_target="tpu_custom_call" | custom-call | tf_op jit(solution)/shard_map/pallas_call | solution.py:286
  73.5 2.9 %collective-permute-done.15 = bf16[512,512]{1,0:T(8,128)(2,1)S(1)} collective-permute-done((bf16[512,512]{1,0:T(8,128)(2,1)S(1)}, bf16[512,512]{1,0:T(8,128)(2,1)S(1)}, u32[]{:S(2)}, u32[]{:S(2)}) %collective-permute-start.15) | collective-permute-done | bytes 524320 | tf_op jit(solution)/shard_map/ppermute | solution.py:370
  87.0 8.0 %collective-permute-done.17 = bf16[128,1536]{1,0:T(8,128)(2,1)S(1)} collective-permute-done((bf16[128,1536]{1,0:T(8,128)(2,1)S(1)}, bf16[128,1536]{1,0:T(8,128)(2,1)S(1)}, u32[]{:S(2)}, u32[]{:S(2)}) %collective-permute-start.17) | collective-permute-done | bytes 393248 | tf_op jit(solution)/shard_map/ppermute | solution.py:216
  99.4 7.2 %collective-permute-done.19 = bf16[128,1536]{1,0:T(8,128)(2,1)S(1)} collective-permute-done((bf16[128,1536]{1,0:T(8,128)(2,1)S(1)}, bf16[128,1536]{1,0:T(8,128)(2,1)S(1)}, u32[]{:S(2)}, u32[]{:S(2)}) %collective-permute-start.19) | collective-permute-done | bytes 393248 | tf_op jit(solution)/shard_map/ppermute | solution.py:216
  111.7 5.9 %collective-permute-done.21 = bf16[128,1536]{1,0:T(8,128)(2,1)S(1)} collective-permute-done((bf16[128,1536]{1,0:T(8,128)(2,1)S(1)}, bf16[128,1536]{1,0:T(8,128)(2,1)S(1)}, u32[]{:S(2)}, u32[]{:S(2)}) %collective-permute-start.21) | collective-permute-done | bytes 393248 | tf_op jit(solution)/shard_map/ppermute | solution.py:216
  119.1 1.6 collective-permute-start.24
  120.8 2.4 %collective-permute-start.27 = (bf16[32,2560]{1,0:T(8,128)(2,1)S(1)}, bf16[32,2560]{1,0:T(8,128)(2,1)S(1)}, u32[]{:S(2)}, u32[]{:S(2)}) collective-permute-start(bf16[32,2560]{1,0:T(8,128)(2,1)S(1)} %get-tuple-element.164), channel_id=1, source_target_pairs={{0,24},{1,25},{2,26},{3,27},{4,28},{5,29},{6,30},{7,31},{8,16},{9,... | collective-permute-start | bytes 491528 | tf_op jit(solution)/shard_map/ppermute | solution.py:216
  123.5 1.7 collective-permute-start.25
  127.2 2.6 %collective-permute-done.23 = bf16[32,1536]{1,0:T(8,128)(2,1)S(1)} collective-permute-done((bf16[32,1536]{1,0:T(8,128)(2,1)S(1)}, bf16[32,1536]{1,0:T(8,128)(2,1)S(1)}, u32[]{:S(2)}, u32[]{:S(2)}) %collective-permute-start.23) | collective-permute-done | bytes 98336 | tf_op jit(solution)/shard_map/ppermute | solution.py:208
  131.0 4.1 %collective-permute-done.25 = bf16[32,2560]{1,0:T(8,128)(2,1)S(1)} collective-permute-done((bf16[32,2560]{1,0:T(8,128)(2,1)S(1)}, bf16[32,2560]{1,0:T(8,128)(2,1)S(1)}, u32[]{:S(2)}, u32[]{:S(2)}) %collective-permute-start.25) | collective-permute-done | bytes 163872 | tf_op jit(solution)/shard_map/ppermute | solution.py:216
  138.8 1.9 collective-permute-start.30
  140.8 2.0 %collective-permute-start.29 = (bf16[32,2560]{1,0:T(8,128)(2,1)S(1)}, bf16[32,2560]{1,0:T(8,128)(2,1)S(1)}, u32[]{:S(2)}, u32[]{:S(2)}) collective-permute-start(bf16[32,2560]{1,0:T(8,128)(2,1)S(1)} %collective-permute-done.28), channel_id=1, source_target_pairs={{0,16},{1,17},{2,18},{3,19},{4,20},{5,21},{6,22},{7,23},{8,0},{9,1... | collective-permute-start | bytes 491528 | tf_op jit(solution)/shard_map/ppermute | solution.py:216
  142.9 3.7 %collective-permute-done.30 = bf16[32,2560]{1,0:T(8,128)(2,1)S(1)} collective-permute-done((bf16[32,2560]{1,0:T(8,128)(2,1)S(1)}, bf16[32,2560]{1,0:T(8,128)(2,1)S(1)}, u32[]{:S(2)}, u32[]{:S(2)}) %collective-permute-start.30) | collective-permute-done | bytes 163872 | tf_op jit(solution)/shard_map/ppermute | solution.py:216
  147.9 1.9 collective-permute-start.34
  152.4 5.1 %collective-permute-done.35.refs_8_ = bf16[4,32,1536]{2,1,0:T(8,128)(2,1)S(1)} collective-permute-done((bf16[4,32,1536]{2,1,0:T(8,128)(2,1)S(1)}, bf16[4,32,1536]{2,1,0:T(8,128)(2,1)S(1)}, u32[]{:S(2)}, u32[]{:S(2)}) %collective-permute-start.35) | collective-permute-done | bytes 393248 | tf_op jit(solution)/shard_map/ppermute | solution.py:216
  157.5 2.6 %collective-permute-done.34.refs_4_ = bf16[4,32,2560]{2,1,0:T(8,128)(2,1)S(1)} collective-permute-done((bf16[4,32,2560]{2,1,0:T(8,128)(2,1)S(1)}, bf16[4,32,2560]{2,1,0:T(8,128)(2,1)S(1)}, u32[]{:S(2)}, u32[]{:S(2)}) %collective-permute-start.34) | collective-permute-done | bytes 655392 | tf_op jit(solution)/shard_map/ppermute | solution.py:208
  162.5 1.8 collective-permute-start.37
  164.6 7.6 %collective-permute-done.37.refs_9_ = bf16[4,32,1536]{2,1,0:T(8,128)(2,1)S(1)} collective-permute-done((bf16[4,32,1536]{2,1,0:T(8,128)(2,1)S(1)}, bf16[4,32,1536]{2,1,0:T(8,128)(2,1)S(1)}, u32[]{:S(2)}, u32[]{:S(2)}) %collective-permute-start.37) | collective-permute-done | bytes 393248 | tf_op jit(solution)/shard_map/ppermute | solution.py:216
  172.2 3.2 %collective-permute-start.39 = (bf16[4,32,1536]{2,1,0:T(8,128)(2,1)S(1)}, bf16[4,32,1536]{2,1,0:T(8,128)(2,1)S(1)}, u32[]{:S(2)}, u32[]{:S(2)}) collective-permute-start(bf16[4,32,1536]{2,1,0:T(8,128)(2,1)S(1)} %collective-permute-done.37.refs_9_), channel_id=1, source_target_pairs={{0,16},{1,17},{2,18},{3,19},{4,20},{5,21},{6,22},{7,23},{8,0},{9,1... | collective-permute-start | bytes 1179656 | tf_op jit(solution)/shard_map/ppermute | solution.py:216
  176.1 4.6 %collective-permute-done.39.refs_10_ = bf16[4,32,1536]{2,1,0:T(8,128)(2,1)S(1)} collective-permute-done((bf16[4,32,1536]{2,1,0:T(8,128)(2,1)S(1)}, bf16[4,32,1536]{2,1,0:T(8,128)(2,1)S(1)}, u32[]{:S(2)}, u32[]{:S(2)}) %collective-permute-start.39) | collective-permute-done | bytes 393248 | tf_op jit(solution)/shard_map/ppermute | solution.py:216
  180.7 5.4 %collective-permute-done.38.refs_6_ = bf16[4,32,2560]{2,1,0:T(8,128)(2,1)S(1)} collective-permute-done((bf16[4,32,2560]{2,1,0:T(8,128)(2,1)S(1)}, bf16[4,32,2560]{2,1,0:T(8,128)(2,1)S(1)}, u32[]{:S(2)}, u32[]{:S(2)}) %collective-permute-start.38) | collective-permute-done | bytes 655392 | tf_op jit(solution)/shard_map/ppermute | solution.py:208
  188.0 10.3 %shard_map.82 = f32[3,512,4096]{2,1,0:T(8,128)} custom-call(bf16[3,128,128]{2,1,0:T(8,128)(2,1)S(1)} %get-tuple-element.185.refs_0_, bf16[3,128,128]{2,1,0:T(8,128)(2,1)S(1)} %get-tuple-element.184.refs_1_, bf16[128,512]{1,0:T(8,128)(2,1)S(1)} %bitcast_select_fusion.refs_2_, bf16[4,32,2560]{2,1,0:T(8,128)(2,1)S(1)} %maximum_bitcast_fusion.refs_3_, ...), custom_call_target="tpu_custom_call" | custom-call | tf_op jit(solution)/shard_map/pallas_call | solution.py:326
  (132 shorter events, 48.4 us)
Async XLA Ops:
  1.8 8.3 %collective-permute-start = (bf16[32,2560]{1,0:T(8,128)(2,1)S(1)}, bf16[32,2560]{1,0:T(8,128)(2,1)S(1)}, u32[]{:S(2)}, u32[]{:S(2)}) collective-permute-start(bf16[32,2560]{1,0:T(8,128)(2,1)S(1)} %slice.280), channel_id=1, source_target_pairs={{0,16},{1,17},{2,18},{3,19},{4,20},{5,21},{6,22},{7,23},{8,0},{9,1... | collective-permute-start | bytes 491528 | tf_op jit(solution)/shard_map/ppermute | solution.py:216
  5.8 7.6 %collective-permute-start.5 = (bf16[32,1536]{1,0:T(8,128)(2,1)S(1)}, bf16[32,1536]{1,0:T(8,128)(2,1)S(1)}, u32[]{:S(2)}, u32[]{:S(2)}) collective-permute-start(bf16[32,1536]{1,0:T(8,128)(2,1)S(1)} %slice.281), channel_id=1, source_target_pairs={{0,6},{1,7},{2,4},{3,5},{4,2},{5,3},{6,0},{7,1},{8,14},{9,15},{10,... | collective-permute-start | bytes 294920 | tf_op jit(solution)/shard_map/ppermute | solution.py:208
  9.4 7.7 %collective-permute-start.2 = (bf16[32,2560]{1,0:T(8,128)(2,1)S(1)}, bf16[32,2560]{1,0:T(8,128)(2,1)S(1)}, u32[]{:S(2)}, u32[]{:S(2)}) collective-permute-start(bf16[32,2560]{1,0:T(8,128)(2,1)S(1)} %slice.280), channel_id=1, source_target_pairs={{0,8},{1,9},{2,10},{3,11},{4,12},{5,13},{6,14},{7,15},{8,24},{9,25... | collective-permute-start | bytes 491528 | tf_op jit(solution)/shard_map/ppermute | solution.py:216
  10.0 8.5 %collective-permute-start.1 = (bf16[32,2560]{1,0:T(8,128)(2,1)S(1)}, bf16[32,2560]{1,0:T(8,128)(2,1)S(1)}, u32[]{:S(2)}, u32[]{:S(2)}) collective-permute-start(bf16[32,2560]{1,0:T(8,128)(2,1)S(1)} %collective-permute-done), channel_id=1, source_target_pairs={{0,16},{1,17},{2,18},{3,19},{4,20},{5,21},{6,22},{7,23},{8,0},{9,1... | collective-permute-start | bytes 491528 | tf_op jit(solution)/shard_map/ppermute | solution.py:216
  18.6 12.2 %collective-permute-start.6 = (bf16[128,2560]{1,0:T(8,128)(2,1)S(1)}, bf16[128,2560]{1,0:T(8,128)(2,1)S(1)}, u32[]{:S(2)}, u32[]{:S(2)}) collective-permute-start(bf16[128,2560]{1,0:T(8,128)(2,1)S(1)} %pad_maximum_fusion.3.x), channel_id=1, source_target_pairs={{0,2},{1,5},{2,0},{3,7},{4,6},{5,1},{6,4},{7,3},{8,10},{9,13},{10,... | collective-permute-start | bytes 1966088 | tf_op jit(solution)/shard_map/ppermute | solution.py:208
  20.1 10.7 %collective-permute-start.7 = (bf16[128,1536]{1,0:T(8,128)(2,1)S(1)}, bf16[128,1536]{1,0:T(8,128)(2,1)S(1)}, u32[]{:S(2)}, u32[]{:S(2)}) collective-permute-start(bf16[128,1536]{1,0:T(8,128)(2,1)S(1)} %pad_maximum_fusion.6.refs_7_), channel_id=1, source_target_pairs={{0,16},{1,17},{2,18},{3,19},{4,20},{5,21},{6,22},{7,23},{8,0},{9,1... | collective-permute-start | bytes 1179656 | tf_op jit(solution)/shard_map/ppermute | solution.py:216
  30.8 12.4 %collective-permute-start.8 = (bf16[128,2560]{1,0:T(8,128)(2,1)S(1)}, bf16[128,2560]{1,0:T(8,128)(2,1)S(1)}, u32[]{:S(2)}, u32[]{:S(2)}) collective-permute-start(bf16[128,2560]{1,0:T(8,128)(2,1)S(1)} %pad_maximum_fusion.3.x), channel_id=1, source_target_pairs={{0,4},{1,3},{2,6},{3,1},{4,0},{5,7},{6,2},{7,5},{8,12},{9,11},{10,... | collective-permute-start | bytes 1966088 | tf_op jit(solution)/shard_map/ppermute | solution.py:208
  32.4 10.8 %collective-permute-start.9 = (bf16[128,1536]{1,0:T(8,128)(2,1)S(1)}, bf16[128,1536]{1,0:T(8,128)(2,1)S(1)}, u32[]{:S(2)}, u32[]{:S(2)}) collective-permute-start(bf16[128,1536]{1,0:T(8,128)(2,1)S(1)} %collective-permute-done.7.refs_8_), channel_id=1, source_target_pairs={{0,16},{1,17},{2,18},{3,19},{4,20},{5,21},{6,22},{7,23},{8,0},{9,1... | collective-permute-start | bytes 1179656 | tf_op jit(solution)/shard_map/ppermute | solution.py:216
  43.2 11.5 %collective-permute-start.10 = (bf16[128,2560]{1,0:T(8,128)(2,1)S(1)}, bf16[128,2560]{1,0:T(8,128)(2,1)S(1)}, u32[]{:S(2)}, u32[]{:S(2)}) collective-permute-start(bf16[128,2560]{1,0:T(8,128)(2,1)S(1)} %collective-permute-done.6.x), channel_id=1, source_target_pairs={{0,4},{1,3},{2,6},{3,1},{4,0},{5,7},{6,2},{7,5},{8,12},{9,11},{10,... | collective-permute-start | bytes 1966088 | tf_op jit(solution)/shard_map/ppermute | solution.py:208
  43.8 10.9 %collective-permute-start.11 = (bf16[128,1536]{1,0:T(8,128)(2,1)S(1)}, bf16[128,1536]{1,0:T(8,128)(2,1)S(1)}, u32[]{:S(2)}, u32[]{:S(2)}) collective-permute-start(bf16[128,1536]{1,0:T(8,128)(2,1)S(1)} %collective-permute-done.9.refs_9_), channel_id=1, source_target_pairs={{0,16},{1,17},{2,18},{3,19},{4,20},{5,21},{6,22},{7,23},{8,0},{9,1... | collective-permute-start | bytes 1179656 | tf_op jit(solution)/shard_map/ppermute | solution.py:216
  59.9 13.5 %collective-permute-start.14 = (bf16[512,512]{1,0:T(8,128)(2,1)S(1)}, bf16[512,512]{1,0:T(8,128)(2,1)S(1)}, u32[]{:S(2)}, u32[]{:S(2)}) collective-permute-start(bf16[512,512]{1,0:T(8,128)(2,1)S(1)} %get-tuple-element.108), channel_id=1, source_target_pairs={{0,1},{1,0},{2,3},{3,2},{4,5},{5,4},{6,7},{7,6},{8,9},{9,8},{10,11... | collective-permute-start | bytes 1572872 | tf_op jit(solution)/shard_map/ppermute | solution.py:370
  82.5 12.5 %collective-permute-start.17 = (bf16[128,1536]{1,0:T(8,128)(2,1)S(1)}, bf16[128,1536]{1,0:T(8,128)(2,1)S(1)}, u32[]{:S(2)}, u32[]{:S(2)}) collective-permute-start(bf16[128,1536]{1,0:T(8,128)(2,1)S(1)} %fusion.30), channel_id=1, source_target_pairs={{0,8},{1,9},{2,10},{3,11},{4,12},{5,13},{6,14},{7,15},{8,24},{9,25... | collective-permute-start | bytes 1179656 | tf_op jit(solution)/shard_map/ppermute | solution.py:216
  83.2 11.8 %collective-permute-start.16 = (bf16[128,2560]{1,0:T(8,128)(2,1)S(1)}, bf16[128,2560]{1,0:T(8,128)(2,1)S(1)}, u32[]{:S(2)}, u32[]{:S(2)}) collective-permute-start(bf16[128,2560]{1,0:T(8,128)(2,1)S(1)} %fusion.8), channel_id=1, source_target_pairs={{0,4},{1,3},{2,6},{3,1},{4,0},{5,7},{6,2},{7,5},{8,12},{9,11},{10,... | collective-permute-start | bytes 1966088 | tf_op jit(solution)/shard_map/ppermute | solution.py:208
  95.1 11.5 %collective-permute-start.19 = (bf16[128,1536]{1,0:T(8,128)(2,1)S(1)}, bf16[128,1536]{1,0:T(8,128)(2,1)S(1)}, u32[]{:S(2)}, u32[]{:S(2)}) collective-permute-start(bf16[128,1536]{1,0:T(8,128)(2,1)S(1)} %add_convert_fusion.4), channel_id=1, source_target_pairs={{0,8},{1,9},{2,10},{3,11},{4,12},{5,13},{6,14},{7,15},{8,24},{9,25... | collective-permute-start | bytes 1179656 | tf_op jit(solution)/shard_map/ppermute | solution.py:216
  95.5 11.2 %collective-permute-start.18 = (bf16[128,2560]{1,0:T(8,128)(2,1)S(1)}, bf16[128,2560]{1,0:T(8,128)(2,1)S(1)}, u32[]{:S(2)}, u32[]{:S(2)}) collective-permute-start(bf16[128,2560]{1,0:T(8,128)(2,1)S(1)} %fusion.11), channel_id=1, source_target_pairs={{0,4},{1,3},{2,6},{3,1},{4,0},{5,7},{6,2},{7,5},{8,12},{9,11},{10,... | collective-permute-start | bytes 1966088 | tf_op jit(solution)/shard_map/ppermute | solution.py:208
  107.0 10.6 %collective-permute-start.21 = (bf16[128,1536]{1,0:T(8,128)(2,1)S(1)}, bf16[128,1536]{1,0:T(8,128)(2,1)S(1)}, u32[]{:S(2)}, u32[]{:S(2)}) collective-permute-start(bf16[128,1536]{1,0:T(8,128)(2,1)S(1)} %add_convert_fusion.3), channel_id=1, source_target_pairs={{0,8},{1,9},{2,10},{3,11},{4,12},{5,13},{6,14},{7,15},{8,24},{9,25... | collective-permute-start | bytes 1179656 | tf_op jit(solution)/shard_map/ppermute | solution.py:216
  108.1 10.6 %collective-permute-start.20 = (bf16[128,2560]{1,0:T(8,128)(2,1)S(1)}, bf16[128,2560]{1,0:T(8,128)(2,1)S(1)}, u32[]{:S(2)}, u32[]{:S(2)}) collective-permute-start(bf16[128,2560]{1,0:T(8,128)(2,1)S(1)} %add_convert_fusion.1), channel_id=1, source_target_pairs={{0,2},{1,5},{2,0},{3,7},{4,6},{5,1},{6,4},{7,3},{8,10},{9,13},{10,... | collective-permute-start | bytes 1966088 | tf_op jit(solution)/shard_map/ppermute | solution.py:208
  119.1 7.2 %collective-permute-start.24 = (bf16[32,1536]{1,0:T(8,128)(2,1)S(1)}, bf16[32,1536]{1,0:T(8,128)(2,1)S(1)}, u32[]{:S(2)}, u32[]{:S(2)}) collective-permute-start(bf16[32,1536]{1,0:T(8,128)(2,1)S(1)} %get-tuple-element.175), channel_id=1, source_target_pairs={{0,6},{1,7},{2,4},{3,5},{4,2},{5,3},{6,0},{7,1},{8,14},{9,15},{10,... | collective-permute-start | bytes 294920 | tf_op jit(solution)/shard_map/ppermute | solution.py:208
  120.8 10.2 %collective-permute-start.27 = (bf16[32,2560]{1,0:T(8,128)(2,1)S(1)}, bf16[32,2560]{1,0:T(8,128)(2,1)S(1)}, u32[]{:S(2)}, u32[]{:S(2)}) collective-permute-start(bf16[32,2560]{1,0:T(8,128)(2,1)S(1)} %get-tuple-element.164), channel_id=1, source_target_pairs={{0,24},{1,25},{2,26},{3,27},{4,28},{5,29},{6,30},{7,31},{8,16},{9,... | collective-permute-start | bytes 491528 | tf_op jit(solution)/shard_map/ppermute | solution.py:216
  123.2 7.8 %collective-permute-start.26 = (bf16[32,2560]{1,0:T(8,128)(2,1)S(1)}, bf16[32,2560]{1,0:T(8,128)(2,1)S(1)}, u32[]{:S(2)}, u32[]{:S(2)}) collective-permute-start(bf16[32,2560]{1,0:T(8,128)(2,1)S(1)} %get-tuple-element.165), channel_id=1, source_target_pairs={{0,16},{1,17},{2,18},{3,19},{4,20},{5,21},{6,22},{7,23},{8,0},{9,1... | collective-permute-start | bytes 491528 | tf_op jit(solution)/shard_map/ppermute | solution.py:216
  123.5 11.6 %collective-permute-start.25 = (bf16[32,2560]{1,0:T(8,128)(2,1)S(1)}, bf16[32,2560]{1,0:T(8,128)(2,1)S(1)}, u32[]{:S(2)}, u32[]{:S(2)}) collective-permute-start(bf16[32,2560]{1,0:T(8,128)(2,1)S(1)} %get-tuple-element.166), channel_id=1, source_target_pairs={{0,8},{1,9},{2,10},{3,11},{4,12},{5,13},{6,14},{7,15},{8,24},{9,25... | collective-permute-start | bytes 491528 | tf_op jit(solution)/shard_map/ppermute | solution.py:216
  135.2 5.6 %collective-permute-start.28 = (bf16[32,2560]{1,0:T(8,128)(2,1)S(1)}, bf16[32,2560]{1,0:T(8,128)(2,1)S(1)}, u32[]{:S(2)}, u32[]{:S(2)}) collective-permute-start(bf16[32,2560]{1,0:T(8,128)(2,1)S(1)} %fusion.51), channel_id=1, source_target_pairs={{0,16},{1,17},{2,18},{3,19},{4,20},{5,21},{6,22},{7,23},{8,0},{9,1... | collective-permute-start | bytes 491528 | tf_op jit(solution)/shard_map/ppermute | solution.py:216
  135.3 7.5 %collective-permute-start.33 = (bf16[32,1536]{1,0:T(8,128)(2,1)S(1)}, bf16[32,1536]{1,0:T(8,128)(2,1)S(1)}, u32[]{:S(2)}, u32[]{:S(2)}) collective-permute-start(bf16[32,1536]{1,0:T(8,128)(2,1)S(1)} %fusion.54), channel_id=1, source_target_pairs={{0,6},{1,7},{2,4},{3,5},{4,2},{5,3},{6,0},{7,1},{8,14},{9,15},{10,... | collective-permute-start | bytes 294920 | tf_op jit(solution)/shard_map/ppermute | solution.py:208
  136.7 6.1 %collective-permute-start.32 = (bf16[32,1536]{1,0:T(8,128)(2,1)S(1)}, bf16[32,1536]{1,0:T(8,128)(2,1)S(1)}, u32[]{:S(2)}, u32[]{:S(2)}) collective-permute-start(bf16[32,1536]{1,0:T(8,128)(2,1)S(1)} %fusion.54), channel_id=1, source_target_pairs={{0,4},{1,3},{2,6},{3,1},{4,0},{5,7},{6,2},{7,5},{8,12},{9,11},{10,... | collective-permute-start | bytes 294920 | tf_op jit(solution)/shard_map/ppermute | solution.py:208
  138.8 7.8 %collective-permute-start.30 = (bf16[32,2560]{1,0:T(8,128)(2,1)S(1)}, bf16[32,2560]{1,0:T(8,128)(2,1)S(1)}, u32[]{:S(2)}, u32[]{:S(2)}) collective-permute-start(bf16[32,2560]{1,0:T(8,128)(2,1)S(1)} %fusion.51), channel_id=1, source_target_pairs={{0,8},{1,9},{2,10},{3,11},{4,12},{5,13},{6,14},{7,15},{8,24},{9,25... | collective-permute-start | bytes 491528 | tf_op jit(solution)/shard_map/ppermute | solution.py:216
  140.8 7.0 %collective-permute-start.29 = (bf16[32,2560]{1,0:T(8,128)(2,1)S(1)}, bf16[32,2560]{1,0:T(8,128)(2,1)S(1)}, u32[]{:S(2)}, u32[]{:S(2)}) collective-permute-start(bf16[32,2560]{1,0:T(8,128)(2,1)S(1)} %collective-permute-done.28), channel_id=1, source_target_pairs={{0,16},{1,17},{2,18},{3,19},{4,20},{5,21},{6,22},{7,23},{8,0},{9,1... | collective-permute-start | bytes 491528 | tf_op jit(solution)/shard_map/ppermute | solution.py:216
  147.9 12.2 %collective-permute-start.34 = (bf16[4,32,2560]{2,1,0:T(8,128)(2,1)S(1)}, bf16[4,32,2560]{2,1,0:T(8,128)(2,1)S(1)}, u32[]{:S(2)}, u32[]{:S(2)}) collective-permute-start(bf16[4,32,2560]{2,1,0:T(8,128)(2,1)S(1)} %maximum_bitcast_fusion.refs_3_), channel_id=1, source_target_pairs={{0,2},{1,5},{2,0},{3,7},{4,6},{5,1},{6,4},{7,3},{8,10},{9,13},{10,... | collective-permute-start | bytes 1966088 | tf_op jit(solution)/shard_map/ppermute | solution.py:208
  149.7 7.8 %collective-permute-start.35 = (bf16[4,32,1536]{2,1,0:T(8,128)(2,1)S(1)}, bf16[4,32,1536]{2,1,0:T(8,128)(2,1)S(1)}, u32[]{:S(2)}, u32[]{:S(2)}) collective-permute-start(bf16[4,32,1536]{2,1,0:T(8,128)(2,1)S(1)} %maximum_bitcast_fusion.1.refs_7_), channel_id=1, source_target_pairs={{0,16},{1,17},{2,18},{3,19},{4,20},{5,21},{6,22},{7,23},{8,0},{9,1... | collective-permute-start | bytes 1179656 | tf_op jit(solution)/shard_map/ppermute | solution.py:216
  160.1 12.2 %collective-permute-start.36 = (bf16[4,32,2560]{2,1,0:T(8,128)(2,1)S(1)}, bf16[4,32,2560]{2,1,0:T(8,128)(2,1)S(1)}, u32[]{:S(2)}, u32[]{:S(2)}) collective-permute-start(bf16[4,32,2560]{2,1,0:T(8,128)(2,1)S(1)} %maximum_bitcast_fusion.refs_3_), channel_id=1, source_target_pairs={{0,4},{1,3},{2,6},{3,1},{4,0},{5,7},{6,2},{7,5},{8,12},{9,11},{10,... | collective-permute-start | bytes 1966088 | tf_op jit(solution)/shard_map/ppermute | solution.py:208
  162.5 9.7 %collective-permute-start.37 = (bf16[4,32,1536]{2,1,0:T(8,128)(2,1)S(1)}, bf16[4,32,1536]{2,1,0:T(8,128)(2,1)S(1)}, u32[]{:S(2)}, u32[]{:S(2)}) collective-permute-start(bf16[4,32,1536]{2,1,0:T(8,128)(2,1)S(1)} %collective-permute-done.35.refs_8_), channel_id=1, source_target_pairs={{0,16},{1,17},{2,18},{3,19},{4,20},{5,21},{6,22},{7,23},{8,0},{9,1... | collective-permute-start | bytes 1179656 | tf_op jit(solution)/shard_map/ppermute | solution.py:216
  172.2 8.5 %collective-permute-start.39 = (bf16[4,32,1536]{2,1,0:T(8,128)(2,1)S(1)}, bf16[4,32,1536]{2,1,0:T(8,128)(2,1)S(1)}, u32[]{:S(2)}, u32[]{:S(2)}) collective-permute-start(bf16[4,32,1536]{2,1,0:T(8,128)(2,1)S(1)} %collective-permute-done.37.refs_9_), channel_id=1, source_target_pairs={{0,16},{1,17},{2,18},{3,19},{4,20},{5,21},{6,22},{7,23},{8,0},{9,1... | collective-permute-start | bytes 1179656 | tf_op jit(solution)/shard_map/ppermute | solution.py:216
  175.5 10.7 %collective-permute-start.38 = (bf16[4,32,2560]{2,1,0:T(8,128)(2,1)S(1)}, bf16[4,32,2560]{2,1,0:T(8,128)(2,1)S(1)}, u32[]{:S(2)}, u32[]{:S(2)}) collective-permute-start(bf16[4,32,2560]{2,1,0:T(8,128)(2,1)S(1)} %collective-permute-done.34.refs_4_), channel_id=1, source_target_pairs={{0,4},{1,3},{2,6},{3,1},{4,0},{5,7},{6,2},{7,5},{8,12},{9,11},{10,... | collective-permute-start | bytes 1966088 | tf_op jit(solution)/shard_map/ppermute | solution.py:208
  (14 other events, 132.4 us)
